TPU v7x, 32 devices: a whole 2x2x4 slice. The times are simulated.
32 devices in a mesh: fsdp: 4 (over z), ctx: 4 (over y, core), tp: 2 (over x).
Axes of the slice: x: 2, y: 2, z: 4, core: 2. Of those that a mesh axis runs over, the one named last changes fastest.
Arguments:
- prompt_x: bfloat16 [4, 1024, 2304], P('fsdp', 'ctx'), may hold values from -6 to 6
- cont_x: bfloat16 [16, 256, 2304], P(('fsdp', 'ctx')), may hold values from -6 to 6
- cont_prompt: int32 [16], P(('fsdp', 'ctx')), may hold values from 0 to 3, as said below
- cont_len: int32 [16], P(('fsdp', 'ctx')), may hold values from 64 to 256, as said below
- attn_norm: bfloat16 [2304], P(('fsdp', 'ctx')), may hold values from 0.25 to 1.75
- attn_post: bfloat16 [2304], P(('fsdp', 'ctx')), may hold values from 0.25 to 1.75
- mlp_norm: bfloat16 [2304], P(('fsdp', 'ctx')), may hold values from 0.25 to 1.75
- mlp_post: bfloat16 [2304], P(('fsdp', 'ctx')), may hold values from 0.25 to 1.75
- w_query: bfloat16 [2304, 2048], P(('fsdp', 'ctx'), 'tp'), may hold values from -0.125 to 0.125
- w_key: bfloat16 [2304, 1024], P(('fsdp', 'ctx'), 'tp'), may hold values from -0.125 to 0.125
- w_value: bfloat16 [2304, 1024], P(('fsdp', 'ctx'), 'tp'), may hold values from -0.125 to 0.125
- w_out: bfloat16 [2048, 2304], P('tp', ('fsdp', 'ctx')), may hold values from -0.125 to 0.125
- w_gate: bfloat16 [2304, 9216], P(('fsdp', 'ctx'), 'tp'), may hold values from -0.125 to 0.125
- w_up: bfloat16 [2304, 9216], P(('fsdp', 'ctx'), 'tp'), may hold values from -0.125 to 0.125
- w_down: bfloat16 [9216, 2304], P('tp', ('fsdp', 'ctx')), may hold values from -0.0625 to 0.0625
- prompt_cot: bfloat16 [4, 1024, 2304], P('fsdp', 'ctx'), may hold values from -6 to 6
- cont_cot: bfloat16 [16, 256, 2304], P(('fsdp', 'ctx')), may hold values from -6 to 6
Outputs:
- y_prompt: bfloat16 [4, 1024, 2304], P('fsdp', 'ctx')
- y_cont: bfloat16 [16, 256, 2304], P(('fsdp', 'ctx'))
- grad_prompt: float32 [4, 1024, 2304], P('fsdp', 'ctx')
- grad_cont: float32 [16, 256, 2304], P(('fsdp', 'ctx'))
- grad_attn_norm: float32 [2304], P(('fsdp', 'ctx'))
- grad_attn_post: float32 [2304], P(('fsdp', 'ctx'))
- grad_mlp_norm: float32 [2304], P(('fsdp', 'ctx'))
- grad_mlp_post: float32 [2304], P(('fsdp', 'ctx'))
- grad_w_query: float32 [2304, 2048], P(('fsdp', 'ctx'), 'tp')
- grad_w_key: float32 [2304, 1024], P(('fsdp', 'ctx'), 'tp')
- grad_w_value: float32 [2304, 1024], P(('fsdp', 'ctx'), 'tp')
- grad_w_out: float32 [2048, 2304], P('tp', ('fsdp', 'ctx'))
- grad_w_gate: float32 [2304, 9216], P(('fsdp', 'ctx'), 'tp')
- grad_w_up: float32 [2304, 9216], P(('fsdp', 'ctx'), 'tp')
- grad_w_down: float32 [9216, 2304], P('tp', ('fsdp', 'ctx'))
Inputs may be any that keep to these rules, and one draw needn't show every extreme that they name: `cont_prompt`: each of the 4 prompts is continued by the same number of continuations. `cont_len`: some continuation is live in all 256 positions.
All inputs are finite; a program needn't handle non-finite values.
Results may differ from a plain program's by a relative error of at most 0.018.
Values may be sent and summed in bfloat16 or wider, within the bound.
No kernel may reach another device: no remote copies, remote signals or barrier semaphores. Data moves between devices by JAX's collectives and lax.ppermute only.
A program may use at most 384 MiB of HBM per device.

v0:
```python
import math

import jax
import jax.numpy as jnp
from jax import lax
from jax.sharding import PartitionSpec as P

HD = 256
PROMPT = 1024


soft_cap = 50.0
norm_eps = 1e-06
masked_fill = -1e30


def norm_parts(values):
    inverse = lax.rsqrt(jnp.mean(values * values, axis=-1, keepdims=True) + norm_eps)
    return (values * inverse, inverse)


def norm_back(grad_out, normal, inverse, scales):
    grad_normal = grad_out * scales
    grad_in = inverse * (
        grad_normal - normal * jnp.mean(grad_normal * normal, axis=-1, keepdims=True)
    )
    return (grad_in, jnp.sum(grad_out * normal, axis=0))


def rotary_tables(places, head_dim):
    half_dim = head_dim // 2
    frequency = jnp.exp(
        jnp.arange(half_dim, dtype=jnp.float32) * (-2.0 * math.log(10000.0) / head_dim)
    )
    angles = places[:, None] * frequency[None, :]
    return (jnp.cos(angles)[:, None, :], jnp.sin(angles)[:, None, :])


def rotary(values, cosine, sine_wave):
    half_dim = values.shape[-1] // 2
    front_half = values[..., :half_dim]
    back_half = values[..., half_dim:]
    return jnp.concatenate(
        [front_half * cosine - back_half * sine_wave, back_half * cosine + front_half * sine_wave],
        axis=-1,
    )


def attend_forward(query_b, key_b, value_b, allowed):
    raw_scores = jnp.einsum("bnkgd,bmkd->bkgnm", query_b, key_b, preferred_element_type=jnp.float32)
    capped = jnp.where(allowed, soft_cap * jnp.tanh(raw_scores / soft_cap), masked_fill)
    row_peak = jnp.max(capped, axis=-1, keepdims=True)
    exponent = jnp.exp(capped - row_peak)
    row_total = jnp.sum(exponent, axis=-1, keepdims=True)
    weight_set = (exponent / row_total).astype(jnp.bfloat16)
    mixed = jnp.einsum("bkgnm,bmkd->bnkgd", weight_set, value_b, preferred_element_type=jnp.float32)
    return (mixed, row_peak + jnp.log(row_total))


def attend_backward(query_b, key_b, value_b, allowed, log_total, grad_mixed):
    raw_scores = jnp.einsum("bnkgd,bmkd->bkgnm", query_b, key_b, preferred_element_type=jnp.float32)
    squashed = jnp.tanh(raw_scores / soft_cap)
    capped = jnp.where(allowed, soft_cap * squashed, masked_fill)
    probabilities = jnp.exp(capped - log_total)
    weight_set = probabilities.astype(jnp.bfloat16)
    grad_value = jnp.einsum(
        "bkgnm,bnkgd->bmkd", weight_set, grad_mixed, preferred_element_type=jnp.float32
    )
    grad_probs = jnp.einsum(
        "bnkgd,bmkd->bkgnm", grad_mixed, value_b, preferred_element_type=jnp.float32
    )
    inner_sum = jnp.sum(probabilities * grad_probs, axis=-1, keepdims=True)
    grad_scores = (probabilities * (grad_probs - inner_sum) * (1.0 - squashed * squashed)).astype(
        jnp.bfloat16
    )
    grad_query = jnp.einsum(
        "bkgnm,bmkd->bnkgd", grad_scores, key_b, preferred_element_type=jnp.float32
    )
    grad_key = jnp.einsum(
        "bkgnm,bnkgd->bmkd", grad_scores, query_b, preferred_element_type=jnp.float32
    )
    return (grad_query, grad_key, grad_value)


def shards(
    prompt_x,
    cont_x,
    cont_prompt,
    cont_len,
    attn_norm,
    attn_post,
    mlp_norm,
    mlp_post,
    w_query,
    w_key,
    w_value,
    w_out,
    w_gate,
    w_up,
    w_down,
    prompt_cot,
    cont_cot,
):
    model_width = prompt_x.shape[2]
    prompt_local = prompt_x.shape[1]
    cont_count = cont_x.shape[0]
    cont_size = cont_x.shape[1]
    cont_rows = cont_count * cont_size
    total_rows = prompt_local + cont_rows
    query_heads = w_query.shape[1] // HD
    key_heads = w_key.shape[1] // HD
    shared_by = query_heads // key_heads
    group_count = lax.axis_size("fsdp")
    ctx_index = lax.axis_index("ctx")
    group_index = lax.axis_index("fsdp")
    share_rows = total_rows // lax.axis_size("tp")
    share_start = lax.axis_index("tp") * share_rows
    query_scale = HD ** (-0.5)

    def take_share(values):
        return lax.dynamic_slice_in_dim(values, share_start, share_rows, 0)

    gathered = (
        lax.all_gather(attn_norm, ("fsdp", "ctx"), axis=0, tiled=True),
        lax.all_gather(attn_post, ("fsdp", "ctx"), axis=0, tiled=True),
        lax.all_gather(mlp_norm, ("fsdp", "ctx"), axis=0, tiled=True),
        lax.all_gather(mlp_post, ("fsdp", "ctx"), axis=0, tiled=True),
        lax.all_gather(w_query, ("fsdp", "ctx"), axis=0, tiled=True),
        lax.all_gather(w_key, ("fsdp", "ctx"), axis=0, tiled=True),
        lax.all_gather(w_value, ("fsdp", "ctx"), axis=0, tiled=True),
        lax.all_gather(w_out, ("fsdp", "ctx"), axis=1, tiled=True),
        lax.all_gather(w_gate, ("fsdp", "ctx"), axis=0, tiled=True),
        lax.all_gather(w_up, ("fsdp", "ctx"), axis=0, tiled=True),
        lax.all_gather(w_down, ("fsdp", "ctx"), axis=1, tiled=True),
    )
    norm_attn = gathered[0].astype(jnp.float32)
    post_attn = gathered[1].astype(jnp.float32)
    norm_mlp = gathered[2].astype(jnp.float32)
    post_mlp = gathered[3].astype(jnp.float32)
    full_query, full_key, full_value, full_out, full_gate, full_up, full_down = gathered[4:]
    residual = jnp.concatenate(
        [prompt_x.reshape(prompt_local, model_width), cont_x.reshape(cont_rows, model_width)],
        axis=0,
    ).astype(jnp.float32)
    prompt_pos = ctx_index * prompt_local + jnp.arange(prompt_local, dtype=jnp.int32)
    cont_pos = PROMPT + jnp.tile(jnp.arange(cont_size, dtype=jnp.int32), cont_count)
    places = jnp.concatenate([prompt_pos, cont_pos]).astype(jnp.float32)
    cosine, sine_wave = rotary_tables(places, HD)
    cont_live = (
        (jnp.arange(cont_size, dtype=jnp.int32)[None, :] < cont_len[:, None])
        .astype(jnp.float32)
        .reshape(cont_rows)
    )
    live_rows = jnp.concatenate([jnp.ones((prompt_local,), jnp.float32), cont_live])
    live_share = take_share(live_rows)
    normal_one, inverse_one = norm_parts(residual)
    attn_in = (normal_one * norm_attn).astype(jnp.bfloat16)
    query_proj = jnp.dot(attn_in, full_query, preferred_element_type=jnp.float32)
    key_proj = jnp.dot(attn_in, full_key, preferred_element_type=jnp.float32)
    value_rows = (
        jnp.dot(attn_in, full_value, preferred_element_type=jnp.float32)
        .astype(jnp.bfloat16)
        .reshape(-1, key_heads, HD)
    )
    query_rows = (
        (rotary(query_proj.reshape(-1, query_heads, HD), cosine, sine_wave) * query_scale)
        .astype(jnp.bfloat16)
        .reshape(-1, key_heads, shared_by, HD)
    )
    key_rows = rotary(key_proj.reshape(-1, key_heads, HD), cosine, sine_wave).astype(jnp.bfloat16)
    prompt_key = key_rows[:prompt_local]
    prompt_value = value_rows[:prompt_local]
    every_key, every_value = (
        lax.all_gather(prompt_key, ("fsdp", "ctx"), axis=0, tiled=True),
        lax.all_gather(prompt_value, ("fsdp", "ctx"), axis=0, tiled=True),
    )
    every_key = every_key.reshape(group_count, -1, key_heads, HD)
    every_value = every_value.reshape(group_count, -1, key_heads, HD)
    own_key = every_key[group_index]
    own_value = every_value[group_index]
    prompt_span = own_key.shape[0]
    prompt_allowed = jnp.arange(prompt_span, dtype=jnp.int32)[None, :] <= prompt_pos[:, None]
    cont_allowed = (
        jnp.arange(prompt_span + cont_size, dtype=jnp.int32)[None, :]
        <= prompt_span + jnp.arange(cont_size, dtype=jnp.int32)[:, None]
    )
    prompt_query = query_rows[:prompt_local][None]
    cont_query = query_rows[prompt_local:].reshape(cont_count, cont_size, key_heads, shared_by, HD)
    cont_key = jnp.concatenate(
        [
            jnp.take(every_key, cont_prompt, axis=0),
            key_rows[prompt_local:].reshape(cont_count, cont_size, key_heads, HD),
        ],
        axis=1,
    )
    cont_value = jnp.concatenate(
        [
            jnp.take(every_value, cont_prompt, axis=0),
            value_rows[prompt_local:].reshape(cont_count, cont_size, key_heads, HD),
        ],
        axis=1,
    )
    prompt_mixed, prompt_total = attend_forward(
        prompt_query, own_key[None], own_value[None], prompt_allowed
    )
    cont_mixed, cont_total = attend_forward(cont_query, cont_key, cont_value, cont_allowed)
    attn_out = jnp.concatenate(
        [prompt_mixed.reshape(prompt_local, -1), cont_mixed.reshape(cont_rows, -1)], axis=0
    ).astype(jnp.bfloat16)
    branch_share = lax.psum_scatter(
        jnp.dot(attn_out, full_out, preferred_element_type=jnp.float32),
        "tp",
        scatter_dimension=0,
        tiled=True,
    )
    normal_two, inverse_two = norm_parts(branch_share)
    middle_share = take_share(residual) + normal_two * post_attn
    normal_three, inverse_three = norm_parts(middle_share)
    mlp_in = lax.all_gather(
        (normal_three * norm_mlp).astype(jnp.bfloat16), "tp", axis=0, tiled=True
    )
    gate_proj = jnp.dot(mlp_in, full_gate, preferred_element_type=jnp.float32)
    up_proj = jnp.dot(mlp_in, full_up, preferred_element_type=jnp.float32)
    inner_value, gelu_pull = jax.vjp(
        lambda gate_in, up_in: jax.nn.gelu(gate_in, approximate=True) * up_in, gate_proj, up_proj
    )
    inner_act = inner_value.astype(jnp.bfloat16)
    mlp_share = lax.psum_scatter(
        jnp.dot(inner_act, full_down, preferred_element_type=jnp.float32),
        "tp",
        scatter_dimension=0,
        tiled=True,
    )
    normal_four, inverse_four = norm_parts(mlp_share)
    result_share = (middle_share + normal_four * post_mlp) * live_share[:, None]
    back_query, back_key, back_value, back_out, back_gate, back_up, back_down = (
        lax.all_gather(w_query, ("fsdp", "ctx"), axis=0, tiled=True),
        lax.all_gather(w_key, ("fsdp", "ctx"), axis=0, tiled=True),
        lax.all_gather(w_value, ("fsdp", "ctx"), axis=0, tiled=True),
        lax.all_gather(w_out, ("fsdp", "ctx"), axis=1, tiled=True),
        lax.all_gather(w_gate, ("fsdp", "ctx"), axis=0, tiled=True),
        lax.all_gather(w_up, ("fsdp", "ctx"), axis=0, tiled=True),
        lax.all_gather(w_down, ("fsdp", "ctx"), axis=1, tiled=True),
    )
    cot_rows = jnp.concatenate(
        [prompt_cot.reshape(prompt_local, model_width), cont_cot.reshape(cont_rows, model_width)],
        axis=0,
    )
    grad_result_share = take_share(cot_rows).astype(jnp.float32) * live_share[:, None]
    grad_mlp_share, grad_post_mlp = norm_back(
        grad_result_share, normal_four, inverse_four, post_mlp
    )
    result_rows, grad_mlp_low = (
        lax.all_gather(result_share.astype(jnp.bfloat16), "tp", axis=0, tiled=True),
        lax.all_gather(grad_mlp_share.astype(jnp.bfloat16), "tp", axis=0, tiled=True),
    )
    grad_down_w = jnp.einsum(
        "rf,rd->fd", inner_act, grad_mlp_low, preferred_element_type=jnp.float32
    )
    grad_inner = jnp.einsum(
        "rd,fd->rf", grad_mlp_low, back_down, preferred_element_type=jnp.float32
    )
    grad_gate, grad_up = gelu_pull(grad_inner)
    grad_gate = grad_gate.astype(jnp.bfloat16)
    grad_up = grad_up.astype(jnp.bfloat16)
    grad_gate_w = jnp.einsum("rd,rf->df", mlp_in, grad_gate, preferred_element_type=jnp.float32)
    grad_up_w = jnp.einsum("rd,rf->df", mlp_in, grad_up, preferred_element_type=jnp.float32)
    grad_mlp_part = jnp.einsum(
        "rf,df->rd", grad_gate, back_gate, preferred_element_type=jnp.float32
    ) + jnp.einsum("rf,df->rd", grad_up, back_up, preferred_element_type=jnp.float32)
    grad_mlp_in = lax.psum_scatter(grad_mlp_part, "tp", scatter_dimension=0, tiled=True)
    grad_middle_norm, grad_norm_mlp = norm_back(grad_mlp_in, normal_three, inverse_three, norm_mlp)
    grad_middle_share = grad_result_share + grad_middle_norm
    grad_branch_share, grad_post_attn = norm_back(
        grad_middle_share, normal_two, inverse_two, post_attn
    )
    grad_branch_low = lax.all_gather(
        grad_branch_share.astype(jnp.bfloat16), "tp", axis=0, tiled=True
    )
    grad_out_w = jnp.einsum(
        "rh,rd->hd", attn_out, grad_branch_low, preferred_element_type=jnp.float32
    )
    grad_attn = jnp.einsum(
        "rd,hd->rh", grad_branch_low, back_out, preferred_element_type=jnp.float32
    ).astype(jnp.bfloat16)
    grad_prompt_mixed = grad_attn[:prompt_local].reshape(1, prompt_local, key_heads, shared_by, HD)
    grad_cont_mixed = grad_attn[prompt_local:].reshape(
        cont_count, cont_size, key_heads, shared_by, HD
    )
    prompt_gq, prompt_gk, prompt_gv = attend_backward(
        prompt_query,
        own_key[None],
        own_value[None],
        prompt_allowed,
        prompt_total,
        grad_prompt_mixed,
    )
    cont_gq, cont_gk, cont_gv = attend_backward(
        cont_query, cont_key, cont_value, cont_allowed, cont_total, grad_cont_mixed
    )
    cont_onehot = (
        cont_prompt[:, None] == jnp.arange(group_count, dtype=jnp.int32)[None, :]
    ).astype(jnp.float32)
    own_onehot = (jnp.arange(group_count, dtype=jnp.int32) == group_index).astype(jnp.float32)[
        :, None, None, None
    ]
    key_term = (
        jnp.einsum(
            "cg,cpkd->gpkd", cont_onehot, cont_gk[:, :prompt_span], precision=lax.Precision.HIGHEST
        )
        + own_onehot * prompt_gk
    )
    value_term = (
        jnp.einsum(
            "cg,cpkd->gpkd", cont_onehot, cont_gv[:, :prompt_span], precision=lax.Precision.HIGHEST
        )
        + own_onehot * prompt_gv
    )
    key_total, value_total = (
        lax.psum_scatter(
            key_term.reshape(-1, key_heads, HD), ("fsdp", "ctx"), scatter_dimension=0, tiled=True
        ),
        lax.psum_scatter(
            value_term.reshape(-1, key_heads, HD), ("fsdp", "ctx"), scatter_dimension=0, tiled=True
        ),
    )
    grad_key_all = jnp.concatenate(
        [key_total, cont_gk[:, prompt_span:].reshape(cont_rows, key_heads, HD)], axis=0
    )
    grad_value_all = jnp.concatenate(
        [value_total, cont_gv[:, prompt_span:].reshape(cont_rows, key_heads, HD)], axis=0
    )
    grad_query_all = jnp.concatenate(
        [
            prompt_gq.reshape(prompt_local, query_heads, HD),
            cont_gq.reshape(cont_rows, query_heads, HD),
        ],
        axis=0,
    )
    grad_query_proj = (
        rotary(grad_query_all * query_scale, cosine, -sine_wave)
        .reshape(-1, query_heads * HD)
        .astype(jnp.bfloat16)
    )
    grad_key_proj = (
        rotary(grad_key_all, cosine, -sine_wave).reshape(-1, key_heads * HD).astype(jnp.bfloat16)
    )
    grad_value_proj = grad_value_all.reshape(-1, key_heads * HD).astype(jnp.bfloat16)
    grad_query_w = jnp.einsum(
        "rd,rh->dh", attn_in, grad_query_proj, preferred_element_type=jnp.float32
    )
    grad_key_w = jnp.einsum("rd,rh->dh", attn_in, grad_key_proj, preferred_element_type=jnp.float32)
    grad_value_w = jnp.einsum(
        "rd,rh->dh", attn_in, grad_value_proj, preferred_element_type=jnp.float32
    )
    grad_attn_part = jnp.einsum(
        "rh,dh->rd", grad_query_proj, back_query, preferred_element_type=jnp.float32
    )
    grad_attn_part = grad_attn_part + jnp.einsum(
        "rh,dh->rd", grad_key_proj, back_key, preferred_element_type=jnp.float32
    )
    grad_attn_part = grad_attn_part + jnp.einsum(
        "rh,dh->rd", grad_value_proj, back_value, preferred_element_type=jnp.float32
    )
    grad_attn_in = lax.psum_scatter(
        grad_attn_part.astype(jnp.bfloat16), "tp", scatter_dimension=0, tiled=True
    ).astype(jnp.float32)
    grad_input_norm, grad_norm_attn = norm_back(
        grad_attn_in, take_share(normal_one), take_share(inverse_one), norm_attn
    )
    grad_input_share = grad_middle_share + grad_input_norm
    gain_terms = jnp.stack([grad_norm_attn, grad_post_attn, grad_norm_mlp, grad_post_mlp], axis=0)[
        None
    ]
    grad_input, gain_parts = (
        lax.all_gather(grad_input_share.astype(jnp.bfloat16), "tp", axis=0, tiled=True).astype(
            grad_input_share.dtype
        ),
        lax.all_gather(gain_terms.astype(jnp.bfloat16), "tp", axis=0, tiled=True).astype(
            gain_terms.dtype
        ),
    )
    gain_sums = jnp.sum(gain_parts, axis=0)
    mlp_shards = (
        lax.psum_scatter(grad_gate_w, ("fsdp", "ctx"), scatter_dimension=0, tiled=True),
        lax.psum_scatter(grad_up_w, ("fsdp", "ctx"), scatter_dimension=0, tiled=True),
        lax.psum_scatter(grad_down_w, ("fsdp", "ctx"), scatter_dimension=1, tiled=True),
        lax.psum_scatter(gain_sums[2], ("fsdp", "ctx"), scatter_dimension=0, tiled=True),
        lax.psum_scatter(gain_sums[3], ("fsdp", "ctx"), scatter_dimension=0, tiled=True),
    )
    attn_shards = (
        lax.psum_scatter(grad_query_w, ("fsdp", "ctx"), scatter_dimension=0, tiled=True),
        lax.psum_scatter(grad_key_w, ("fsdp", "ctx"), scatter_dimension=0, tiled=True),
        lax.psum_scatter(grad_value_w, ("fsdp", "ctx"), scatter_dimension=0, tiled=True),
        lax.psum_scatter(grad_out_w, ("fsdp", "ctx"), scatter_dimension=1, tiled=True),
        lax.psum_scatter(gain_sums[0], ("fsdp", "ctx"), scatter_dimension=0, tiled=True),
        lax.psum_scatter(gain_sums[1], ("fsdp", "ctx"), scatter_dimension=0, tiled=True),
    )
    y_prompt = result_rows[:prompt_local].reshape(1, prompt_local, model_width)
    y_cont = result_rows[prompt_local:].reshape(cont_count, cont_size, model_width)
    grad_prompt = grad_input[:prompt_local].reshape(1, prompt_local, model_width)
    grad_cont = grad_input[prompt_local:].reshape(cont_count, cont_size, model_width)
    return (
        y_prompt,
        y_cont,
        grad_prompt,
        grad_cont,
        attn_shards[4],
        attn_shards[5],
        mlp_shards[3],
        mlp_shards[4],
        attn_shards[0],
        attn_shards[1],
        attn_shards[2],
        attn_shards[3],
        mlp_shards[0],
        mlp_shards[1],
        mlp_shards[2],
    )


def solution(mesh):
    in_specs = (
        P("fsdp", "ctx", None),
        P(("fsdp", "ctx"), None, None),
        P(("fsdp", "ctx")),
        P(("fsdp", "ctx")),
        P(("fsdp", "ctx")),
        P(("fsdp", "ctx")),
        P(("fsdp", "ctx")),
        P(("fsdp", "ctx")),
        P(("fsdp", "ctx"), "tp"),
        P(("fsdp", "ctx"), "tp"),
        P(("fsdp", "ctx"), "tp"),
        P("tp", ("fsdp", "ctx")),
        P(("fsdp", "ctx"), "tp"),
        P(("fsdp", "ctx"), "tp"),
        P("tp", ("fsdp", "ctx")),
        P("fsdp", "ctx", None),
        P(("fsdp", "ctx"), None, None),
    )
    out_specs = (
        P("fsdp", "ctx", None),
        P(("fsdp", "ctx"), None, None),
        P("fsdp", "ctx", None),
        P(("fsdp", "ctx"), None, None),
        P(("fsdp", "ctx")),
        P(("fsdp", "ctx")),
        P(("fsdp", "ctx")),
        P(("fsdp", "ctx")),
        P(("fsdp", "ctx"), "tp"),
        P(("fsdp", "ctx"), "tp"),
        P(("fsdp", "ctx"), "tp"),
        P("tp", ("fsdp", "ctx")),
        P(("fsdp", "ctx"), "tp"),
        P(("fsdp", "ctx"), "tp"),
        P("tp", ("fsdp", "ctx")),
    )
    return jax.shard_map(shards, mesh=mesh, in_specs=in_specs, out_specs=out_specs, check_vma=False)
```

profile of v0, /device:TPU:0, one launch (start us, length us, event | category | flops | bytes accessed | tf_op | source)
XLA Modules:
  0.0 3058.5 jit_solution(6892584013730012237)
XLA Ops:
  14.9 63.6 %all-reduce.10 = (bf16[2304]{0:T(1024)(128)(2,1)S(1)}, bf16[2304]{0:T(1024)(128)(2,1)S(1)}, bf16[2304]{0:T(1024)(128)(2,1)S(1)}, bf16[2304]{0:T(1024)(128)(2,1)S(1)}) all-reduce(bf16[2304]{0:T(1024)(128)(2,1)S(1)} %dynamic-update-slice.1, ...), channel_id=1, replica_groups=mesh['fsdp'=4,'ctx'=4,'tp'=2] {'fsdp','ctx'}, use_global_device_ids=true, to_apply=%add.1 | all-reduce | flops 9216 | bytes 36864
  111.6 41.8 %all-gather.23.cloned.1.call-done = bf16[2304,1024]{1,0:T(8,128)(2,1)} async-done(((bf16[144,1024]{1,0:T(8,128)(2,1)}), bf16[2304,1024]{1,0:T(8,128)(2,1)}) %all-gather.23.cloned.1.call-update) | async-done | bytes 4718608 | tf_op jit(solution)/shard_map/all_gather | solution.py:128
  167.8 37.4 %all-gather.17.cloned.1.call-done = bf16[4096,2,256]{2,0,1:T(8,128)(2,1)} async-done(((bf16[256,2,256]{2,0,1:T(8,128)(2,1)}), bf16[4096,2,256]{2,0,1:T(8,128)(2,1)}) %all-gather.17.cloned.1.call-update) | async-done | bytes 4194320 | tf_op jit(solution)/shard_map/all_gather | solution.py:175
  208.9 48.0 %all-gather.21.cloned.1.call-done = bf16[4096,2,256]{2,0,1:T(8,128)(2,1)} async-done(((bf16[256,2,256]{2,0,1:T(8,128)(2,1)}), bf16[4096,2,256]{2,0,1:T(8,128)(2,1)}) %all-gather.21.cloned.1.call-update) | async-done | bytes 4194320 | tf_op jit(solution)/shard_map/all_gather | solution.py:174
  270.1 40.8 %all-gather.25.cloned.1.call-done = bf16[1024,2304]{0,1:T(8,128)(2,1)} async-done(((bf16[1024,144]{0,1:T(8,128)(2,1)}), bf16[1024,2304]{0,1:T(8,128)(2,1)}) %all-gather.25.cloned.1.call-update) | async-done | bytes 4718608 | tf_op jit(solution)/shard_map/all_gather | solution.py:131
  320.9 56.1 %reduce-scatter.14.cloned.1.call-done = f32[256,2304]{1,0:T(8,128)} async-done(((f32[512,2304]{1,0:T(8,128)}), f32[256,2304]{1,0:T(8,128)}) %reduce-scatter.14.cloned.1.call-update) | async-done | bytes 2359312 | tf_op jit(solution)/shard_map/reduce_scatter | solution.py:210
  385.3 34.1 %all-gather.27.cloned.1.call-done = bf16[512,2304]{1,0:T(8,128)(2,1)} async-done(((bf16[256,2304]{1,0:T(8,128)(2,1)}), bf16[512,2304]{1,0:T(8,128)(2,1)}) %all-gather.27.cloned.1.call-update) | async-done | bytes 2359312 | tf_op jit(solution)/shard_map/all_gather | solution.py:219
  419.4 111.8 %all-gather.29.cloned.1.call-done = bf16[2304,4608]{1,0:T(8,128)(2,1)} async-done(((bf16[144,4608]{1,0:T(8,128)(2,1)}), bf16[2304,4608]{1,0:T(8,128)(2,1)}) %all-gather.29.cloned.1.call-update) | async-done | bytes 21233680 | tf_op jit(solution)/shard_map/all_gather | solution.py:132
  531.2 18.3 fusion.115
  549.5 93.3 %all-gather.31.cloned.1.call-done = bf16[2304,4608]{1,0:T(8,128)(2,1)} async-done(((bf16[144,4608]{1,0:T(8,128)(2,1)}), bf16[2304,4608]{1,0:T(8,128)(2,1)}) %all-gather.31.cloned.1.call-update) | async-done | bytes 21233680 | tf_op jit(solution)/shard_map/all_gather | solution.py:133
  642.9 21.2 multiply_convert_fusion.1
  664.1 90.6 %all-gather.33.cloned.1.call-done = bf16[4608,2304]{0,1:T(8,128)(2,1)} async-done(((bf16[4608,144]{0,1:T(8,128)(2,1)}), bf16[4608,2304]{0,1:T(8,128)(2,1)}) %all-gather.33.cloned.1.call-update) | async-done | bytes 21233680 | tf_op jit(solution)/shard_map/all_gather | solution.py:134
  754.6 17.1 fusion.116
  772.8 59.2 %reduce-scatter.16.cloned.1.call-done = f32[256,2304]{1,0:T(8,128)} async-done(((f32[512,2304]{1,0:T(8,128)}), f32[256,2304]{1,0:T(8,128)}) %reduce-scatter.16.cloned.1.call-update) | async-done | bytes 2359312 | tf_op jit(solution)/shard_map/reduce_scatter | solution.py:228
  840.3 36.2 %all-gather.37.cloned.1.call-done = bf16[512,2304]{1,0:T(8,128)(2,1)} async-done(((bf16[256,2304]{1,0:T(8,128)(2,1)}), bf16[512,2304]{1,0:T(8,128)(2,1)}) %all-gather.37.cloned.1.call-update) | async-done | bytes 2359312 | tf_op jit(solution)/shard_map/all_gather | solution.py:255
  876.5 27.6 multiply_convert_fusion
  904.1 16.1 fusion.117
  936.3 59.9 %reduce-scatter.18.cloned.1.call-done = f32[256,2304]{1,0:T(8,128)} async-done(((f32[512,2304]{1,0:T(8,128)}), f32[256,2304]{1,0:T(8,128)}) %reduce-scatter.18.cloned.1.call-update) | async-done | bytes 2359312 | tf_op jit(solution)/shard_map/reduce_scatter | solution.py:271
  1005.2 36.1 %all-gather.39.cloned.1.call-done = bf16[512,2304]{1,0:T(8,128)(2,1)} async-done(((bf16[256,2304]{1,0:T(8,128)(2,1)}), bf16[512,2304]{1,0:T(8,128)(2,1)}) %all-gather.39.cloned.1.call-update) | async-done | bytes 2359312 | tf_op jit(solution)/shard_map/all_gather | solution.py:277
  1115.6 89.2 %reduce-scatter.22.cloned.1.call-done = f32[256,2,256]{2,0,1:T(8,128)} async-done(((f32[4096,2,256]{2,0,1:T(8,128)}), f32[256,2,256]{2,0,1:T(8,128)}) %reduce-scatter.22.cloned.1.call-update) | async-done | bytes 524304 | tf_op jit(solution)/shard_map/reduce_scatter | solution.py:323
  1208.4 105.4 %reduce-scatter.20.cloned.1.call-done = f32[256,2,256]{2,0,1:T(8,128)} async-done(((f32[4096,2,256]{2,0,1:T(8,128)}), f32[256,2,256]{2,0,1:T(8,128)}) %reduce-scatter.20.cloned.1.call-update) | async-done | bytes 524304 | tf_op jit(solution)/shard_map/reduce_scatter | solution.py:320
  1327.9 29.0 reduce-scatter.24.cloned.1.call-done
  1390.3 20.6 fusion.121
  1412.6 20.1 fusion.119
  1432.8 23.0 fusion.120
  1464.8 62.7 %all-reduce.9 = (f32[2304]{0:T(1024)S(1)}, f32[2304]{0:T(1024)S(1)}, f32[2304]{0:T(1024)S(1)}, f32[2304]{0:T(1024)S(1)}) all-reduce(f32[2304]{0:T(1024)S(1)} %get-tuple-element.38, f32[2304]{0:T(1024)S(1)} %get-tuple-element.37, f32[2304]{0:T(1024)S(1)} %get-tuple-element.36, ...), channel_id=8, replica_groups=mesh['fsdp'=4,'ctx'=4,'tp'=2] {'fsdp','ctx'}, use_global_device_ids=true, to_apply=%region_25.27.clone | all-reduce | flops 9216 | bytes 73728
  1549.7 116.4 %reduce-scatter.26.cloned.1.call-done = f32[144,1024]{1,0:T(8,128)} async-done(((f32[2304,1024]{1,0:T(8,128)}), f32[144,1024]{1,0:T(8,128)}) %reduce-scatter.26.cloned.1.call-update) | async-done | bytes 589840 | tf_op jit(solution)/shard_map/reduce_scatter | solution.py:392
  1666.1 79.8 %reduce-scatter.30.cloned.1.call-done = f32[144,512]{1,0:T(8,128)} async-done(((f32[2304,512]{1,0:T(8,128)}), f32[144,512]{1,0:T(8,128)}) %reduce-scatter.30.cloned.1.call-update) | async-done | bytes 294928 | tf_op jit(solution)/shard_map/reduce_scatter | solution.py:394
  1745.9 79.4 %reduce-scatter.28.cloned.1.call-done = f32[144,512]{1,0:T(8,128)} async-done(((f32[2304,512]{1,0:T(8,128)}), f32[144,512]{1,0:T(8,128)}) %reduce-scatter.28.cloned.1.call-update) | async-done | bytes 294928 | tf_op jit(solution)/shard_map/reduce_scatter | solution.py:393
  1825.3 408.5 %reduce-scatter.38.cloned.1.call-done = f32[4608,144]{0,1:T(8,128)} async-done(((f32[4608,2304]{0,1:T(8,128)}), f32[4608,144]{0,1:T(8,128)}) %reduce-scatter.38.cloned.1.call-update) | async-done | bytes 2654224 | tf_op jit(solution)/shard_map/reduce_scatter | solution.py:387
  2233.7 409.1 %reduce-scatter.34.cloned.1.call-done = f32[144,4608]{1,0:T(8,128)} async-done(((f32[2304,4608]{1,0:T(8,128)}), f32[144,4608]{1,0:T(8,128)}) %reduce-scatter.34.cloned.1.call-update) | async-done | bytes 2654224 | tf_op jit(solution)/shard_map/reduce_scatter | solution.py:385
  2642.8 408.4 %reduce-scatter.36.cloned.1.call-done = f32[144,4608]{1,0:T(8,128)} async-done(((f32[2304,4608]{1,0:T(8,128)}), f32[144,4608]{1,0:T(8,128)}) %reduce-scatter.36.cloned.1.call-update) | async-done | bytes 2654224 | tf_op jit(solution)/shard_map/reduce_scatter | solution.py:386
  (353 shorter events, 279.1 us)
Async XLA Ops:
  7.2 73.5 %all-gather.15.cloned.1.call-start = ((), (), s32[]{:S(2)}) async-start(), calls=%async_computation.13 | async-start | bytes 2506752 | tf_op jit(solution)/shard_map/all_gather | solution.py:130
  7.9 91.0 %all-gather.19.cloned.1.call-start = ((), (), s32[]{:S(2)}) async-start(), calls=%async_computation.15 | async-start | bytes 2506752 | tf_op jit(solution)/shard_map/all_gather | solution.py:129
  8.7 144.7 %all-gather.23.cloned.1.call-start = ((), (), s32[]{:S(2)}) async-start(), calls=%async_computation.17 | async-start | bytes 5013504 | tf_op jit(solution)/shard_map/all_gather | solution.py:128
  9.4 195.8 %all-gather.17.cloned.1.call-start = ((), (), s32[]{:S(2)}) async-start(), calls=%async_computation.14 | async-start | bytes 4456448 | tf_op jit(solution)/shard_map/all_gather | solution.py:175
  78.4 75.0 %copy-start.53 = (f32[2304]{0:T(1024)}, f32[2304]{0:T(1024)S(1)}, u32[]{:S(2)}) copy-start(f32[2304]{0:T(1024)S(1)} %convert_element_type.124) | copy-start | bytes 27652
  80.6 72.8 %copy-start.71 = (f32[512]{0:T(512)}, f32[512]{0:T(512)S(1)}, u32[]{:S(2)}) copy-start(f32[512]{0:T(512)S(1)} %add_rsqrt_fusion) | copy-start | bytes 6148
  86.6 170.2 %all-gather.21.cloned.1.call-start = ((), (), s32[]{:S(2)}) async-start(), calls=%async_computation.16 | async-start | bytes 4456448 | tf_op jit(solution)/shard_map/all_gather | solution.py:174
  88.5 74.5 %copy-start.18 = (f32[512,128]{1,0:T(8,128)}, f32[512,128]{1,0:T(8,128)S(1)}, u32[]{:S(2)}) copy-start(f32[512,128]{1,0:T(8,128)S(1)} %get-tuple-element.79) | copy-start | bytes 786436
  108.5 202.4 %all-gather.25.cloned.1.call-start = ((), (), s32[]{:S(2)}) async-start(), calls=%async_computation.18 | async-start | bytes 5013504 | tf_op jit(solution)/shard_map/all_gather | solution.py:131
  109.1 267.9 %reduce-scatter.14.cloned.1.call-start = ((), (), s32[]{:S(2)}) async-start(), calls=%async_computation.19 | async-start | bytes 7077888 | tf_op jit(solution)/shard_map/reduce_scatter | solution.py:210
  318.3 101.1 %all-gather.27.cloned.1.call-start = ((), (), s32[]{:S(2)}) async-start(), calls=%async_computation.20 | async-start | bytes 3538944 | tf_op jit(solution)/shard_map/all_gather | solution.py:219
  383.2 148.0 %all-gather.29.cloned.1.call-start = ((), (), s32[]{:S(2)}) async-start(), calls=%async_computation.21 | async-start | bytes 22560768 | tf_op jit(solution)/shard_map/all_gather | solution.py:132
  384.0 258.9 %all-gather.31.cloned.1.call-start = ((), (), s32[]{:S(2)}) async-start(), calls=%async_computation.22 | async-start | bytes 22560768 | tf_op jit(solution)/shard_map/all_gather | solution.py:133
  384.6 370.1 %all-gather.33.cloned.1.call-start = ((), (), s32[]{:S(2)}) async-start(), calls=%async_computation.23 | async-start | bytes 22560768 | tf_op jit(solution)/shard_map/all_gather | solution.py:134
  385.3 446.7 %reduce-scatter.16.cloned.1.call-start = ((), (), s32[]{:S(2)}) async-start(), calls=%async_computation.24 | async-start | bytes 7077888 | tf_op jit(solution)/shard_map/reduce_scatter | solution.py:228
  771.8 104.7 %all-gather.37.cloned.1.call-start = ((), (), s32[]{:S(2)}) async-start(), calls=%async_computation.26 | async-start | bytes 3538944 | tf_op jit(solution)/shard_map/all_gather | solution.py:255
  772.8 67.5 %copy-start.70 = (f32[256]{0:T(256)}, f32[256]{0:T(256)S(1)}, u32[]{:S(2)}) copy-start(f32[256]{0:T(256)S(1)} %dynamic_slice.22) | copy-start | bytes 3076
  840.2 156.0 %reduce-scatter.18.cloned.1.call-start = ((), (), s32[]{:S(2)}) async-start(), calls=%async_computation.27 | async-start | bytes 7077888 | tf_op jit(solution)/shard_map/reduce_scatter | solution.py:271
  936.0 105.2 %all-gather.39.cloned.1.call-start = ((), (), s32[]{:S(2)}) async-start(), calls=%async_computation.28 | async-start | bytes 3538944 | tf_op jit(solution)/shard_map/all_gather | solution.py:277
  1005.0 199.8 %reduce-scatter.22.cloned.1.call-start = ((), (), s32[]{:S(2)}) async-start(), calls=%async_computation.30 | async-start | bytes 8912896 | tf_op jit(solution)/shard_map/reduce_scatter | solution.py:323
  1100.0 213.7 %reduce-scatter.20.cloned.1.call-start = ((), (), s32[]{:S(2)}) async-start(), calls=%async_computation.29 | async-start | bytes 8912896 | tf_op jit(solution)/shard_map/reduce_scatter | solution.py:320
  1100.6 256.3 %reduce-scatter.24.cloned.1.call-start = ((), (), s32[]{:S(2)}) async-start(), calls=%async_computation.31 | async-start | bytes 3538944 | tf_op jit(solution)/shard_map/reduce_scatter | solution.py:365
  1115.6 199.7 %copy-start.29 = (bf16[2304,512]{1,0:T(8,128)(2,1)S(1)}, bf16[2304,512]{1,0:T(8,128)(2,1)}, u32[]{:S(2)}) copy-start(bf16[2304,512]{1,0:T(8,128)(2,1)} %all-gather.19.cloned.1.call-done) | copy-start | bytes 7077892
  1322.3 134.4 %all-gather.35.cloned.1.call-start = ((), (), s32[]{:S(2)}) async-start(), calls=%async_computation.25 | async-start | bytes 3538944 | tf_op jit(solution)/shard_map/all_gather | solution.py:254
  1323.0 207.0 %all-gather.41.cloned.1.call-start = ((), (), s32[]{:S(2)}) async-start(), calls=%async_computation.32 | async-start | bytes 3538944 | tf_op jit(solution)/shard_map/all_gather | solution.py:376
  1363.7 186.0 %reduce-scatter.32.cloned.1.call-start = ((), (), s32[]{:S(2)}) async-start(), calls=%async_computation.36 | async-start | bytes 10027008 | tf_op jit(solution)/shard_map/reduce_scatter | solution.py:395
  1372.2 293.8 %reduce-scatter.26.cloned.1.call-start = ((), (), s32[]{:S(2)}) async-start(), calls=%async_computation.33 | async-start | bytes 10027008 | tf_op jit(solution)/shard_map/reduce_scatter | solution.py:392
  1379.1 366.8 %reduce-scatter.30.cloned.1.call-start = ((), (), s32[]{:S(2)}) async-start(), calls=%async_computation.35 | async-start | bytes 5013504 | tf_op jit(solution)/shard_map/reduce_scatter | solution.py:394
  1383.9 441.4 %reduce-scatter.28.cloned.1.call-start = ((), (), s32[]{:S(2)}) async-start(), calls=%async_computation.34 | async-start | bytes 5013504 | tf_op jit(solution)/shard_map/reduce_scatter | solution.py:393
  1388.7 845.0 %reduce-scatter.38.cloned.1.call-start = ((), (), s32[]{:S(2)}) async-start(), calls=%async_computation.39 | async-start | bytes 45121536 | tf_op jit(solution)/shard_map/reduce_scatter | solution.py:387
  1411.0 1231.8 %reduce-scatter.34.cloned.1.call-start = ((), (), s32[]{:S(2)}) async-start(), calls=%async_computation.37 | async-start | bytes 45121536 | tf_op jit(solution)/shard_map/reduce_scatter | solution.py:385
  1432.8 1618.4 %reduce-scatter.36.cloned.1.call-start = ((), (), s32[]{:S(2)}) async-start(), calls=%async_computation.38 | async-start | bytes 45121536 | tf_op jit(solution)/shard_map/reduce_scatter | solution.py:386
  (75 other events, 719.6 us)
Sparse Core Ops, SparseCore 0:
  10.3 45.1 all-gather.14
  57.8 41.0 all-gather.18
  101.2 52.1 all-gather.22
  156.0 49.1 all-gather.16
  207.8 49.0 all-gather.20
  259.0 51.8 all-gather.24
  318.4 58.5 reduce-scatter.13
  383.4 36.0 all-gather.26
  421.1 110.0 all-gather.28
  532.8 110.0 all-gather.30
  644.6 110.0 all-gather.32
  771.9 60.0 reduce-scatter.15
  840.4 36.0 all-gather.36
  936.2 59.9 reduce-scatter.17
  1005.1 36.0 all-gather.38
  1100.1 104.6 reduce-scatter.21
  1209.3 104.4 reduce-scatter.19
  1322.4 34.4 reduce-scatter.23
  1359.0 36.0 all-gather.34
  1397.1 36.0 all-gather.40
  1437.9 111.7 reduce-scatter.31
  1554.9 111.1 reduce-scatter.25
  1670.5 75.2 reduce-scatter.29
  1750.6 74.5 reduce-scatter.27
  1830.1 403.6 reduce-scatter.37
  2239.0 403.7 reduce-scatter.33
  2647.5 403.6 reduce-scatter.35
where the time goes:
time: 3070 us; the launch traced here: 3060 us
  waiting for transfers between devices  2500 us (81%)
  matrix products  275 us (9%)
  blocking collectives  131 us (4%)
  other arithmetic  72.6 us (2%)
  local copies, waits for them, and re-layouts  57.2 us (2%)
    reduce_scatter x1, waiting for transfers between devices, shards(): lax.psum_scatter(grad_gate_w, ('fsdp', 'ctx'), scatter_dimension=0, tiled...  409 us
    reduce_scatter x1, waiting for transfers between devices, shards(): lax.psum_scatter(grad_down_w, ('fsdp', 'ctx'), scatter_dimension=1, tiled...  408 us
    reduce_scatter x1, waiting for transfers between devices, shards(): lax.psum_scatter(grad_up_w, ('fsdp', 'ctx'), scatter_dimension=0, tiled=T...  408 us
    unnamed x2, blocking collectives  126 us
    reduce_scatter x1, waiting for transfers between devices, shards(): lax.psum_scatter(grad_query_w, ('fsdp', 'ctx'), scatter_dimension=0, tile...  116 us
    all_gather x1, waiting for transfers between devices, shards(): lax.all_gather(w_gate, ('fsdp', 'ctx'), axis=0, tiled=True)  112 us
    reduce_scatter x1, waiting for transfers between devices, shards(): lax.psum_scatter(key_term.reshape(-1, key_heads, HD), ('fsdp', 'ctx'), sc...  105 us
    all_gather x1, waiting for transfers between devices, shards(): lax.all_gather(w_up, ('fsdp', 'ctx'), axis=0, tiled=True)  93.3 us
  transfers between devices with their start and end apart: 27, of which 24 were waited for; matrix products, arithmetic and copies ran while one was open for 7% of the time, Pallas kernels for 0%

commit v1 on v0

v1 whole, which is shorter than its diff:
```python
import math

import jax
import jax.numpy as jnp
from jax import lax
from jax.sharding import PartitionSpec as P

HD = 256
PROMPT = 1024

soft_cap = 50.0
norm_eps = 1e-06
masked_fill = -1e30
bf16 = jnp.bfloat16
f32 = jnp.float32


def norm_parts(values):
    inverse = lax.rsqrt(jnp.mean(values * values, axis=-1, keepdims=True) + norm_eps)
    return (values * inverse, inverse)


def norm_back(grad_normal, normal, inverse):
    return inverse * (
        grad_normal - normal * jnp.mean(grad_normal * normal, axis=-1, keepdims=True)
    )


def rotary_tables(places, head_dim):
    half_dim = head_dim // 2
    frequency = jnp.exp(
        jnp.arange(half_dim, dtype=f32) * (-2.0 * math.log(10000.0) / head_dim)
    )
    angles = places[:, None] * frequency[None, :]
    return (jnp.cos(angles), jnp.sin(angles))


def rotary(values, cosine, sine_wave):
    half_dim = values.shape[-1] // 2
    front_half = values[..., :half_dim]
    back_half = values[..., half_dim:]
    return jnp.concatenate(
        [front_half * cosine - back_half * sine_wave, back_half * cosine + front_half * sine_wave],
        axis=-1,
    )


def matmul(left, right):
    return jnp.dot(left, right, preferred_element_type=f32)


def matmul_rt(left, right):
    return lax.dot_general(left, right, (((1,), (1,)), ((), ())), preferred_element_type=f32)


def matmul_lt(left, right):
    return lax.dot_general(left, right, (((0,), (0,)), ((), ())), preferred_element_type=f32)


def attend_forward(query, key, value, allowed):
    raw_scores = matmul_rt(query, key)
    capped = jnp.where(allowed, soft_cap * jnp.tanh(raw_scores / soft_cap), masked_fill)
    row_peak = jnp.max(capped, axis=-1, keepdims=True)
    exponent = jnp.exp(capped - row_peak)
    row_total = jnp.sum(exponent, axis=-1, keepdims=True)
    weight_set = (exponent / row_total).astype(bf16)
    return (matmul(weight_set, value), row_peak + jnp.log(row_total))


def attend_backward(query, key, value, allowed, log_total, grad_mixed):
    raw_scores = matmul_rt(query, key)
    squashed = jnp.tanh(raw_scores / soft_cap)
    capped = jnp.where(allowed, soft_cap * squashed, masked_fill)
    probabilities = jnp.exp(capped - log_total)
    weight_set = probabilities.astype(bf16)
    grad_value = matmul_lt(weight_set, grad_mixed)
    grad_probs = matmul_rt(grad_mixed, value)
    inner_sum = jnp.sum(probabilities * grad_probs, axis=-1, keepdims=True)
    grad_scores = (probabilities * (grad_probs - inner_sum) * (1.0 - squashed * squashed)).astype(
        bf16
    )
    return (matmul(grad_scores, key), matmul_lt(grad_scores, query), grad_value)


def shards(
    prompt_x,
    cont_x,
    cont_prompt,
    cont_len,
    attn_norm,
    attn_post,
    mlp_norm,
    mlp_post,
    w_query,
    w_key,
    w_value,
    w_out,
    w_gate,
    w_up,
    w_down,
    prompt_cot,
    cont_cot,
):
    width = prompt_x.shape[2]
    prompt_local = prompt_x.shape[1]
    cont_count = cont_x.shape[0]
    cont_size = cont_x.shape[1]
    cont_rows = cont_count * cont_size
    rows = prompt_local + cont_rows
    z_size = lax.axis_size("fsdp")
    c_size = lax.axis_size("ctx")
    y_size = c_size // 2
    z = lax.axis_index("fsdp")
    c = lax.axis_index("ctx")
    y = c // 2
    core = c % 2
    t = lax.axis_index("tp")
    part = w_query.shape[0]
    q_cols = w_query.shape[1] // 2
    kv_cols = w_key.shape[1] // 2
    shared_by = q_cols // kv_cols
    a_cols = q_cols + 2 * kv_cols
    block = w_gate.shape[1] // z_size
    share = rows // 2
    query_scale = HD ** (-0.5)

    def z_shift(values, step):
        return lax.ppermute(values, "fsdp", [(i, (i + step) % z_size) for i in range(z_size)])

    def y_next(values):
        return lax.ppermute(values, "ctx", [(i, (i + 2) % c_size) for i in range(c_size)])

    def core_swap(values):
        return lax.ppermute(values, "ctx", [(i, i ^ 1) for i in range(c_size)])

    def tp_swap(values):
        return lax.ppermute(values, "tp", [(0, 1), (1, 0)])

    def by_core(own, other):
        return (jnp.where(core == 0, own, other), jnp.where(core == 0, other, own))

    def gather_grid(own):
        held = jnp.zeros((z_size, y_size) + own.shape, own.dtype)
        tail = (0,) * own.ndim
        chunk = own
        for step in range(z_size):
            if step:
                chunk = z_shift(chunk, 1)
            turn = chunk
            for hop in range(y_size):
                if hop:
                    turn = y_next(turn)
                held = lax.dynamic_update_slice(
                    held,
                    turn[None, None],
                    ((z - step) % z_size, (y - hop) % y_size) + tail,
                )
        return held

    def scatter_grid(take):
        sums = {}
        for step in list(range(1, z_size)) + [0]:
            to_z = (z - step) % z_size
            total = take(to_z, (y - 1) % y_size)
            for hop in range(2, y_size + 1):
                total = y_next(total.astype(bf16)).astype(f32) + take(to_z, (y - hop) % y_size)
            sums[step] = total
        total = sums[1]
        for step in list(range(2, z_size)) + [0]:
            total = z_shift(total.astype(bf16), 1).astype(f32) + sums[step]
        return total

    def taker(values):
        tail = (0,) * (values.ndim - 2)

        def take(z_at, y_at):
            piece = lax.dynamic_slice(values, (z_at, y_at) + tail, (1, 1) + values.shape[2:])
            return piece[0, 0].astype(f32)

        return take

    def take_share(values):
        return lax.dynamic_slice_in_dim(values, t * share, share, 0)

    def give_share(values):
        return lax.dynamic_slice_in_dim(values, (1 - t) * share, share, 0)

    def rows_of(mine, other):
        return jnp.concatenate(
            [jnp.where(t == 0, mine, other), jnp.where(t == 0, other, mine)], axis=0
        )

    gain_one = attn_norm.astype(f32)[:, None]
    gain_three = mlp_norm.astype(f32)[:, None]
    scaled_q = (w_query.astype(f32) * gain_one).astype(bf16)
    scaled_k = (w_key.astype(f32) * gain_one).astype(bf16)
    scaled_v = (w_value.astype(f32) * gain_one).astype(bf16)

    def head_cols(which):
        return jnp.concatenate(
            [
                lax.dynamic_slice_in_dim(scaled_q, which * q_cols, q_cols, 1),
                lax.dynamic_slice_in_dim(scaled_k, which * kv_cols, kv_cols, 1),
                lax.dynamic_slice_in_dim(scaled_v, which * kv_cols, kv_cols, 1),
            ],
            axis=1,
        )

    mine, other = by_core(head_cols(core), core_swap(head_cols(1 - core)))
    attn_w = gather_grid(jnp.stack([mine, other], axis=0)).reshape(width, a_cols)

    post_low = jnp.zeros((1, 8, 256), bf16)
    post_low = post_low.at[0, 0, :part].set(attn_post).at[0, 1, :part].set(mlp_post)
    post_all = lax.all_gather(post_low, ("fsdp", "ctx"), axis=0, tiled=True)
    post_attn = post_all[:, 0, :part].reshape(1, width).astype(f32)
    post_mlp = post_all[:, 1, :part].reshape(1, width).astype(f32)

    residual = jnp.concatenate(
        [prompt_x.reshape(prompt_local, width), cont_x.reshape(cont_rows, width)], axis=0
    ).astype(f32)
    normal_one, inverse_one = norm_parts(residual)
    normal_low = normal_one.astype(bf16)
    chip_rows = jnp.concatenate([normal_low, core_swap(normal_low)], axis=0)

    out_t = w_out.T
    mine, other = by_core(
        lax.dynamic_slice_in_dim(out_t, core * q_cols, q_cols, 1),
        core_swap(lax.dynamic_slice_in_dim(out_t, (1 - core) * q_cols, q_cols, 1)),
    )
    out_w = gather_grid(jnp.stack([mine, other], axis=0)).reshape(width, q_cols)

    def mlp_weight(local):
        blocks = local.reshape(part, z_size, block)
        held = jnp.zeros((z_size, part, block), bf16)
        for step in range(z_size):
            piece = lax.dynamic_slice_in_dim(local, ((z + step) % z_size) * block, block, 1)
            if step:
                piece = z_shift(piece, step)
            held = lax.dynamic_update_slice(held, piece[None], ((z - step) % z_size, 0, 0))
        del blocks
        full = jnp.zeros((z_size, y_size, 2, part, block), bf16)
        turn = held
        for hop in range(y_size):
            if hop:
                turn = y_next(turn)
            cross = tp_swap(turn)
            keep = jnp.where(t == core, turn, cross)
            give = jnp.where(t == core, cross, turn)
            got = core_swap(give)
            y_at = (y - hop) % y_size
            full = lax.dynamic_update_slice(full, keep[:, None, None], (0, y_at, core, 0, 0))
            full = lax.dynamic_update_slice(full, got[:, None, None], (0, y_at, 1 - core, 0, 0))
        return full.reshape(width, block)

    gate_w = mlp_weight((w_gate.astype(f32) * gain_three).astype(bf16))
    up_w = mlp_weight((w_up.astype(f32) * gain_three).astype(bf16))
    down_w = mlp_weight(w_down.T)

    core_of = (core, 1 - core)
    cont_places = PROMPT + jnp.tile(jnp.arange(cont_size, dtype=jnp.int32), cont_count)
    prompt_places = [
        (y * 2 + which) * prompt_local + jnp.arange(prompt_local, dtype=jnp.int32)
        for which in core_of
    ]
    places = jnp.concatenate(
        [prompt_places[0], cont_places, prompt_places[1], cont_places]
    ).astype(f32)
    cosine, sine_wave = rotary_tables(places, HD)
    projected = matmul(chip_rows, attn_w)
    query_rows = jnp.stack(
        [
            (rotary(projected[:, i * HD : (i + 1) * HD], cosine, sine_wave) * query_scale).astype(bf16)
            for i in range(shared_by)
        ],
        axis=0,
    ).reshape(shared_by, 2, rows, HD)
    key_rows = rotary(projected[:, q_cols : q_cols + HD], cosine, sine_wave).astype(bf16)
    value_rows = projected[:, q_cols + HD :].astype(bf16)
    kv_rows = jnp.concatenate([key_rows, value_rows], axis=1).reshape(2, rows, 2 * HD)
    prompt_kv = kv_rows[:, :prompt_local].reshape(2 * prompt_local, 2 * HD)
    every_kv = gather_grid(prompt_kv).reshape(z_size, y_size * 2 * prompt_local, 2 * HD)
    span = every_kv.shape[1]
    own_kv = lax.dynamic_slice(every_kv, (z, 0, 0), (1, span, 2 * HD))[0]
    key_places = (
        (jnp.arange(y_size, dtype=jnp.int32)[:, None, None] * 2
         + jnp.stack(core_of)[None, :, None]) * prompt_local
        + jnp.arange(prompt_local, dtype=jnp.int32)[None, None, :]
    ).reshape(1, span)
    head_places = jnp.tile(jnp.concatenate(prompt_places), shared_by)
    prompt_allowed = key_places <= head_places[:, None]
    cont_allowed = jnp.tile(
        jnp.arange(span + cont_size, dtype=jnp.int32)[None, :]
        <= span + jnp.arange(cont_size, dtype=jnp.int32)[:, None],
        (shared_by, 1),
    )
    prompt_query = query_rows[:, :, :prompt_local].reshape(-1, HD)
    prompt_mixed, prompt_total = attend_forward(
        prompt_query, own_kv[:, :HD], own_kv[:, HD:], prompt_allowed
    )
    prompt_mixed = prompt_mixed.astype(bf16).reshape(shared_by, 2, prompt_local, HD)
    other_prompt = core_swap(cont_prompt)
    which_prompt = [cont_prompt[i] for i in range(cont_count)] + [
        other_prompt[i] for i in range(cont_count)
    ]
    conts = []
    for i in range(2 * cont_count):
        at = prompt_local + (i % cont_count) * cont_size
        half = i // cont_count
        kv = jnp.concatenate(
            [
                lax.dynamic_slice(every_kv, (which_prompt[i], 0, 0), (1, span, 2 * HD))[0],
                kv_rows[half, at : at + cont_size],
            ],
            axis=0,
        )
        query = query_rows[:, half, at : at + cont_size].reshape(-1, HD)
        mixed, total = attend_forward(query, kv[:, :HD], kv[:, HD:], cont_allowed)
        conts.append((query, kv, mixed.astype(bf16).reshape(shared_by, cont_size, HD), total))

    def rows_order(prompt_part, cont_parts):
        halves = []
        for half in range(2):
            pieces = [prompt_part[:, half]] + cont_parts[half * cont_count : (half + 1) * cont_count]
            halves.append(jnp.concatenate(pieces, axis=1))
        heads = jnp.concatenate(halves, axis=1)
        return jnp.concatenate([heads[i] for i in range(shared_by)], axis=1)

    attn_out = rows_order(prompt_mixed, [entry[2] for entry in conts])

    def to_shares(partial):
        low = partial.astype(bf16)
        summed = partial[:rows] + core_swap(low[rows:]).astype(f32)
        return take_share(summed) + tp_swap(give_share(summed).astype(bf16)).astype(f32)

    branch = to_shares(matmul_rt(attn_out, out_w))

    normal_two, inverse_two = norm_parts(branch)
    middle = take_share(residual) + normal_two * post_attn
    normal_three, inverse_three = norm_parts(middle)

    def ring_rows(own, step_fn):
        sums = []
        chunk = own
        for step in range(z_size):
            if step:
                chunk = z_shift(chunk, 1)
            both = jnp.concatenate([chunk, core_swap(chunk)], axis=0)
            partial = step_fn(step, both)
            sums.append(
                partial[:share] + core_swap(partial[share:].astype(bf16)).astype(f32)
            )
        total = sums[1]
        for step in list(range(2, z_size)) + [0]:
            total = z_shift(total.astype(bf16), 1).astype(f32) + sums[step]
        return total

    mlp_in, gates, ups, inners = {}, {}, {}, {}

    def mlp_forward(step, both):
        mlp_in[step] = both
        gates[step] = matmul(both, gate_w)
        ups[step] = matmul(both, up_w)
        inners[step] = (jax.nn.gelu(gates[step], approximate=True) * ups[step]).astype(bf16)
        return matmul_rt(inners[step], down_w)

    mlp_share = ring_rows(normal_three.astype(bf16), mlp_forward)

    normal_four, inverse_four = norm_parts(mlp_share)
    cont_live = (
        (jnp.arange(cont_size, dtype=jnp.int32)[None, :] < cont_len[:, None])
        .astype(f32)
        .reshape(cont_rows)
    )
    live_rows = jnp.concatenate([jnp.ones((prompt_local,), f32), cont_live])
    live = take_share(live_rows)[:, None]
    result_share = ((middle + normal_four * post_mlp) * live).astype(bf16)
    result_rows = rows_of(result_share, tp_swap(result_share))
    cot_rows = jnp.concatenate(
        [prompt_cot.reshape(prompt_local, width), cont_cot.reshape(cont_rows, width)], axis=0
    )
    grad_result = take_share(cot_rows).astype(f32) * live
    grad_post_mlp = jnp.sum(grad_result * normal_four, axis=0)
    grad_mlp = norm_back(grad_result * post_mlp, normal_four, inverse_four)

    grad_outs, grad_gates, grad_ups = {}, {}, {}

    def mlp_backward(step, both):
        grad_outs[step] = both
        grad_inner = matmul(both, down_w)
        pull = jax.vjp(
            lambda gate_in, up_in: jax.nn.gelu(gate_in, approximate=True) * up_in,
            gates[step],
            ups[step],
        )[1]
        grad_gate, grad_up = pull(grad_inner)
        grad_gates[step] = grad_gate.astype(bf16)
        grad_ups[step] = grad_up.astype(bf16)
        return matmul_rt(grad_gates[step], gate_w) + matmul_rt(grad_ups[step], up_w)

    grad_three = ring_rows(grad_mlp.astype(bf16), mlp_backward)

    def joined(pieces):
        return jnp.concatenate([pieces[step] for step in range(z_size)], axis=0)

    all_in, all_grad = joined(mlp_in), joined(grad_outs)
    grad_down_w = matmul_lt(all_grad, joined(inners)).astype(bf16)
    grad_gate_w = matmul_lt(all_in, joined(grad_gates)).astype(bf16)
    grad_up_w = matmul_lt(all_in, joined(grad_ups)).astype(bf16)

    def mlp_grad(full):
        full = full.reshape(z_size, y_size, 2, part, block)

        def of_core(which):
            return lax.dynamic_slice(
                full, (0, 0, which, 0, 0), (z_size, y_size, 1, part, block)
            )[:, :, 0]

        mine, got = of_core(core), core_swap(of_core(1 - core))
        keep = jnp.where(t == core, mine, got).astype(f32)
        summed = keep + tp_swap(jnp.where(t == core, got, mine)).astype(f32)

        def y_term(at):
            return lax.dynamic_slice(summed, (0, at, 0, 0), (z_size, 1, part, block))[:, 0]

        total = y_term((y - 1) % y_size)
        for hop in range(2, y_size + 1):
            total = y_next(total.astype(bf16)).astype(f32) + y_term((y - hop) % y_size)
        low = total.astype(bf16)
        held = jnp.zeros((part, z_size * block), bf16)
        for step in range(z_size):
            piece = lax.dynamic_slice_in_dim(low, (z + step) % z_size, 1, 0)[0]
            if step:
                piece = z_shift(piece, step)
            held = lax.dynamic_update_slice(held, piece, (0, ((z - step) % z_size) * block))
        return held.astype(f32)

    raw_down = mlp_grad(grad_down_w)
    raw_gate = mlp_grad(grad_gate_w)
    raw_up = mlp_grad(grad_up_w)

    grad_middle = grad_result + norm_back(grad_three, normal_three, inverse_three)
    grad_post_attn = jnp.sum(grad_middle * normal_two, axis=0)
    grad_branch = norm_back(grad_middle * post_attn, normal_two, inverse_two).astype(bf16)
    branch_rows = rows_of(grad_branch, tp_swap(grad_branch))
    branch_chip = jnp.concatenate([branch_rows, core_swap(branch_rows)], axis=0)
    grad_attn = matmul(branch_chip, out_w).astype(bf16)
    grad_out_w = matmul_lt(branch_chip, attn_out).astype(bf16)
    post_terms = jnp.stack([grad_post_attn, grad_post_mlp], axis=1).astype(bf16)
    grad_out_w = jnp.concatenate(
        [grad_out_w, post_terms, jnp.zeros((width, 126), bf16)], axis=1
    ).reshape(z_size, y_size, 2 * part, q_cols + 128)
    out_sum = scatter_grid(taker(grad_out_w))

    grad_heads = jnp.stack(
        [grad_attn[:, i * HD : (i + 1) * HD] for i in range(shared_by)], axis=0
    ).reshape(shared_by, 2, rows, HD)
    prompt_gq, prompt_gk, prompt_gv = attend_backward(
        prompt_query,
        own_kv[:, :HD],
        own_kv[:, HD:],
        prompt_allowed,
        prompt_total,
        grad_heads[:, :, :prompt_local].reshape(-1, HD),
    )
    prompt_gkv = jnp.concatenate([prompt_gk, prompt_gv], axis=1)
    cont_gq, cont_gkv, own_gkv = [], [], []
    for i in range(2 * cont_count):
        at = prompt_local + (i % cont_count) * cont_size
        half = i // cont_count
        query, kv, _, total = conts[i]
        gq, gk, gv = attend_backward(
            query,
            kv[:, :HD],
            kv[:, HD:],
            cont_allowed,
            total,
            grad_heads[:, half, at : at + cont_size].reshape(-1, HD),
        )
        cont_gq.append(gq.reshape(shared_by, cont_size, HD))
        gkv = jnp.concatenate([gk, gv], axis=1)
        cont_gkv.append(gkv[:span])
        own_gkv.append(gkv[span:])

    def kv_take(z_at, y_at):
        length = 2 * prompt_local
        def piece(values):
            return lax.dynamic_slice_in_dim(values, y_at * length, length, 0)

        total = jnp.where(z_at == z, piece(prompt_gkv), 0.0)
        for which, term in zip(which_prompt, cont_gkv):
            total = total + jnp.where(z_at == which, piece(term), 0.0)
        return total

    kv_sum = scatter_grid(kv_take).reshape(2, prompt_local, 2 * HD)
    halves = []
    for half in range(2):
        halves.append(kv_sum[half])
        halves.extend(own_gkv[half * cont_count : (half + 1) * cont_count])
    grad_kv = jnp.concatenate(halves, axis=0)
    grad_q = rows_order(prompt_gq.reshape(shared_by, 2, prompt_local, HD), cont_gq)
    grad_proj = jnp.concatenate(
        [
            rotary(grad_q[:, i * HD : (i + 1) * HD] * query_scale, cosine, -sine_wave)
            for i in range(shared_by)
        ]
        + [rotary(grad_kv[:, :HD], cosine, -sine_wave), grad_kv[:, HD:]],
        axis=1,
    ).astype(bf16)
    grad_attn_w = matmul_lt(chip_rows, grad_proj).astype(bf16)
    attn_sum = scatter_grid(taker(grad_attn_w.reshape(z_size, y_size, 2 * part, a_cols)))
    grad_one = to_shares(matmul_rt(grad_proj, attn_w))
    grad_input = grad_middle + norm_back(grad_one, take_share(normal_one), take_share(inverse_one))
    input_low = grad_input.astype(bf16)
    input_rows = rows_of(input_low, tp_swap(input_low)).astype(f32)

    def split_core(summed):
        mine = lax.dynamic_slice_in_dim(summed, core * part, part, 0)
        give = lax.dynamic_slice_in_dim(summed, (1 - core) * part, part, 0).astype(bf16)
        return mine, core_swap(give).astype(f32)

    out_mine, out_got = split_core(out_sum)
    first, second = by_core(out_mine[:, :q_cols], out_got[:, :q_cols])
    grad_out = jnp.concatenate([first, second], axis=1).T
    post_sum = out_mine[:, q_cols : q_cols + 2] + out_got[:, q_cols : q_cols + 2]
    attn_mine, attn_got = split_core(attn_sum)
    first, second = by_core(attn_mine, attn_got)

    def both_cores(start, size):
        return jnp.concatenate([first[:, start : start + size], second[:, start : start + size]], axis=1)

    raw_q = both_cores(0, q_cols)
    raw_k = both_cores(q_cols, kv_cols)
    raw_v = both_cores(q_cols + kv_cols, kv_cols)

    def gain_sum(raw, weight):
        return jnp.sum(raw * weight.astype(f32), axis=1)

    gain_terms = jnp.stack(
        [
            gain_sum(raw_q, w_query) + gain_sum(raw_k, w_key) + gain_sum(raw_v, w_value),
            post_sum[:, 0],
            gain_sum(raw_gate, w_gate) + gain_sum(raw_up, w_up),
            post_sum[:, 1],
        ],
        axis=0,
    )
    gain_grads = gain_terms + tp_swap(gain_terms)

    return (
        result_rows[:prompt_local].reshape(1, prompt_local, width),
        result_rows[prompt_local:].reshape(cont_count, cont_size, width),
        input_rows[:prompt_local].reshape(1, prompt_local, width),
        input_rows[prompt_local:].reshape(cont_count, cont_size, width),
        gain_grads[0],
        gain_grads[1],
        gain_grads[2],
        gain_grads[3],
        raw_q * gain_one,
        raw_k * gain_one,
        raw_v * gain_one,
        grad_out,
        raw_gate * gain_three,
        raw_up * gain_three,
        raw_down.T,
    )


def solution(mesh):
    in_specs = (
        P("fsdp", "ctx", None),
        P(("fsdp", "ctx"), None, None),
        P(("fsdp", "ctx")),
        P(("fsdp", "ctx")),
        P(("fsdp", "ctx")),
        P(("fsdp", "ctx")),
        P(("fsdp", "ctx")),
        P(("fsdp", "ctx")),
        P(("fsdp", "ctx"), "tp"),
        P(("fsdp", "ctx"), "tp"),
        P(("fsdp", "ctx"), "tp"),
        P("tp", ("fsdp", "ctx")),
        P(("fsdp", "ctx"), "tp"),
        P(("fsdp", "ctx"), "tp"),
        P("tp", ("fsdp", "ctx")),
        P("fsdp", "ctx", None),
        P(("fsdp", "ctx"), None, None),
    )
    out_specs = (
        P("fsdp", "ctx", None),
        P(("fsdp", "ctx"), None, None),
        P("fsdp", "ctx", None),
        P(("fsdp", "ctx"), None, None),
        P(("fsdp", "ctx")),
        P(("fsdp", "ctx")),
        P(("fsdp", "ctx")),
        P(("fsdp", "ctx")),
        P(("fsdp", "ctx"), "tp"),
        P(("fsdp", "ctx"), "tp"),
        P(("fsdp", "ctx"), "tp"),
        P("tp", ("fsdp", "ctx")),
        P(("fsdp", "ctx"), "tp"),
        P(("fsdp", "ctx"), "tp"),
        P("tp", ("fsdp", "ctx")),
    )
    return jax.shard_map(shards, mesh=mesh, in_specs=in_specs, out_specs=out_specs, check_vma=False)
```

time: 3070 us -> 1480 us (0.48)
  waiting for transfers between devices: 2500 us -> 856 us
  blocking collectives: 131 us -> 26.3 us
  starting transfers between devices: 2.11 us -> 102 us
  other arithmetic: 72.6 us -> 144 us
  matrix products: 275 us -> 231 us
  local copies, waits for them, and re-layouts: 57.2 us -> 100 us
    reduce_scatter x13 -> x0, waiting for transfers between devices: 1920 us -> none  [the longest x1 409 us: shards(): lax.psum_scatter(grad_gate_w, ('fsdp', 'ctx'), scatter_dimension=0, tiled...]
    ppermute x0 -> x127, waiting for transfers between devices: none -> 856 us  [the longest x48 381 us: z_shift(): lax.ppermute(values, 'fsdp', [(i, (i + step) % z_size) for i in range(z_s...]
    all_gather x14 -> x0, waiting for transfers between devices: 580 us -> none  [the longest x1 112 us: shards(): lax.all_gather(w_gate, ('fsdp', 'ctx'), axis=0, tiled=True)]
    unnamed x2 -> x0, blocking collectives: 126 us -> none
    ppermute x0 -> x127, starting transfers between devices: none -> 102 us  [the longest x48 54.1 us: z_shift(): lax.ppermute(values, 'fsdp', [(i, (i + step) % z_size) for i in range(z_s...]
    dot_general x33 -> x51, matrix products: 275 us -> 231 us  [the longest x20 82.3 us: matmul(): return jnp.dot(left, right, preferred_element_type=f32)]
  transfers between devices with their start and end apart: 27 -> 127, of which waited for: 24 -> 49; matrix products, arithmetic and copies ran while one was open for 7% -> 30% of each run, Pallas kernels for 0% -> 0%
where the time goes in v1:
time: 1480 us; the launch traced here: 1470 us
  waiting for transfers between devices  856 us (58%)
  matrix products  231 us (16%)
  other arithmetic  144 us (10%)
  starting transfers between devices  102 us (7%)
  local copies, waits for them, and re-layouts  100 us (7%)
  blocking collectives  26.3 us (2%)
    ppermute x48, waiting for transfers between devices, z_shift(): lax.ppermute(values, 'fsdp', [(i, (i + step) % z_size) for i in range(z_s...  381 us
    ppermute x15, waiting for transfers between devices, tp_swap(): return lax.ppermute(values, 'tp', [(0, 1), (1, 0)])  360 us
    ppermute x30, waiting for transfers between devices, y_next(): lax.ppermute(values, 'ctx', [(i, (i + 2) % c_size) for i in range(c_size)])  112 us
    dot_general x20, matrix products, matmul(): return jnp.dot(left, right, preferred_element_type=f32)  82.3 us
    dot_general x20, matrix products, matmul_rt(): lax.dot_general(left, right, (((1,), (1,)), ((), ())), preferred_element_...  79.2 us
    dot_general x11, matrix products, matmul_lt(): lax.dot_general(left, right, (((0,), (0,)), ((), ())), preferred_element_...  69.8 us
    ppermute x48, starting transfers between devices, z_shift(): lax.ppermute(values, 'fsdp', [(i, (i + step) % z_size) for i in range(z_s...  54.1 us
    unnamed x353, local copies, waits for them, and re-layouts  42.3 us
  transfers between devices with their start and end apart: 127, of which 49 were waited for; matrix products, arithmetic and copies ran while one was open for 30% of the time, Pallas kernels for 0%

profile of v1, /device:TPU:0, one launch (start us, length us, event | category | flops | bytes accessed | tf_op | source)
XLA Modules:
  0.0 1470.3 jit_solution(375553717822300617)
XLA Ops:
  18.6 26.3 %all_gather.3 = bf16[16,8,256]{2,1,0:T(8,128)(2,1)S(1)} all-gather(bf16[1,8,256]{2,1,0:T(8,128)(2,1)S(1)} %scatter.9), channel_id=1, replica_groups=mesh['fsdp'=4,'ctx'=4,'tp'=2] {'fsdp','ctx'}, dimensions={0}, use_global_device_ids=true | all-gather | bytes 69632 | tf_op jit(solution)/shard_map/all_gather | solution.py:214
  73.1 19.2 %collective-permute-done.37 = bf16[144,1152]{1,0:T(8,128)(2,1)S(1)} collective-permute-done((bf16[144,1152]{1,0:T(8,128)(2,1)S(1)}, bf16[144,1152]{1,0:T(8,128)(2,1)S(1)}, u32[]{:S(2)}, u32[]{:S(2)}) %collective-permute-start.37) | collective-permute-done | bytes 331808 | tf_op jit(solution)/shard_map/ppermute | solution.py:128
  92.3 21.0 %collective-permute-start.30 = (bf16[144,1152]{1,0:T(8,128)(2,1)S(1)}, bf16[144,1152]{1,0:T(8,128)(2,1)S(1)}, u32[]{:S(2)}, u32[]{:S(2)}) collective-permute-start(bf16[144,1152]{1,0:T(8,128)(2,1)S(1)} %copy-done.79), channel_id=1, source_target_pairs={{0,16},{8,24},{16,0},{24,8},{1,17},{9,25},{17,1},{25,9},{2,18},{10... | collective-permute-start | bytes 995336 | tf_op jit(solution)/shard_map/ppermute | solution.py:128
  118.6 17.5 %collective-permute-done.29 = bf16[144,1152]{1,0:T(8,128)(2,1)S(1)} collective-permute-done((bf16[144,1152]{1,0:T(8,128)(2,1)S(1)}, bf16[144,1152]{1,0:T(8,128)(2,1)S(1)}, u32[]{:S(2)}, u32[]{:S(2)}) %collective-permute-start.29) | collective-permute-done | bytes 331808 | tf_op jit(solution)/shard_map/ppermute | solution.py:128
  150.7 21.7 %collective-permute-done.21 = bf16[2,144,512]{2,1,0:T(8,128)(2,1)S(1)} collective-permute-done((bf16[2,144,512]{2,1,0:T(8,128)(2,1)S(1)}, bf16[2,144,512]{2,1,0:T(8,128)(2,1)S(1)}, u32[]{:S(2)}, u32[]{:S(2)}) %collective-permute-start.21) | collective-permute-done | bytes 294944 | tf_op jit(solution)/shard_map/ppermute | solution.py:128
  187.7 17.3 %collective-permute-done.24 = bf16[2,144,512]{2,1,0:T(8,128)(2,1)S(1)} collective-permute-done((bf16[2,144,512]{2,1,0:T(8,128)(2,1)S(1)}, bf16[2,144,512]{2,1,0:T(8,128)(2,1)S(1)}, u32[]{:S(2)}, u32[]{:S(2)}) %collective-permute-start.24) | collective-permute-done | bytes 294944 | tf_op jit(solution)/shard_map/ppermute | solution.py:131
  210.7 26.4 %collective-permute-done.32 = bf16[4,144,1152]{2,1,0:T(8,128)(2,1)S(1)} collective-permute-done((bf16[4,144,1152]{2,1,0:T(8,128)(2,1)S(1)}, bf16[4,144,1152]{2,1,0:T(8,128)(2,1)S(1)}, u32[]{:S(2)}, u32[]{:S(2)}) %collective-permute-start.32) | collective-permute-done | bytes 1327136 | tf_op jit(solution)/shard_map/ppermute | solution.py:137
  238.6 19.9 %collective-permute-done.40 = bf16[4,144,1152]{2,1,0:T(8,128)(2,1)S(1)} collective-permute-done((bf16[4,144,1152]{2,1,0:T(8,128)(2,1)S(1)}, bf16[4,144,1152]{2,1,0:T(8,128)(2,1)S(1)}, u32[]{:S(2)}, u32[]{:S(2)}) %collective-permute-start.40) | collective-permute-done | bytes 1327136 | tf_op jit(solution)/shard_map/ppermute | solution.py:137
  275.7 36.0 %collective-permute-done.8 = bf16[2,144,1024]{2,1,0:T(8,128)(2,1)S(1)} collective-permute-done((bf16[2,144,1024]{2,1,0:T(8,128)(2,1)S(1)}, bf16[2,144,1024]{2,1,0:T(8,128)(2,1)S(1)}, u32[]{:S(2)}, u32[]{:S(2)}) %collective-permute-start.8) | collective-permute-done | bytes 589856 | tf_op jit(solution)/shard_map/ppermute | solution.py:131
  330.5 13.8 collective-permute-done.51
  345.6 27.2 %collective-permute-done.35 = bf16[4,144,1152]{2,1,0:T(8,128)(2,1)S(1)} collective-permute-done((bf16[4,144,1152]{2,1,0:T(8,128)(2,1)S(1)}, bf16[4,144,1152]{2,1,0:T(8,128)(2,1)S(1)}, u32[]{:S(2)}, u32[]{:S(2)}) %collective-permute-start.35) | collective-permute-done | bytes 1327136 | tf_op jit(solution)/shard_map/ppermute | solution.py:137
  374.3 26.1 %collective-permute-done.43 = bf16[4,144,1152]{2,1,0:T(8,128)(2,1)S(1)} collective-permute-done((bf16[4,144,1152]{2,1,0:T(8,128)(2,1)S(1)}, bf16[4,144,1152]{2,1,0:T(8,128)(2,1)S(1)}, u32[]{:S(2)}, u32[]{:S(2)}) %collective-permute-start.43) | collective-permute-done | bytes 1327136 | tf_op jit(solution)/shard_map/ppermute | solution.py:137
  468.3 27.1 %collective-permute-done.26 = bf16[256,2304]{1,0:T(8,128)(2,1)S(1)} collective-permute-done((bf16[256,2304]{1,0:T(8,128)(2,1)S(1)}, bf16[256,2304]{1,0:T(8,128)(2,1)S(1)}, u32[]{:S(2)}, u32[]{:S(2)}) %collective-permute-start.26) | collective-permute-done | bytes 1179680 | tf_op jit(solution)/shard_map/ppermute | solution.py:137
  502.9 25.8 %collective-permute-done.27 = bf16[256,2304]{1,0:T(8,128)(2,1)S(1)} collective-permute-done((bf16[256,2304]{1,0:T(8,128)(2,1)S(1)}, bf16[256,2304]{1,0:T(8,128)(2,1)S(1)}, u32[]{:S(2)}, u32[]{:S(2)}) %collective-permute-start.27) | collective-permute-done | bytes 1179680 | tf_op jit(solution)/shard_map/ppermute | solution.py:128
  540.4 17.9 %collective-permute-done.55 = bf16[256,2304]{1,0:T(8,128)(2,1)S(1)} collective-permute-done((bf16[256,2304]{1,0:T(8,128)(2,1)S(1)}, bf16[256,2304]{1,0:T(8,128)(2,1)S(1)}, u32[]{:S(2)}, u32[]{:S(2)}) %collective-permute-start.55) | collective-permute-done | bytes 1179680 | tf_op jit(solution)/shard_map/ppermute | solution.py:128
  572.9 24.2 %collective-permute-done.59 = bf16[256,2304]{1,0:T(8,128)(2,1)S(1)} collective-permute-done((bf16[256,2304]{1,0:T(8,128)(2,1)S(1)}, bf16[256,2304]{1,0:T(8,128)(2,1)S(1)}, u32[]{:S(2)}, u32[]{:S(2)}) %collective-permute-start.59) | collective-permute-done | bytes 1179680 | tf_op jit(solution)/shard_map/ppermute | solution.py:128
  617.4 15.3 %collective-permute-done.54 = bf16[256,2304]{1,0:T(8,128)(2,1)S(1)} collective-permute-done((bf16[256,2304]{1,0:T(8,128)(2,1)S(1)}, bf16[256,2304]{1,0:T(8,128)(2,1)S(1)}, u32[]{:S(2)}, u32[]{:S(2)}) %collective-permute-start.54) | collective-permute-done | bytes 1179680 | tf_op jit(solution)/shard_map/ppermute | solution.py:128
  645.9 17.1 %collective-permute-done.58 = bf16[256,2304]{1,0:T(8,128)(2,1)S(1)} collective-permute-done((bf16[256,2304]{1,0:T(8,128)(2,1)S(1)}, bf16[256,2304]{1,0:T(8,128)(2,1)S(1)}, u32[]{:S(2)}, u32[]{:S(2)}) %collective-permute-start.58) | collective-permute-done | bytes 1179680 | tf_op jit(solution)/shard_map/ppermute | solution.py:128
  666.1 27.2 %collective-permute-done.62 = bf16[256,2304]{1,0:T(8,128)(2,1)} collective-permute-done((bf16[256,2304]{1,0:T(8,128)(2,1)}, bf16[256,2304]{1,0:T(8,128)(2,1)}, u32[]{:S(2)}, u32[]{:S(2)}) %collective-permute-start.62) | collective-permute-done | bytes 1179680 | tf_op jit(solution)/shard_map/ppermute | solution.py:128
  728.2 12.8 collective-permute-done.66
  794.9 14.5 collective-permute-done.74
  821.3 16.2 %convolution_convert_fusion = bf16[2304,1152]{1,0:T(8,128)(2,1)S(1)} fusion(bf16[2048,2304]{1,0:T(8,128)(2,1)} %constant_dynamic-update-slice_fusion.14, bf16[512,1152]{1,0:T(8,128)(2,1)} %copy-done.140, bf16[512,1152]{1,0:T(8,128)(2,1)} %copy-done.139, bf16[512,1152]{1,0:T(8,128)(2,1)} %copy-done.138, bf16[512,1152]{1,0:T(8,128)(2,1)} %copy-done.141), kind=kOutput, calls=%fused_computation | convolution fusion | flops 10893164544 | bytes 19464192 | tf_op jit(solution)/shard_map/dot_general | solution.py:57
  863.1 15.9 %convolution_convert_fusion.2 = bf16[2304,1152]{1,0:T(8,128)(2,1)S(1)} fusion(bf16[2048,2304]{1,0:T(8,128)(2,1)} %get-tuple-element.134, bf16[512,1152]{1,0:T(8,128)(2,1)} %get-tuple-element.80, bf16[512,1152]{1,0:T(8,128)(2,1)} %copy-done.128, bf16[512,1152]{1,0:T(8,128)(2,1)} %copy-done.127, bf16[512,1152]{1,0:T(8,128)(2,1)S(1)} %copy-done.126), kind=kOutput, calls=%fused_computation.2 | convolution fusion | flops 10893164544 | bytes 19464192 | tf_op jit(solution)/shard_map/dot_general | solution.py:57
  879.1 14.0 collective-permute-done.73
  894.5 16.1 %convolution_convert_fusion.1 = bf16[2304,1152]{1,0:T(8,128)(2,1)S(1)} fusion(bf16[2048,2304]{1,0:T(8,128)(2,1)} %get-tuple-element.134, bf16[512,1152]{1,0:T(8,128)(2,1)} %get-tuple-element.81, bf16[512,1152]{1,0:T(8,128)(2,1)} %copy-done.145, bf16[512,1152]{1,0:T(8,128)(2,1)} %copy-done.144, bf16[512,1152]{1,0:T(8,128)(2,1)S(1)} %copy-done.143), kind=kOutput, calls=%fused_computation.1 | convolution fusion | flops 10893164544 | bytes 19464192 | tf_op jit(solution)/shard_map/dot_general | solution.py:57
  943.9 76.6 %collective-permute-done.80 = bf16[256,2304]{1,0:T(8,128)(2,1)S(1)} collective-permute-done((bf16[256,2304]{1,0:T(8,128)(2,1)S(1)}, bf16[256,2304]{1,0:T(8,128)(2,1)S(1)}, u32[]{:S(2)}, u32[]{:S(2)}) %collective-permute-start.80) | collective-permute-done | bytes 1179680 | tf_op jit(solution)/shard_map/ppermute | solution.py:137
  1028.0 49.5 %collective-permute-done.115 = bf16[4,2,144,1152]{3,2,1,0:T(8,128)(2,1)} collective-permute-done((bf16[4,2,144,1152]{3,2,1,0:T(8,128)(2,1)}, bf16[4,2,144,1152]{3,2,1,0:T(8,128)(2,1)}, u32[]{:S(2)}, u32[]{:S(2)}) %collective-permute-start.115) | collective-permute-done | bytes 2654240 | tf_op jit(solution)/shard_map/ppermute | solution.py:137
  1081.6 49.2 %collective-permute-done.109 = bf16[4,2,144,1152]{3,2,1,0:T(8,128)(2,1)} collective-permute-done((bf16[4,2,144,1152]{3,2,1,0:T(8,128)(2,1)}, bf16[4,2,144,1152]{3,2,1,0:T(8,128)(2,1)}, u32[]{:S(2)}, u32[]{:S(2)}) %collective-permute-start.109) | collective-permute-done | bytes 2654240 | tf_op jit(solution)/shard_map/ppermute | solution.py:137
  1248.6 40.1 %collective-permute-done.125 = bf16[144,1152]{1,0:T(8,128)(2,1)S(1)} collective-permute-done((bf16[144,1152]{1,0:T(8,128)(2,1)S(1)}, bf16[144,1152]{1,0:T(8,128)(2,1)S(1)}, u32[]{:S(2)}, u32[]{:S(2)}) %collective-permute-start.125) | collective-permute-done | bytes 331808 | tf_op jit(solution)/shard_map/ppermute | solution.py:128
  1305.1 13.0 collective-permute-done.118
  1415.7 22.0 %collective-permute-done.90 = bf16[256,2304]{1,0:T(8,128)(2,1)S(1)} collective-permute-done((bf16[256,2304]{1,0:T(8,128)(2,1)S(1)}, bf16[256,2304]{1,0:T(8,128)(2,1)S(1)}, u32[]{:S(2)}, u32[]{:S(2)}) %collective-permute-start.90) | collective-permute-done | bytes 1179680 | tf_op jit(solution)/shard_map/ppermute | solution.py:137
  1444.2 21.9 %collective-permute-done.120 = f32[4,144]{1,0:T(4,128)S(1)} collective-permute-done((f32[4,144]{1,0:T(4,128)S(1)}, f32[4,144]{1,0:T(4,128)S(1)}, u32[]{:S(2)}, u32[]{:S(2)}) %collective-permute-start.120) | collective-permute-done | bytes 2336 | tf_op jit(solution)/shard_map/ppermute | solution.py:137
  (902 shorter events, 670.6 us)
Async XLA Ops:
  0.6 60.7 %collective-permute-start.16 = (s32[1]{0:T(128)}, s32[1]{0:T(128)}, u32[]{:S(2)}, u32[]{:S(2)}) collective-permute-start(s32[1]{0:T(128)} %param.23), channel_id=1, source_target_pairs={{0,2},{2,0},{4,6},{6,4},{1,3},{3,1},{5,7},{7,5},{8,10},{10,8},{12,... | collective-permute-start | bytes 20 | tf_op jit(solution)/shard_map/ppermute | solution.py:134
  2.7 60.7 %collective-permute-start.17 = (bf16[144,512]{1,0:T(8,128)(2,1)}, bf16[144,512]{1,0:T(8,128)(2,1)}, u32[]{:S(2)}, u32[]{:S(2)}) collective-permute-start(bf16[144,512]{1,0:T(8,128)(2,1)} %dynamic-slice_bitcast_fusion.26), channel_id=1, source_target_pairs={{0,2},{2,0},{4,6},{6,4},{1,3},{3,1},{5,7},{7,5},{8,10},{10,8},{12,... | collective-permute-start | bytes 442376 | tf_op jit(solution)/shard_map/ppermute | solution.py:134
  7.3 58.7 %collective-permute-start.1 = (bf16[144,1024]{1,0:T(8,128)(2,1)}, bf16[144,1024]{1,0:T(8,128)(2,1)}, u32[]{:S(2)}, u32[]{:S(2)}) collective-permute-start(bf16[144,1024]{1,0:T(8,128)(2,1)} %pad_maximum_fusion.23), channel_id=1, source_target_pairs={{0,2},{2,0},{4,6},{6,4},{1,3},{3,1},{5,7},{7,5},{8,10},{10,8},{12,... | collective-permute-start | bytes 884744 | tf_op jit(solution)/shard_map/ppermute | solution.py:134
  9.8 106.5 %collective-permute-start.47 = (bf16[144,1152]{1,0:T(8,128)(2,1)S(1)}, bf16[144,1152]{1,0:T(8,128)(2,1)}, u32[]{:S(2)}, u32[]{:S(2)}) collective-permute-start(bf16[144,1152]{1,0:T(8,128)(2,1)S(1)} %get-tuple-element.125), channel_id=1, source_target_pairs={{0,24},{8,0},{16,8},{24,16},{1,25},{9,1},{17,9},{25,17},{2,26},{10... | collective-permute-start | bytes 995336 | tf_op jit(solution)/shard_map/ppermute | solution.py:128
  14.5 55.4 %collective-permute-start.45 = (bf16[144,1152]{1,0:T(8,128)(2,1)}, bf16[144,1152]{1,0:T(8,128)(2,1)}, u32[]{:S(2)}, u32[]{:S(2)}) collective-permute-start(bf16[144,1152]{1,0:T(8,128)(2,1)} %get-tuple-element.126), channel_id=1, source_target_pairs={{0,8},{8,16},{16,24},{24,0},{1,9},{9,17},{17,25},{25,1},{2,10},{10... | collective-permute-start | bytes 995336 | tf_op jit(solution)/shard_map/ppermute | solution.py:128
  63.5 54.0 %collective-permute-start.39 = (bf16[144,1152]{1,0:T(8,128)(2,1)}, bf16[144,1152]{1,0:T(8,128)(2,1)S(1)}, u32[]{:S(2)}, u32[]{:S(2)}) collective-permute-start(bf16[144,1152]{1,0:T(8,128)(2,1)} %get-tuple-element.131), channel_id=1, source_target_pairs={{0,24},{8,0},{16,8},{24,16},{1,25},{9,1},{17,9},{25,17},{2,26},{10... | collective-permute-start | bytes 995336 | tf_op jit(solution)/shard_map/ppermute | solution.py:128
  92.2 57.6 %collective-permute-start.31 = (bf16[144,1152]{1,0:T(8,128)(2,1)S(1)}, bf16[144,1152]{1,0:T(8,128)(2,1)S(1)}, u32[]{:S(2)}, u32[]{:S(2)}) collective-permute-start(bf16[144,1152]{1,0:T(8,128)(2,1)S(1)} %copy-done.78), channel_id=1, source_target_pairs={{0,24},{8,0},{16,8},{24,16},{1,25},{9,1},{17,9},{25,17},{2,26},{10... | collective-permute-start | bytes 995336 | tf_op jit(solution)/shard_map/ppermute | solution.py:128
  92.3 56.0 %collective-permute-start.30 = (bf16[144,1152]{1,0:T(8,128)(2,1)S(1)}, bf16[144,1152]{1,0:T(8,128)(2,1)S(1)}, u32[]{:S(2)}, u32[]{:S(2)}) collective-permute-start(bf16[144,1152]{1,0:T(8,128)(2,1)S(1)} %copy-done.79), channel_id=1, source_target_pairs={{0,16},{8,24},{16,0},{24,8},{1,17},{9,25},{17,1},{25,9},{2,18},{10... | collective-permute-start | bytes 995336 | tf_op jit(solution)/shard_map/ppermute | solution.py:128
  116.4 198.0 %collective-permute-start = (bf16[512,2304]{1,0:T(8,128)(2,1)}, bf16[512,2304]{1,0:T(8,128)(2,1)}, u32[]{:S(2)}, u32[]{:S(2)}) collective-permute-start(bf16[512,2304]{1,0:T(8,128)(2,1)} %get-tuple-element.101), channel_id=1, source_target_pairs={{0,2},{2,0},{4,6},{6,4},{1,3},{3,1},{5,7},{7,5},{8,10},{10,8},{12,... | collective-permute-start | bytes 7077896 | tf_op jit(solution)/shard_map/ppermute | solution.py:134
  205.1 106.7 %collective-permute-start.50 = (bf16[4,144,1152]{2,1,0:T(8,128)(2,1)S(1)}, bf16[4,144,1152]{2,1,0:T(8,128)(2,1)S(1)}, u32[]{:S(2)}, u32[]{:S(2)}) collective-permute-start(bf16[4,144,1152]{2,1,0:T(8,128)(2,1)S(1)} %bitcast_dynamic-update-slice_fusion.31), channel_id=1, source_target_pairs={{0,4},{2,6},{4,0},{6,2},{1,5},{3,7},{5,1},{7,3},{8,12},{10,14},{12... | collective-permute-start | bytes 3981320 | tf_op jit(solution)/shard_map/ppermute | solution.py:131
  207.6 104.7 %collective-permute-start.34 = (bf16[4,144,1152]{2,1,0:T(8,128)(2,1)S(1)}, bf16[4,144,1152]{2,1,0:T(8,128)(2,1)S(1)}, u32[]{:S(2)}, u32[]{:S(2)}) collective-permute-start(bf16[4,144,1152]{2,1,0:T(8,128)(2,1)S(1)} %bitcast_dynamic-update-slice_fusion.38), channel_id=1, source_target_pairs={{0,4},{2,6},{4,0},{6,2},{1,5},{3,7},{5,1},{7,3},{8,12},{10,14},{12... | collective-permute-start | bytes 3981320 | tf_op jit(solution)/shard_map/ppermute | solution.py:131
  311.7 155.9 %collective-permute-start.49 = (bf16[4,144,1152]{2,1,0:T(8,128)(2,1)}, bf16[4,144,1152]{2,1,0:T(8,128)(2,1)S(1)}, u32[]{:S(2)}, u32[]{:S(2)}) collective-permute-start(bf16[4,144,1152]{2,1,0:T(8,128)(2,1)} %broadcast_select_fusion.1), channel_id=1, source_target_pairs={{0,2},{2,0},{4,6},{6,4},{1,3},{3,1},{5,7},{7,5},{8,10},{10,8},{12,... | collective-permute-start | bytes 3981320 | tf_op jit(solution)/shard_map/ppermute | solution.py:134
  311.8 147.9 %collective-permute-start.33 = (bf16[4,144,1152]{2,1,0:T(8,128)(2,1)}, bf16[4,144,1152]{2,1,0:T(8,128)(2,1)}, u32[]{:S(2)}, u32[]{:S(2)}) collective-permute-start(bf16[4,144,1152]{2,1,0:T(8,128)(2,1)} %broadcast_select_fusion.5), channel_id=1, source_target_pairs={{0,2},{2,0},{4,6},{6,4},{1,3},{3,1},{5,7},{7,5},{8,10},{10,8},{12,... | collective-permute-start | bytes 3981320 | tf_op jit(solution)/shard_map/ppermute | solution.py:134
  312.9 59.9 %collective-permute-start.35 = (bf16[4,144,1152]{2,1,0:T(8,128)(2,1)S(1)}, bf16[4,144,1152]{2,1,0:T(8,128)(2,1)S(1)}, u32[]{:S(2)}, u32[]{:S(2)}) collective-permute-start(bf16[4,144,1152]{2,1,0:T(8,128)(2,1)S(1)} %collective-permute-done.34), channel_id=1, source_target_pairs={{0,1},{1,0},{2,3},{3,2},{4,5},{5,4},{6,7},{7,6},{8,9},{9,8},{10,11... | collective-permute-start | bytes 3981320 | tf_op jit(solution)/shard_map/ppermute | solution.py:137
  314.4 86.0 %collective-permute-start.43 = (bf16[4,144,1152]{2,1,0:T(8,128)(2,1)S(1)}, bf16[4,144,1152]{2,1,0:T(8,128)(2,1)S(1)}, u32[]{:S(2)}, u32[]{:S(2)}) collective-permute-start(bf16[4,144,1152]{2,1,0:T(8,128)(2,1)S(1)} %collective-permute-done.42), channel_id=1, source_target_pairs={{0,1},{1,0},{2,3},{3,2},{4,5},{5,4},{6,7},{7,6},{8,9},{9,8},{10,11... | collective-permute-start | bytes 3981320 | tf_op jit(solution)/shard_map/ppermute | solution.py:137
  426.5 76.2 %collective-permute-start.52 = (bf16[4,144,1152]{2,1,0:T(8,128)(2,1)}, bf16[4,144,1152]{2,1,0:T(8,128)(2,1)S(1)}, u32[]{:S(2)}, u32[]{:S(2)}) collective-permute-start(bf16[4,144,1152]{2,1,0:T(8,128)(2,1)} %broadcast_select_fusion), channel_id=1, source_target_pairs={{0,2},{2,0},{4,6},{6,4},{1,3},{3,1},{5,7},{7,5},{8,10},{10,8},{12,... | collective-permute-start | bytes 3981320 | tf_op jit(solution)/shard_map/ppermute | solution.py:134
  435.9 64.2 %collective-permute-start.36 = (bf16[4,144,1152]{2,1,0:T(8,128)(2,1)}, bf16[4,144,1152]{2,1,0:T(8,128)(2,1)}, u32[]{:S(2)}, u32[]{:S(2)}) collective-permute-start(bf16[4,144,1152]{2,1,0:T(8,128)(2,1)} %broadcast_select_fusion.4), channel_id=1, source_target_pairs={{0,2},{2,0},{4,6},{6,4},{1,3},{3,1},{5,7},{7,5},{8,10},{10,8},{12,... | collective-permute-start | bytes 3981320 | tf_op jit(solution)/shard_map/ppermute | solution.py:134
  748.3 164.8 %collective-permute-start.79 = (bf16[256,2304]{1,0:T(8,128)(2,1)}, bf16[256,2304]{1,0:T(8,128)(2,1)}, u32[]{:S(2)}, u32[]{:S(2)}) collective-permute-start(bf16[256,2304]{1,0:T(8,128)(2,1)} %slice.694), channel_id=1, source_target_pairs={{0,2},{2,0},{4,6},{6,4},{1,3},{3,1},{5,7},{7,5},{8,10},{10,8},{12,... | collective-permute-start | bytes 3538952 | tf_op jit(solution)/shard_map/ppermute | solution.py:134
  783.5 77.3 %collective-permute-start.69 = (bf16[256,2304]{1,0:T(8,128)(2,1)}, bf16[256,2304]{1,0:T(8,128)(2,1)}, u32[]{:S(2)}, u32[]{:S(2)}) collective-permute-start(bf16[256,2304]{1,0:T(8,128)(2,1)} %fusion.66), channel_id=1, source_target_pairs={{0,8},{8,16},{16,24},{24,0},{1,9},{9,17},{17,25},{25,1},{2,10},{10... | collective-permute-start | bytes 3538952 | tf_op jit(solution)/shard_map/ppermute | solution.py:128
  839.3 90.9 %collective-permute-start.121 = (bf16[4,2,144,1152]{3,2,1,0:T(8,128)(2,1)}, bf16[4,2,144,1152]{3,2,1,0:T(8,128)(2,1)}, u32[]{:S(2)}, u32[]{:S(2)}) collective-permute-start(bf16[4,2,144,1152]{3,2,1,0:T(8,128)(2,1)} %dynamic-slice_bitcast_fusion), channel_id=1, source_target_pairs={{0,2},{2,0},{4,6},{6,4},{1,3},{3,1},{5,7},{7,5},{8,10},{10,8},{12,... | collective-permute-start | bytes 7962632 | tf_op jit(solution)/shard_map/ppermute | solution.py:134
  934.6 87.7 %collective-permute-start.122 = (bf16[4,2,144,1152]{3,2,1,0:T(8,128)(2,1)}, bf16[4,2,144,1152]{3,2,1,0:T(8,128)(2,1)}, u32[]{:S(2)}, u32[]{:S(2)}) collective-permute-start(bf16[4,2,144,1152]{3,2,1,0:T(8,128)(2,1)} %bitcast_select_fusion.2), channel_id=1, source_target_pairs={{0,1},{1,0},{2,3},{3,2},{4,5},{5,4},{6,7},{7,6},{8,9},{9,8},{10,11... | collective-permute-start | bytes 7962632 | tf_op jit(solution)/shard_map/ppermute | solution.py:137
  935.1 85.4 %collective-permute-start.80 = (bf16[256,2304]{1,0:T(8,128)(2,1)S(1)}, bf16[256,2304]{1,0:T(8,128)(2,1)S(1)}, u32[]{:S(2)}, u32[]{:S(2)}) collective-permute-start(bf16[256,2304]{1,0:T(8,128)(2,1)S(1)} %multiply_convert_fusion.3), channel_id=1, source_target_pairs={{0,1},{1,0},{2,3},{3,2},{4,5},{5,4},{6,7},{7,6},{8,9},{9,8},{10,11... | collective-permute-start | bytes 3538952 | tf_op jit(solution)/shard_map/ppermute | solution.py:137
  939.6 138.0 %collective-permute-start.115 = (bf16[4,2,144,1152]{3,2,1,0:T(8,128)(2,1)}, bf16[4,2,144,1152]{3,2,1,0:T(8,128)(2,1)}, u32[]{:S(2)}, u32[]{:S(2)}) collective-permute-start(bf16[4,2,144,1152]{3,2,1,0:T(8,128)(2,1)} %bitcast_select_fusion.4), channel_id=1, source_target_pairs={{0,1},{1,0},{2,3},{3,2},{4,5},{5,4},{6,7},{7,6},{8,9},{9,8},{10,11... | collective-permute-start | bytes 7962632 | tf_op jit(solution)/shard_map/ppermute | solution.py:137
  941.9 188.9 %collective-permute-start.109 = (bf16[4,2,144,1152]{3,2,1,0:T(8,128)(2,1)}, bf16[4,2,144,1152]{3,2,1,0:T(8,128)(2,1)}, u32[]{:S(2)}, u32[]{:S(2)}) collective-permute-start(bf16[4,2,144,1152]{3,2,1,0:T(8,128)(2,1)} %bitcast_select_fusion.6), channel_id=1, source_target_pairs={{0,1},{1,0},{2,3},{3,2},{4,5},{5,4},{6,7},{7,6},{8,9},{9,8},{10,11... | collective-permute-start | bytes 7962632 | tf_op jit(solution)/shard_map/ppermute | solution.py:137
  1022.3 112.8 %collective-permute-start.81 = (bf16[512,2304]{1,0:T(8,128)(2,1)}, bf16[512,2304]{1,0:T(8,128)(2,1)}, u32[]{:S(2)}, u32[]{:S(2)}) collective-permute-start(bf16[512,2304]{1,0:T(8,128)(2,1)} %pad_maximum_fusion.5), channel_id=1, source_target_pairs={{0,2},{2,0},{4,6},{6,4},{1,3},{3,1},{5,7},{7,5},{8,10},{10,8},{12,... | collective-permute-start | bytes 7077896 | tf_op jit(solution)/shard_map/ppermute | solution.py:134
  1026.1 180.0 %collective-permute-start.123 = (bf16[4,144,1152]{2,1,0:T(8,128)(2,1)}, bf16[4,144,1152]{2,1,0:T(8,128)(2,1)}, u32[]{:S(2)}, u32[]{:S(2)}) collective-permute-start(bf16[4,144,1152]{2,1,0:T(8,128)(2,1)} %fusion.112), channel_id=1, source_target_pairs={{0,4},{2,6},{4,0},{6,2},{1,5},{3,7},{5,1},{7,3},{8,12},{10,14},{12... | collective-permute-start | bytes 3981320 | tf_op jit(solution)/shard_map/ppermute | solution.py:131
  1081.4 127.5 %collective-permute-start.116 = (bf16[4,144,1152]{2,1,0:T(8,128)(2,1)}, bf16[4,144,1152]{2,1,0:T(8,128)(2,1)}, u32[]{:S(2)}, u32[]{:S(2)}) collective-permute-start(bf16[4,144,1152]{2,1,0:T(8,128)(2,1)} %fusion.111), channel_id=1, source_target_pairs={{0,4},{2,6},{4,0},{6,2},{1,5},{3,7},{5,1},{7,3},{8,12},{10,14},{12... | collective-permute-start | bytes 3981320 | tf_op jit(solution)/shard_map/ppermute | solution.py:131
  1134.7 77.0 %collective-permute-start.110 = (bf16[4,144,1152]{2,1,0:T(8,128)(2,1)}, bf16[4,144,1152]{2,1,0:T(8,128)(2,1)}, u32[]{:S(2)}, u32[]{:S(2)}) collective-permute-start(bf16[4,144,1152]{2,1,0:T(8,128)(2,1)} %fusion.110), channel_id=1, source_target_pairs={{0,4},{2,6},{4,0},{6,2},{1,5},{3,7},{5,1},{7,3},{8,12},{10,14},{12... | collective-permute-start | bytes 3981320 | tf_op jit(solution)/shard_map/ppermute | solution.py:131
  1203.4 167.9 %collective-permute-start.106 = (bf16[288,640]{1,0:T(8,128)(2,1)S(1)}, bf16[288,640]{1,0:T(8,128)(2,1)}, u32[]{:S(2)}, u32[]{:S(2)}) collective-permute-start(bf16[288,640]{1,0:T(8,128)(2,1)S(1)} %get-tuple-element.96), channel_id=1, source_target_pairs={{0,4},{2,6},{4,0},{6,2},{1,5},{3,7},{5,1},{7,3},{8,12},{10,14},{12... | collective-permute-start | bytes 1105928 | tf_op jit(solution)/shard_map/ppermute | solution.py:131
  1208.9 81.3 %collective-permute-start.86 = (bf16[512,512]{1,0:T(8,128)(2,1)S(1)}, bf16[512,512]{1,0:T(8,128)(2,1)S(1)}, u32[]{:S(2)}, u32[]{:S(2)}) collective-permute-start(bf16[512,512]{1,0:T(8,128)(2,1)S(1)} %get-tuple-element.68), channel_id=1, source_target_pairs={{0,4},{2,6},{4,0},{6,2},{1,5},{3,7},{5,1},{7,3},{8,12},{10,14},{12... | collective-permute-start | bytes 1572872 | tf_op jit(solution)/shard_map/ppermute | solution.py:131
  1234.1 56.0 %collective-permute-start.126 = (bf16[144,1152]{1,0:T(8,128)(2,1)S(1)}, bf16[144,1152]{1,0:T(8,128)(2,1)S(1)}, u32[]{:S(2)}, u32[]{:S(2)}) collective-permute-start(bf16[144,1152]{1,0:T(8,128)(2,1)S(1)} %get-tuple-element.112), channel_id=1, source_target_pairs={{0,24},{8,0},{16,8},{24,16},{1,25},{9,1},{17,9},{25,17},{2,26},{10... | collective-permute-start | bytes 995336 | tf_op jit(solution)/shard_map/ppermute | solution.py:128
  1304.9 54.7 %collective-permute-start.104 = (bf16[288,640]{1,0:T(8,128)(2,1)}, bf16[288,640]{1,0:T(8,128)(2,1)}, u32[]{:S(2)}, u32[]{:S(2)}) collective-permute-start(bf16[288,640]{1,0:T(8,128)(2,1)} %get-tuple-element.97), channel_id=1, source_target_pairs={{0,4},{2,6},{4,0},{6,2},{1,5},{3,7},{5,1},{7,3},{8,12},{10,14},{12... | collective-permute-start | bytes 1105928 | tf_op jit(solution)/shard_map/ppermute | solution.py:131
  (264 other events, 6155.5 us)

commit v2 on v1

--- a/solution.py
+++ b/solution.py
@@ -43,6 +43,10 @@
         [front_half * cosine - back_half * sine_wave, back_half * cosine + front_half * sine_wave],
         axis=-1,
     )
+
+
+def tie(first, *others):
+    return lax.optimization_barrier((first,) + others)[0]
 
 
 def matmul(left, right):
@@ -139,36 +143,69 @@
     def by_core(own, other):
         return (jnp.where(core == 0, own, other), jnp.where(core == 0, other, own))
 
-    def gather_grid(own):
+    def place(held, piece, *index):
+        piece = piece.reshape((1,) * len(index) + piece.shape)
+        return lax.dynamic_update_slice(held, piece, index + (0,) * (held.ndim - len(index)))
+
+    def gather_grid(own, waits=()):
         held = jnp.zeros((z_size, y_size) + own.shape, own.dtype)
-        tail = (0,) * own.ndim
-        chunk = own
+        chunk, arrivals, extra = own, [], list(waits)
         for step in range(z_size):
             if step:
-                chunk = z_shift(chunk, 1)
+                chunk = tie(ahead, turn)
+            ahead = z_shift(chunk, 1) if step < z_size - 1 else None
+            if ahead is not None:
+                arrivals.append(ahead)
+            elif step:
+                arrivals[-1] = chunk
             turn = chunk
             for hop in range(y_size):
                 if hop:
                     turn = y_next(turn)
-                held = lax.dynamic_update_slice(
-                    held,
-                    turn[None, None],
-                    ((z - step) % z_size, (y - hop) % y_size) + tail,
-                )
-        return held
-
-    def scatter_grid(take):
-        sums = {}
-        for step in list(range(1, z_size)) + [0]:
-            to_z = (z - step) % z_size
-            total = take(to_z, (y - 1) % y_size)
+                held = place(held, turn, (z - step) % z_size, (y - hop) % y_size)
+        return held, arrivals, None
+
+    def row_of(values, at):
+        return lax.dynamic_slice_in_dim(values, at, 1, 0)[0]
+
+    def scatter_y(values):
+        def column(at):
+            return lax.dynamic_slice_in_dim(values, at, 1, 1)[:, 0].astype(f32)
+
+        total = column((y - 1) % y_size)
+        for hop in range(2, y_size + 1):
+            total = y_next(total.astype(bf16)).astype(f32) + column((y - hop) % y_size)
+        return total
+
+    def scatter_z(values):
+        low = values.astype(bf16)
+        terms = [row_of(values, z)]
+        for step in range(1, z_size):
+            terms.append(z_shift(row_of(low, (z + step) % z_size), step))
+        return terms
+
+    def add_up(terms):
+        total = terms[0].astype(f32)
+        for term in terms[1:]:
+            total = total + term.astype(f32)
+        return total
+
+    def scatter_grid(take, groups, waits=()):
+        steps, sent = list(range(1, z_size)) + [0], {}
+        for size in groups:
+            now, steps = steps[:size], steps[size:]
+
+            def terms(y_at):
+                return jnp.stack([take((z + step) % z_size, y_at) for step in now], axis=0)
+
+            total = terms((y - 1) % y_size)
             for hop in range(2, y_size + 1):
-                total = y_next(total.astype(bf16)).astype(f32) + take(to_z, (y - hop) % y_size)
-            sums[step] = total
-        total = sums[1]
-        for step in list(range(2, z_size)) + [0]:
-            total = z_shift(total.astype(bf16), 1).astype(f32) + sums[step]
-        return total
+                total = y_next(total.astype(bf16)).astype(f32) + terms((y - hop) % y_size)
+            if waits:
+                total, waits = tie(total, waits[0]), waits[1:]
+            for i, step in enumerate(now):
+                sent[step] = z_shift(total[i].astype(bf16), step) if step else total[i]
+        return [sent[step] for step in range(z_size)], total
 
     def taker(values):
         tail = (0,) * (values.ndim - 2)
@@ -192,9 +229,22 @@
 
     gain_one = attn_norm.astype(f32)[:, None]
     gain_three = mlp_norm.astype(f32)[:, None]
+    pairs = (2,) * (z_size // 2)
+    same_core = [[y_at * 2 * 2 + which * 2 + t_at for y_at in range(y_size) for t_at in range(2)] for which in range(2)]
+
+    def over_z(values):
+        return lax.all_to_all(values, "fsdp", 0, 0, tiled=True)
+
+    def z_blocks(local):
+        return jnp.stack([local[:, i * block : (i + 1) * block] for i in range(z_size)], axis=0)
+
     scaled_q = (w_query.astype(f32) * gain_one).astype(bf16)
     scaled_k = (w_key.astype(f32) * gain_one).astype(bf16)
     scaled_v = (w_value.astype(f32) * gain_one).astype(bf16)
+
+    gains = jnp.concatenate(
+        [attn_post[:, None], mlp_post[:, None], jnp.zeros((part, 126), bf16)], axis=1
+    )
 
     def head_cols(which):
         return jnp.concatenate(
@@ -202,18 +252,42 @@
                 lax.dynamic_slice_in_dim(scaled_q, which * q_cols, q_cols, 1),
                 lax.dynamic_slice_in_dim(scaled_k, which * kv_cols, kv_cols, 1),
                 lax.dynamic_slice_in_dim(scaled_v, which * kv_cols, kv_cols, 1),
+                lax.dynamic_slice_in_dim(w_out.T, which * q_cols, q_cols, 1),
+                gains,
             ],
             axis=1,
         )
 
     mine, other = by_core(head_cols(core), core_swap(head_cols(1 - core)))
-    attn_w = gather_grid(jnp.stack([mine, other], axis=0)).reshape(width, a_cols)
-
-    post_low = jnp.zeros((1, 8, 256), bf16)
-    post_low = post_low.at[0, 0, :part].set(attn_post).at[0, 1, :part].set(mlp_post)
-    post_all = lax.all_gather(post_low, ("fsdp", "ctx"), axis=0, tiled=True)
-    post_attn = post_all[:, 0, :part].reshape(1, width).astype(f32)
-    post_mlp = post_all[:, 1, :part].reshape(1, width).astype(f32)
+    attn_own = jnp.stack([mine, other], axis=0)
+    gate_low = z_blocks((w_gate.astype(f32) * gain_three).astype(bf16))
+    up_low = z_blocks((w_up.astype(f32) * gain_three).astype(bf16))
+    down_low = z_blocks(w_down.T)
+    attn_grid, attn_z, _ = gather_grid(attn_own)
+    gate_held = over_z(tie(gate_low, attn_z[-1]))
+    attn_grid = attn_grid.reshape(width, a_cols + q_cols + 128)
+    attn_w = attn_grid[:, :a_cols]
+    out_w = attn_grid[:, a_cols : a_cols + q_cols]
+    prompt_x, cont_x = tie((prompt_x, cont_x), attn_own)
+
+    def spread(held):
+        return lax.all_gather(
+            held, ("ctx", "tp"), axis=0, tiled=False, axis_index_groups=same_core
+        ).reshape((y_size, 2) + held.shape)
+
+    def spread_end(every):
+        mine = lax.dynamic_slice_in_dim(every, core, 1, 1)[:, 0]
+        got = core_swap(lax.dynamic_slice_in_dim(every, 1 - core, 1, 1)[:, 0])
+        full = jnp.zeros((z_size, y_size, 2, part, block), bf16)
+        for which, rows_at in ((core, mine), (1 - core, got)):
+            full = lax.dynamic_update_slice(
+                full, rows_at.transpose(1, 0, 2, 3)[:, :, None], (0, 0, which, 0, 0)
+            )
+        return full.reshape(width, block)
+
+    gate_every = spread(gate_held)
+    up_held = over_z(tie(up_low, gate_held))
+    up_every = spread(up_held)
 
     residual = jnp.concatenate(
         [prompt_x.reshape(prompt_local, width), cont_x.reshape(cont_rows, width)], axis=0
@@ -221,40 +295,6 @@
     normal_one, inverse_one = norm_parts(residual)
     normal_low = normal_one.astype(bf16)
     chip_rows = jnp.concatenate([normal_low, core_swap(normal_low)], axis=0)
-
-    out_t = w_out.T
-    mine, other = by_core(
-        lax.dynamic_slice_in_dim(out_t, core * q_cols, q_cols, 1),
-        core_swap(lax.dynamic_slice_in_dim(out_t, (1 - core) * q_cols, q_cols, 1)),
-    )
-    out_w = gather_grid(jnp.stack([mine, other], axis=0)).reshape(width, q_cols)
-
-    def mlp_weight(local):
-        blocks = local.reshape(part, z_size, block)
-        held = jnp.zeros((z_size, part, block), bf16)
-        for step in range(z_size):
-            piece = lax.dynamic_slice_in_dim(local, ((z + step) % z_size) * block, block, 1)
-            if step:
-                piece = z_shift(piece, step)
-            held = lax.dynamic_update_slice(held, piece[None], ((z - step) % z_size, 0, 0))
-        del blocks
-        full = jnp.zeros((z_size, y_size, 2, part, block), bf16)
-        turn = held
-        for hop in range(y_size):
-            if hop:
-                turn = y_next(turn)
-            cross = tp_swap(turn)
-            keep = jnp.where(t == core, turn, cross)
-            give = jnp.where(t == core, cross, turn)
-            got = core_swap(give)
-            y_at = (y - hop) % y_size
-            full = lax.dynamic_update_slice(full, keep[:, None, None], (0, y_at, core, 0, 0))
-            full = lax.dynamic_update_slice(full, got[:, None, None], (0, y_at, 1 - core, 0, 0))
-        return full.reshape(width, block)
-
-    gate_w = mlp_weight((w_gate.astype(f32) * gain_three).astype(bf16))
-    up_w = mlp_weight((w_up.astype(f32) * gain_three).astype(bf16))
-    down_w = mlp_weight(w_down.T)
 
     core_of = (core, 1 - core)
     cont_places = PROMPT + jnp.tile(jnp.arange(cont_size, dtype=jnp.int32), cont_count)
@@ -278,8 +318,12 @@
     value_rows = projected[:, q_cols + HD :].astype(bf16)
     kv_rows = jnp.concatenate([key_rows, value_rows], axis=1).reshape(2, rows, 2 * HD)
     prompt_kv = kv_rows[:, :prompt_local].reshape(2 * prompt_local, 2 * HD)
-    every_kv = gather_grid(prompt_kv).reshape(z_size, y_size * 2 * prompt_local, 2 * HD)
+    every_kv, kv_z, kv_y = gather_grid(tie(prompt_kv, up_held))
+    every_kv = every_kv.reshape(z_size, y_size * 2 * prompt_local, 2 * HD)
     span = every_kv.shape[1]
+    down_held = over_z(tie(down_low, kv_z[-1]))
+    down_every = spread(down_held)
+    every_kv = tie(every_kv, down_held)
     own_kv = lax.dynamic_slice(every_kv, (z, 0, 0), (1, span, 2 * HD))[0]
     key_places = (
         (jnp.arange(y_size, dtype=jnp.int32)[:, None, None] * 2
@@ -332,27 +376,46 @@
         summed = partial[:rows] + core_swap(low[rows:]).astype(f32)
         return take_share(summed) + tp_swap(give_share(summed).astype(bf16)).astype(f32)
 
-    branch = to_shares(matmul_rt(attn_out, out_w))
+    pick = (
+        jnp.arange(8, dtype=jnp.int32)[:, None] == jnp.arange(128, dtype=jnp.int32)[None, :]
+    ).astype(bf16)
+    post_rows = matmul_rt(pick, attn_grid[:, a_cols + q_cols :])
+    post_attn, post_mlp = post_rows[0:1], post_rows[1:2]
+    branch_partial = matmul_rt(attn_out, out_w)
+    branch_core = branch_partial[:rows] + core_swap(branch_partial[rows:].astype(bf16)).astype(f32)
+    branch_give = give_share(branch_core).astype(bf16)
+    branch_got = tp_swap(branch_give)
+    gate_w = spread_end(tie(gate_every, branch_give))
+    branch = take_share(branch_core) + tie(branch_got, gate_w).astype(f32)
+    up_w = spread_end(up_every)
 
     normal_two, inverse_two = norm_parts(branch)
     middle = take_share(residual) + normal_two * post_attn
     normal_three, inverse_three = norm_parts(middle)
 
-    def ring_rows(own, step_fn):
+    three_low = normal_three.astype(bf16)
+    down_w = spread_end(tie(down_every, three_low))
+
+    def ring_rows(own, step_fn, before_last=None, own_first=False):
         sums = []
         chunk = own
         for step in range(z_size):
             if step:
                 chunk = z_shift(chunk, 1)
+            if step == 1 and own_first:
+                chunk = tie(chunk, partial)
             both = jnp.concatenate([chunk, core_swap(chunk)], axis=0)
             partial = step_fn(step, both)
             sums.append(
                 partial[:share] + core_swap(partial[share:].astype(bf16)).astype(f32)
             )
-        total = sums[1]
+        total, lows = sums[1], []
         for step in list(range(2, z_size)) + [0]:
-            total = z_shift(total.astype(bf16), 1).astype(f32) + sums[step]
-        return total
+            lows.append(total.astype(bf16))
+            if step == 0 and before_last is not None:
+                lows[-1] = tie(lows[-1], before_last())
+            total = z_shift(lows[-1], 1).astype(f32) + sums[step]
+        return total, lows
 
     mlp_in, gates, ups, inners = {}, {}, {}, {}
 
@@ -363,7 +426,7 @@
         inners[step] = (jax.nn.gelu(gates[step], approximate=True) * ups[step]).astype(bf16)
         return matmul_rt(inners[step], down_w)
 
-    mlp_share = ring_rows(normal_three.astype(bf16), mlp_forward)
+    mlp_share, _ = ring_rows(three_low, mlp_forward)
 
     normal_four, inverse_four = norm_parts(mlp_share)
     cont_live = (
@@ -397,60 +460,53 @@
         grad_ups[step] = grad_up.astype(bf16)
         return matmul_rt(grad_gates[step], gate_w) + matmul_rt(grad_ups[step], up_w)
 
-    grad_three = ring_rows(grad_mlp.astype(bf16), mlp_backward)
+    def blocks_back(got):
+        return jnp.concatenate([got[i] for i in range(z_size)], axis=1).astype(f32)
+
+    def reduce_terms(full):
+        full = full.reshape(z_size, y_size, 2, part, block)
+
+        def of_core(which):
+            return lax.dynamic_slice_in_dim(full, which, 1, 2)[:, :, 0].transpose(1, 0, 2, 3)
+
+        halves = by_core(of_core(core), core_swap(of_core(1 - core)))
+        return jnp.stack(halves, axis=1).reshape((y_size * 2 * z_size,) + full.shape[3:])
+
+    def reduce(every):
+        return lax.psum_scatter(
+            every, ("ctx", "tp"), scatter_dimension=0, tiled=True, axis_index_groups=same_core
+        )
 
     def joined(pieces):
         return jnp.concatenate([pieces[step] for step in range(z_size)], axis=0)
 
-    all_in, all_grad = joined(mlp_in), joined(grad_outs)
-    grad_down_w = matmul_lt(all_grad, joined(inners)).astype(bf16)
-    grad_gate_w = matmul_lt(all_in, joined(grad_gates)).astype(bf16)
-    grad_up_w = matmul_lt(all_in, joined(grad_ups)).astype(bf16)
-
-    def mlp_grad(full):
-        full = full.reshape(z_size, y_size, 2, part, block)
-
-        def of_core(which):
-            return lax.dynamic_slice(
-                full, (0, 0, which, 0, 0), (z_size, y_size, 1, part, block)
-            )[:, :, 0]
-
-        mine, got = of_core(core), core_swap(of_core(1 - core))
-        keep = jnp.where(t == core, mine, got).astype(f32)
-        summed = keep + tp_swap(jnp.where(t == core, got, mine)).astype(f32)
-
-        def y_term(at):
-            return lax.dynamic_slice(summed, (0, at, 0, 0), (z_size, 1, part, block))[:, 0]
-
-        total = y_term((y - 1) % y_size)
-        for hop in range(2, y_size + 1):
-            total = y_next(total.astype(bf16)).astype(f32) + y_term((y - hop) % y_size)
-        low = total.astype(bf16)
-        held = jnp.zeros((part, z_size * block), bf16)
-        for step in range(z_size):
-            piece = lax.dynamic_slice_in_dim(low, (z + step) % z_size, 1, 0)[0]
-            if step:
-                piece = z_shift(piece, step)
-            held = lax.dynamic_update_slice(held, piece, (0, ((z - step) % z_size) * block))
-        return held.astype(f32)
-
-    raw_down = mlp_grad(grad_down_w)
-    raw_gate = mlp_grad(grad_gate_w)
-    raw_up = mlp_grad(grad_up_w)
+    down_terms = []
+
+    def before_last():
+        grad_down_w = matmul_lt(joined(grad_outs), joined(inners)).astype(bf16)
+        down_terms.append(reduce_terms(grad_down_w))
+        return down_terms[0]
+
+    grad_three, lows = ring_rows(grad_mlp.astype(bf16), mlp_backward, before_last, True)
+    down_sum = reduce(down_terms[0])
+    all_in = joined(mlp_in)
+    grad_gate_w = matmul_lt(tie(all_in, lows[2]), joined(grad_gates)).astype(bf16)
+    gate_terms = reduce_terms(grad_gate_w)
+    gate_sum = reduce(gate_terms)
+    grad_three = tie(grad_three, gate_terms)
 
     grad_middle = grad_result + norm_back(grad_three, normal_three, inverse_three)
     grad_post_attn = jnp.sum(grad_middle * normal_two, axis=0)
     grad_branch = norm_back(grad_middle * post_attn, normal_two, inverse_two).astype(bf16)
-    branch_rows = rows_of(grad_branch, tp_swap(grad_branch))
+    grad_up_w = matmul_lt(tie(all_in, grad_branch), joined(grad_ups)).astype(bf16)
+    up_terms = reduce_terms(grad_up_w)
+    up_sum = reduce(up_terms)
+    down_got = over_z(tie(down_sum, grad_branch))
+    branch_rows = rows_of(grad_branch, tie(tp_swap(grad_branch), up_terms, down_got))
     branch_chip = jnp.concatenate([branch_rows, core_swap(branch_rows)], axis=0)
     grad_attn = matmul(branch_chip, out_w).astype(bf16)
-    grad_out_w = matmul_lt(branch_chip, attn_out).astype(bf16)
-    post_terms = jnp.stack([grad_post_attn, grad_post_mlp], axis=1).astype(bf16)
-    grad_out_w = jnp.concatenate(
-        [grad_out_w, post_terms, jnp.zeros((width, 126), bf16)], axis=1
-    ).reshape(z_size, y_size, 2 * part, q_cols + 128)
-    out_sum = scatter_grid(taker(grad_out_w))
-
+    grad_out_w = matmul_lt(tie(branch_chip, grad_attn), attn_out).astype(bf16)
+    out_y = scatter_y(grad_out_w.reshape(z_size, y_size, 2 * part, q_cols)).astype(bf16)
     grad_heads = jnp.stack(
         [grad_attn[:, i * HD : (i + 1) * HD] for i in range(shared_by)], axis=0
     ).reshape(shared_by, 2, rows, HD)
@@ -463,6 +519,8 @@
         grad_heads[:, :, :prompt_local].reshape(-1, HD),
     )
     prompt_gkv = jnp.concatenate([prompt_gk, prompt_gv], axis=1)
+    gate_got = over_z(tie(gate_sum, grad_attn))
+    grad_heads = tie(grad_heads, gate_got)
     cont_gq, cont_gkv, own_gkv = [], [], []
     for i in range(2 * cont_count):
         at = prompt_local + (i % cont_count) * cont_size
@@ -483,6 +541,7 @@
 
     def kv_take(z_at, y_at):
         length = 2 * prompt_local
+
         def piece(values):
             return lax.dynamic_slice_in_dim(values, y_at * length, length, 0)
 
@@ -491,26 +550,53 @@
             total = total + jnp.where(z_at == which, piece(term), 0.0)
         return total
 
-    kv_sum = scatter_grid(kv_take).reshape(2, prompt_local, 2 * HD)
+    out_got = over_z(out_y)
+    kv_terms, kv_total = scatter_grid(kv_take, pairs, (out_y, out_got))
+    grad_q = rows_order(prompt_gq.reshape(shared_by, 2, prompt_local, HD), cont_gq)
+    grad_q_proj = jnp.concatenate(
+        [
+            rotary(grad_q[:, i * HD : (i + 1) * HD] * query_scale, cosine, -sine_wave)
+            for i in range(shared_by)
+        ],
+        axis=1,
+    ).astype(bf16)
+    grad_q_w = matmul_lt(chip_rows, grad_q_proj).astype(bf16)
+    post_terms = jnp.stack([grad_post_attn, grad_post_mlp], axis=0)
+    post_terms = post_terms.reshape(2, z_size, y_size, 2, part).transpose(1, 2, 3, 0, 4)
+    q_y = scatter_y(tie(grad_q_w, kv_total).reshape(z_size, y_size, 2 * part, q_cols))
+    kv_low = add_up(tie(kv_terms, q_y))
+    up_got = over_z(tie(up_sum, q_y))
+    kv_sum = kv_low.reshape(2, prompt_local, 2 * HD)
     halves = []
     for half in range(2):
         halves.append(kv_sum[half])
         halves.extend(own_gkv[half * cont_count : (half + 1) * cont_count])
     grad_kv = jnp.concatenate(halves, axis=0)
-    grad_q = rows_order(prompt_gq.reshape(shared_by, 2, prompt_local, HD), cont_gq)
-    grad_proj = jnp.concatenate(
-        [
-            rotary(grad_q[:, i * HD : (i + 1) * HD] * query_scale, cosine, -sine_wave)
-            for i in range(shared_by)
-        ]
-        + [rotary(grad_kv[:, :HD], cosine, -sine_wave), grad_kv[:, HD:]],
-        axis=1,
+    grad_kv_proj = jnp.concatenate(
+        [rotary(grad_kv[:, :HD], cosine, -sine_wave), grad_kv[:, HD:]], axis=1
     ).astype(bf16)
-    grad_attn_w = matmul_lt(chip_rows, grad_proj).astype(bf16)
-    attn_sum = scatter_grid(taker(grad_attn_w.reshape(z_size, y_size, 2 * part, a_cols)))
-    grad_one = to_shares(matmul_rt(grad_proj, attn_w))
+    one_partial = matmul_rt(grad_q_proj, attn_w[:, :q_cols]) + matmul_rt(
+        grad_kv_proj, attn_w[:, q_cols:]
+    )
+    one_core = one_partial[:rows] + core_swap(one_partial[rows:].astype(bf16)).astype(f32)
+    one_give = give_share(one_core).astype(bf16)
+    one_got = tp_swap(one_give)
+    grad_kv_w = matmul_lt(tie(chip_rows, one_give), grad_kv_proj).astype(bf16)
+    kvw_y = scatter_y(grad_kv_w.reshape(z_size, y_size, 2 * part, 2 * kv_cols))
+    q_got = over_z(tie(q_y, up_got).astype(bf16))
+    one_got = tie(one_got, up_got, q_got, kvw_y)
+    grad_one = take_share(one_core) + one_got.astype(f32)
+    post_z = scatter_z(scatter_y(tie(post_terms, one_give)))
     grad_input = grad_middle + norm_back(grad_one, take_share(normal_one), take_share(inverse_one))
     input_low = grad_input.astype(bf16)
+    kvw_got = over_z(kvw_y.astype(bf16))
+    raw_down = blocks_back(tie(down_got, input_low))
+    raw_gate = blocks_back(tie(gate_got, input_low))
+    raw_up = blocks_back(tie(up_got, input_low))
+    out_sum = jnp.sum(tie(out_got, input_low).astype(f32), axis=0)
+    q_sum = jnp.sum(tie(q_got, input_low).astype(f32), axis=0)
+    kvw_sum = jnp.sum(tie(kvw_got, input_low).astype(f32), axis=0)
+    post_sum = add_up(tie(post_z, input_low))
     input_rows = rows_of(input_low, tp_swap(input_low)).astype(f32)
 
     def split_core(summed):
@@ -518,19 +604,12 @@
         give = lax.dynamic_slice_in_dim(summed, (1 - core) * part, part, 0).astype(bf16)
         return mine, core_swap(give).astype(f32)
 
-    out_mine, out_got = split_core(out_sum)
-    first, second = by_core(out_mine[:, :q_cols], out_got[:, :q_cols])
-    grad_out = jnp.concatenate([first, second], axis=1).T
-    post_sum = out_mine[:, q_cols : q_cols + 2] + out_got[:, q_cols : q_cols + 2]
-    attn_mine, attn_got = split_core(attn_sum)
-    first, second = by_core(attn_mine, attn_got)
-
-    def both_cores(start, size):
-        return jnp.concatenate([first[:, start : start + size], second[:, start : start + size]], axis=1)
-
-    raw_q = both_cores(0, q_cols)
-    raw_k = both_cores(q_cols, kv_cols)
-    raw_v = both_cores(q_cols + kv_cols, kv_cols)
+    grad_out = jnp.concatenate(by_core(*split_core(out_sum)), axis=1).T
+    post_sum = row_of(post_sum, core) + core_swap(row_of(post_sum, 1 - core))
+    raw_q = jnp.concatenate(by_core(*split_core(q_sum)), axis=1)
+    first, second = by_core(*split_core(kvw_sum))
+    raw_k = jnp.concatenate([first[:, :kv_cols], second[:, :kv_cols]], axis=1)
+    raw_v = jnp.concatenate([first[:, kv_cols:], second[:, kv_cols:]], axis=1)
 
     def gain_sum(raw, weight):
         return jnp.sum(raw * weight.astype(f32), axis=1)
@@ -538,9 +617,9 @@
     gain_terms = jnp.stack(
         [
             gain_sum(raw_q, w_query) + gain_sum(raw_k, w_key) + gain_sum(raw_v, w_value),
-            post_sum[:, 0],
+            post_sum[0],
             gain_sum(raw_gate, w_gate) + gain_sum(raw_up, w_up),
-            post_sum[:, 1],
+            post_sum[1],
         ],
         axis=0,
     )

time: 1480 us -> 1230 us (0.83)
  waiting for transfers between devices: 856 us -> 599 us
  local copies, waits for them, and re-layouts: 100 us -> 145 us
  blocking collectives: 26.3 us -> 0 us
    ppermute x15 -> x6, waiting for transfers between devices: 360 us -> 82.5 us  [tp_swap(): return lax.ppermute(values, 'tp', [(0, 1), (1, 0)])]
    ppermute x48 -> x24, waiting for transfers between devices: 381 us -> 228 us  [z_shift(): lax.ppermute(values, 'fsdp', [(i, (i + step) % z_size) for i in range(z_s...]
    ppermute x30 -> x14, waiting for transfers between devices: 112 us -> 217 us  [y_next(): lax.ppermute(values, 'ctx', [(i, (i + 2) % c_size) for i in range(c_size)])]
    all_to_all x0 -> x9, waiting for transfers between devices: none -> 51.3 us  [over_z(): return lax.all_to_all(values, 'fsdp', 0, 0, tiled=True)]
    all_to_all x0 -> x9, starting transfers between devices: none -> 47.9 us  [over_z(): return lax.all_to_all(values, 'fsdp', 0, 0, tiled=True)]
    ppermute x48 -> x24, starting transfers between devices: 54.1 us -> 17.9 us  [z_shift(): lax.ppermute(values, 'fsdp', [(i, (i + step) % z_size) for i in range(z_s...]
    all_gather x1 -> x0, blocking collectives: 26.3 us -> none  [shards(): post_all = lax.all_gather(post_low, ('fsdp', 'ctx'), axis=0, tiled=True)]
    another operation x5 -> x18, other arithmetic: 6.55 us -> 28 us
  transfers between devices with their start and end apart: 127 -> 91, of which waited for: 49 -> 44; matrix products, arithmetic and copies ran while one was open for 30% -> 36% of each run, Pallas kernels for 0% -> 0%
where the time goes in v2:
time: 1230 us; the launch traced here: 1220 us
  waiting for transfers between devices  599 us (49%)
  matrix products  222 us (18%)
  local copies, waits for them, and re-layouts  145 us (12%)
  other arithmetic  131 us (11%)
  starting transfers between devices  95.6 us (8%)
  between operations  23.8 us (2%)
    ppermute x24, waiting for transfers between devices, z_shift(): lax.ppermute(values, 'fsdp', [(i, (i + step) % z_size) for i in range(z_s...  228 us
    ppermute x14, waiting for transfers between devices, y_next(): lax.ppermute(values, 'ctx', [(i, (i + 2) % c_size) for i in range(c_size)])  217 us
    ppermute x6, waiting for transfers between devices, tp_swap(): return lax.ppermute(values, 'tp', [(0, 1), (1, 0)])  82.5 us
    dot_general x20, matrix products, matmul(): return jnp.dot(left, right, preferred_element_type=f32)  81.6 us
    dot_general x22, matrix products, matmul_rt(): lax.dot_general(left, right, (((1,), (1,)), ((), ())), preferred_element_...  76.5 us
    dot_general x12, matrix products, matmul_lt(): lax.dot_general(left, right, (((0,), (0,)), ((), ())), preferred_element_...  63.8 us
    unnamed x379, local copies, waits for them, and re-layouts  59.1 us
    all_to_all x9, waiting for transfers between devices, over_z(): return lax.all_to_all(values, 'fsdp', 0, 0, tiled=True)  51.3 us
  transfers between devices with their start and end apart: 91, of which 44 were waited for; matrix products, arithmetic and copies ran while one was open for 36% of the time, Pallas kernels for 0%

profile of v2, /device:TPU:0, one launch (start us, length us, event | category | flops | bytes accessed | tf_op | source)
XLA Modules:
  0.0 1215.8 jit_solution(12827358648044812539)
XLA Ops:
  23.2 20.6 %collective-permute-done.2 = bf16[2,144,1664]{2,1,0:T(8,128)(2,1)} collective-permute-done((bf16[2,144,1664]{2,1,0:T(8,128)(2,1)}, bf16[2,144,1664]{2,1,0:T(8,128)(2,1)}, u32[]{:S(2)}, u32[]{:S(2)}) %collective-permute-start.2) | collective-permute-done | bytes 958496 | tf_op jit(solution)/shard_map/ppermute | solution.py:135
  48.2 21.7 %collective-permute-done.4 = bf16[2,144,1664]{2,1,0:T(8,128)(2,1)S(1)} collective-permute-done((bf16[2,144,1664]{2,1,0:T(8,128)(2,1)}, bf16[2,144,1664]{2,1,0:T(8,128)(2,1)S(1)}, u32[]{:S(2)}, u32[]{:S(2)}) %collective-permute-start.4) | collective-permute-done | bytes 958496 | tf_op jit(solution)/shard_map/ppermute | solution.py:135
  75.7 18.0 %collective-permute-done.6 = bf16[2,144,1664]{2,1,0:T(8,128)(2,1)S(1)} collective-permute-done((bf16[2,144,1664]{2,1,0:T(8,128)(2,1)S(1)}, bf16[2,144,1664]{2,1,0:T(8,128)(2,1)S(1)}, u32[]{:S(2)}, u32[]{:S(2)}) %collective-permute-start.6) | collective-permute-done | bytes 958496 | tf_op jit(solution)/shard_map/ppermute | solution.py:135
  106.6 23.4 %all-to-all-done = bf16[4,144,1152]{2,1,0:T(8,128)(2,1)} async-done(((bf16[4,144,1152]{2,1,0:T(8,128)(2,1)}), bf16[4,144,1152]{2,1,0:T(8,128)(2,1)}, u32[]{:S(2)}, u32[]{:S(2)}) %all-to-all-start) | async-done | bytes 1327136 | tf_op jit(solution)/shard_map/all_to_all | solution.py:236
  154.1 25.7 %collective-permute-done.8 = bf16[2,144,1664]{2,1,0:T(8,128)(2,1)} collective-permute-done((bf16[2,144,1664]{2,1,0:T(8,128)(2,1)}, bf16[2,144,1664]{2,1,0:T(8,128)(2,1)}, u32[]{:S(2)}, u32[]{:S(2)}) %collective-permute-start.8) | collective-permute-done | bytes 958496 | tf_op jit(solution)/shard_map/ppermute | solution.py:135
  182.1 8.3 fusion
  200.3 10.2 collective-permute-done.10
  264.8 11.3 collective-permute-done.15
  327.9 37.2 %collective-permute-done.18 = bf16[256,2304]{1,0:T(8,128)(2,1)S(1)} collective-permute-done((bf16[256,2304]{1,0:T(8,128)(2,1)}, bf16[256,2304]{1,0:T(8,128)(2,1)S(1)}, u32[]{:S(2)}, u32[]{:S(2)}) %collective-permute-start.18) | collective-permute-done | bytes 1179680 | tf_op jit(solution)/shard_map/ppermute | solution.py:141
  372.9 25.7 %collective-permute-done.20 = bf16[256,2304]{1,0:T(8,128)(2,1)} collective-permute-done((bf16[256,2304]{1,0:T(8,128)(2,1)S(1)}, bf16[256,2304]{1,0:T(8,128)(2,1)}, u32[]{:S(2)}, u32[]{:S(2)}) %collective-permute-start.20) | collective-permute-done | bytes 1179680 | tf_op jit(solution)/shard_map/ppermute | solution.py:132
  409.9 19.3 %collective-permute-done.26 = bf16[256,2304]{1,0:T(8,128)(2,1)} collective-permute-done((bf16[256,2304]{1,0:T(8,128)(2,1)}, bf16[256,2304]{1,0:T(8,128)(2,1)}, u32[]{:S(2)}, u32[]{:S(2)}) %collective-permute-start.26) | collective-permute-done | bytes 1179680 | tf_op jit(solution)/shard_map/ppermute | solution.py:132
  448.1 11.7 collective-permute-done.30
  502.7 20.0 %collective-permute-done.25 = bf16[256,2304]{1,0:T(8,128)(2,1)} collective-permute-done((bf16[256,2304]{1,0:T(8,128)(2,1)S(1)}, bf16[256,2304]{1,0:T(8,128)(2,1)}, u32[]{:S(2)}, u32[]{:S(2)}) %collective-permute-start.25) | collective-permute-done | bytes 1179680 | tf_op jit(solution)/shard_map/ppermute | solution.py:132
  534.1 19.8 %collective-permute-done.29 = bf16[256,2304]{1,0:T(8,128)(2,1)S(1)} collective-permute-done((bf16[256,2304]{1,0:T(8,128)(2,1)S(1)}, bf16[256,2304]{1,0:T(8,128)(2,1)S(1)}, u32[]{:S(2)}, u32[]{:S(2)}) %collective-permute-start.29) | collective-permute-done | bytes 1179680 | tf_op jit(solution)/shard_map/ppermute | solution.py:132
  555.2 27.7 %collective-permute-done.33 = bf16[256,2304]{1,0:T(8,128)(2,1)S(1)} collective-permute-done((bf16[256,2304]{1,0:T(8,128)(2,1)S(1)}, bf16[256,2304]{1,0:T(8,128)(2,1)S(1)}, u32[]{:S(2)}, u32[]{:S(2)}) %collective-permute-start.33) | collective-permute-done | bytes 1179680 | tf_op jit(solution)/shard_map/ppermute | solution.py:132
  604.3 14.5 %collective-permute-done.37 = bf16[256,2304]{1,0:T(8,128)(2,1)S(1)} collective-permute-done((bf16[256,2304]{1,0:T(8,128)(2,1)S(1)}, bf16[256,2304]{1,0:T(8,128)(2,1)S(1)}, u32[]{:S(2)}, u32[]{:S(2)}) %collective-permute-start.37) | collective-permute-done | bytes 1179680 | tf_op jit(solution)/shard_map/ppermute | solution.py:132
  640.7 8.3 collective-permute-done.42
  663.8 15.7 %collective-permute-done.46 = bf16[256,2304]{1,0:T(8,128)(2,1)S(1)} collective-permute-done((bf16[256,2304]{1,0:T(8,128)(2,1)S(1)}, bf16[256,2304]{1,0:T(8,128)(2,1)S(1)}, u32[]{:S(2)}, u32[]{:S(2)}) %collective-permute-start.46) | collective-permute-done | bytes 1179680 | tf_op jit(solution)/shard_map/ppermute | solution.py:132
  690.2 15.2 %convolution_convert_fusion.2 = bf16[2304,1152]{1,0:T(8,128)(2,1)S(1)} fusion(bf16[2048,2304]{1,0:T(8,128)(2,1)} %constant_dynamic-update-slice_fusion.6, bf16[512,1152]{1,0:T(8,128)(2,1)S(1)} %copy-done.156, bf16[512,1152]{1,0:T(8,128)(2,1)S(1)} %copy-done.154, bf16[512,1152]{1,0:T(8,128)(2,1)S(1)} %copy-done.152, bf16[512,1152]{1,0:T(8,128)(2,1)} %copy-done.163), kind=kOutput, calls=%fused_computation.2 | convolution fusion | flops 10893164544 | bytes 19464192 | tf_op jit(solution)/shard_map/dot_general | solution.py:61
  743.7 15.1 %convolution_convert_fusion.1 = bf16[2304,1152]{1,0:T(8,128)(2,1)S(1)} fusion(bf16[2048,2304]{1,0:T(8,128)(2,1)} %get-tuple-element.83, bf16[512,1152]{1,0:T(8,128)(2,1)S(1)} %copy-done.144, bf16[512,1152]{1,0:T(8,128)(2,1)S(1)} %copy-done.143, bf16[512,1152]{1,0:T(8,128)(2,1)S(1)} %copy-done.141, bf16[512,1152]{1,0:T(8,128)(2,1)S(1)} %copy-done.139), kind=kOutput, calls=%fused_computation.1 | convolution fusion | flops 10893164544 | bytes 19464192 | tf_op jit(solution)/shard_map/dot_general | solution.py:61
  765.8 24.0 %collective-permute-done.50 = bf16[256,2304]{1,0:T(8,128)(2,1)S(1)} collective-permute-done((bf16[256,2304]{1,0:T(8,128)(2,1)S(1)}, bf16[256,2304]{1,0:T(8,128)(2,1)S(1)}, u32[]{:S(2)}, u32[]{:S(2)}) %collective-permute-start.50) | collective-permute-done | bytes 1179680 | tf_op jit(solution)/shard_map/ppermute | solution.py:132
  807.9 14.8 %convolution_convert_fusion = bf16[2304,1152]{1,0:T(8,128)(2,1)S(1)} fusion(bf16[2048,2304]{1,0:T(8,128)(2,1)} %get-tuple-element.83, bf16[512,1152]{1,0:T(8,128)(2,1)S(1)} %copy-done.165, bf16[512,1152]{1,0:T(8,128)(2,1)S(1)} %copy-done.162, bf16[512,1152]{1,0:T(8,128)(2,1)S(1)} %copy-done.160, bf16[512,1152]{1,0:T(8,128)(2,1)S(1)} %copy-done.158), kind=kOutput, calls=%fused_computation | convolution fusion | flops 10893164544 | bytes 19464192 | tf_op jit(solution)/shard_map/dot_general | solution.py:61
  837.7 36.2 %collective-permute-done.53 = bf16[256,2304]{1,0:T(8,128)(2,1)} collective-permute-done((bf16[256,2304]{1,0:T(8,128)(2,1)S(1)}, bf16[256,2304]{1,0:T(8,128)(2,1)}, u32[]{:S(2)}, u32[]{:S(2)}) %collective-permute-start.53) | collective-permute-done | bytes 1179680 | tf_op jit(solution)/shard_map/ppermute | solution.py:141
  910.6 33.0 %collective-permute-done.57 = bf16[4,288,512]{2,1,0:T(8,128)(2,1)S(1)} collective-permute-done((bf16[4,288,512]{2,1,0:T(8,128)(2,1)S(1)}, bf16[4,288,512]{2,1,0:T(8,128)(2,1)S(1)}, u32[]{:S(2)}, u32[]{:S(2)}) %collective-permute-start.57) | collective-permute-done | bytes 1179680 | tf_op jit(solution)/shard_map/ppermute | solution.py:135
  982.7 11.2 collective-permute-done.56
  997.9 18.6 %collective-permute-done.58 = bf16[2,512,512]{2,1,0:T(8,128)(2,1)} collective-permute-done((bf16[2,512,512]{2,1,0:T(8,128)(2,1)}, bf16[2,512,512]{2,1,0:T(8,128)(2,1)}, u32[]{:S(2)}, u32[]{:S(2)}) %collective-permute-start.58) | collective-permute-done | bytes 1048608 | tf_op jit(solution)/shard_map/ppermute | solution.py:135
  1024.4 15.6 %collective-permute-done.62 = bf16[4,288,512]{2,1,0:T(8,128)(2,1)S(1)} collective-permute-done((bf16[4,288,512]{2,1,0:T(8,128)(2,1)S(1)}, bf16[4,288,512]{2,1,0:T(8,128)(2,1)S(1)}, u32[]{:S(2)}, u32[]{:S(2)}) %collective-permute-start.62) | collective-permute-done | bytes 1179680 | tf_op jit(solution)/shard_map/ppermute | solution.py:135
  1041.4 12.1 collective-permute-done.60
  1071.2 13.7 %all-to-all-start.6 = ((bf16[4,144,1152]{2,1,0:T(8,128)(2,1)}), bf16[4,144,1152]{2,1,0:T(8,128)(2,1)S(1)}, u32[]{:S(2)}, u32[]{:S(2)}) async-start(bf16[4,144,1152]{2,1,0:T(8,128)(2,1)} %reduce-scatter.8.cloned.1.call-done), calls=%async_computation.9 | async-start | bytes 2654208 | tf_op jit(solution)/shard_map/all_to_all | solution.py:236
  1091.7 25.6 %all-to-all-done.6 = bf16[4,144,1152]{2,1,0:T(8,128)(2,1)S(1)} async-done(((bf16[4,144,1152]{2,1,0:T(8,128)(2,1)}), bf16[4,144,1152]{2,1,0:T(8,128)(2,1)S(1)}, u32[]{:S(2)}, u32[]{:S(2)}) %all-to-all-start.6) | async-done | bytes 1327136 | tf_op jit(solution)/shard_map/all_to_all | solution.py:236
  1136.3 22.2 %collective-permute-done.69 = bf16[4,2,2,144]{3,1,0,2:T(2,128)(2,1)S(1)} collective-permute-done((bf16[4,2,2,144]{3,1,0,2:T(2,128)(2,1)S(1)}, bf16[4,2,2,144]{3,1,0,2:T(2,128)(2,1)S(1)}, u32[]{:S(2)}, u32[]{:S(2)}) %collective-permute-start.69) | collective-permute-done | bytes 4640 | tf_op jit(solution)/shard_map/ppermute | solution.py:135
  1192.0 9.0 collective-permute-done.66
  (810 shorter events, 586.4 us)
Async XLA Ops:
  23.1 193.4 %collective-permute-start.16 = (s32[1]{0:T(128)}, s32[1]{0:T(128)}, u32[]{:S(2)}, u32[]{:S(2)}) collective-permute-start(s32[1]{0:T(128)} %param.19), channel_id=1, source_target_pairs={{0,2},{2,0},{4,6},{6,4},{1,3},{3,1},{5,7},{7,5},{8,10},{10,8},{12,... | collective-permute-start | bytes 20 | tf_op jit(solution)/shard_map/ppermute | solution.py:138
  96.4 33.6 %all-to-all-start = ((bf16[4,144,1152]{2,1,0:T(8,128)(2,1)}), bf16[4,144,1152]{2,1,0:T(8,128)(2,1)}, u32[]{:S(2)}, u32[]{:S(2)}) async-start(bf16[4,144,1152]{2,1,0:T(8,128)(2,1)} %pad_maximum_fusion.11), calls=%async_computation | async-start | bytes 2654208 | tf_op jit(solution)/shard_map/all_to_all | solution.py:236
  100.7 213.8 %all-gather.7.cloned.1.call-start = ((), (), s32[]{:S(2)}) async-start(), calls=%async_computation.15 | async-start | bytes 6635520 | tf_op jit(solution)/shard_map/all_gather | solution.py:274
  133.5 48.6 %collective-permute-start.1 = (bf16[512,2304]{1,0:T(8,128)(2,1)}, bf16[512,2304]{1,0:T(8,128)(2,1)}, u32[]{:S(2)}, u32[]{:S(2)}) collective-permute-start(bf16[512,2304]{1,0:T(8,128)(2,1)} %get-tuple-element.183), channel_id=1, source_target_pairs={{0,2},{2,0},{4,6},{6,4},{1,3},{3,1},{5,7},{7,5},{8,10},{10,8},{12,... | collective-permute-start | bytes 7077896 | tf_op jit(solution)/shard_map/ppermute | solution.py:138
  145.4 34.5 %collective-permute-start.8 = (bf16[2,144,1664]{2,1,0:T(8,128)(2,1)}, bf16[2,144,1664]{2,1,0:T(8,128)(2,1)}, u32[]{:S(2)}, u32[]{:S(2)}) collective-permute-start(bf16[2,144,1664]{2,1,0:T(8,128)(2,1)} %collective-permute-done.7), channel_id=1, source_target_pairs={{0,4},{2,6},{4,0},{6,2},{1,5},{3,7},{5,1},{7,3},{8,12},{10,14},{12... | collective-permute-start | bytes 2875400 | tf_op jit(solution)/shard_map/ppermute | solution.py:135
  149.8 45.3 %all-to-all-start.1 = ((bf16[4,144,1152]{2,1,0:T(8,128)(2,1)}), bf16[4,144,1152]{2,1,0:T(8,128)(2,1)}, u32[]{:S(2)}, u32[]{:S(2)}) async-start(bf16[4,144,1152]{2,1,0:T(8,128)(2,1)} %pad_maximum_fusion.10), calls=%async_computation.1 | async-start | bytes 2654208 | tf_op jit(solution)/shard_map/all_to_all | solution.py:236
  154.1 214.3 %all-gather.9.cloned.1.call-start = ((), (), s32[]{:S(2)}) async-start(), calls=%async_computation.16 | async-start | bytes 6635520 | tf_op jit(solution)/shard_map/all_gather | solution.py:274
  245.5 33.7 %all-to-all-start.2 = ((bf16[4,144,1152]{2,1,0:T(8,128)(2,1)}), bf16[4,144,1152]{2,1,0:T(8,128)(2,1)}, u32[]{:S(2)}, u32[]{:S(2)}) async-start(bf16[4,144,1152]{2,1,0:T(8,128)(2,1)} %pad_maximum_fusion.12), calls=%async_computation.2 | async-start | bytes 2654208 | tf_op jit(solution)/shard_map/all_to_all | solution.py:236
  249.8 193.5 %all-gather.11.cloned.1.call-start = ((), (), s32[]{:S(2)}) async-start(), calls=%async_computation.17 | async-start | bytes 6635520 | tf_op jit(solution)/shard_map/all_gather | solution.py:274
  322.2 503.8 %reduce-scatter.4.cloned.1.call-start = ((), (), s32[]{:S(2)}) async-start(), calls=%async_computation.12 | async-start | bytes 6635520 | tf_op jit(solution)/shard_map/reduce_scatter | solution.py:476
  322.4 42.7 %collective-permute-start.18 = (bf16[256,2304]{1,0:T(8,128)(2,1)}, bf16[256,2304]{1,0:T(8,128)(2,1)S(1)}, u32[]{:S(2)}, u32[]{:S(2)}) collective-permute-start(bf16[256,2304]{1,0:T(8,128)(2,1)} %dynamic-slice_convert_fusion.1), channel_id=1, source_target_pairs={{0,1},{1,0},{2,3},{3,2},{4,5},{5,4},{6,7},{7,6},{8,9},{9,8},{10,11... | collective-permute-start | bytes 3538952 | tf_op jit(solution)/shard_map/ppermute | solution.py:141
  371.6 37.8 %collective-permute-start.22 = (bf16[2,4,144,1152]{3,2,0,1:T(8,128)(2,1)S(1)}, bf16[2,4,144,1152]{3,2,0,1:T(8,128)(2,1)S(1)}, u32[]{:S(2)}, u32[]{:S(2)}) collective-permute-start(bf16[2,4,144,1152]{3,2,0,1:T(8,128)(2,1)S(1)} %bitcast.520), channel_id=1, source_target_pairs={{0,2},{2,0},{4,6},{6,4},{1,3},{3,1},{5,7},{7,5},{8,10},{10,8},{12,... | collective-permute-start | bytes 7962632 | tf_op jit(solution)/shard_map/ppermute | solution.py:138
  445.2 32.7 %collective-permute-start.23 = (bf16[2,4,144,1152]{3,2,0,1:T(8,128)(2,1)S(1)}, bf16[2,4,144,1152]{3,2,0,1:T(8,128)(2,1)S(1)}, u32[]{:S(2)}, u32[]{:S(2)}) collective-permute-start(bf16[2,4,144,1152]{3,2,0,1:T(8,128)(2,1)S(1)} %dynamic-slice_bitcast_fusion.3), channel_id=1, source_target_pairs={{0,2},{2,0},{4,6},{6,4},{1,3},{3,1},{5,7},{7,5},{8,10},{10,8},{12,... | collective-permute-start | bytes 7962632 | tf_op jit(solution)/shard_map/ppermute | solution.py:138
  652.6 53.7 %collective-permute-start.41 = (bf16[256,2304]{1,0:T(8,128)(2,1)}, bf16[256,2304]{1,0:T(8,128)(2,1)}, u32[]{:S(2)}, u32[]{:S(2)}) collective-permute-start(bf16[256,2304]{1,0:T(8,128)(2,1)} %fusion.74), channel_id=1, source_target_pairs={{0,8},{8,16},{16,24},{24,0},{1,9},{9,17},{17,25},{25,1},{2,10},{10... | collective-permute-start | bytes 3538952 | tf_op jit(solution)/shard_map/ppermute | solution.py:132
  727.0 161.0 %reduce-scatter.6.cloned.1.call-start = ((), (), s32[]{:S(2)}) async-start(), calls=%async_computation.13 | async-start | bytes 6635520 | tf_op jit(solution)/shard_map/reduce_scatter | solution.py:476
  759.1 32.5 %collective-permute-start.52 = (bf16[2,4,144,1152]{3,2,0,1:T(8,128)(2,1)S(1)}, bf16[2,4,144,1152]{3,2,0,1:T(8,128)(2,1)S(1)}, u32[]{:S(2)}, u32[]{:S(2)}) collective-permute-start(bf16[2,4,144,1152]{3,2,0,1:T(8,128)(2,1)S(1)} %dynamic-slice_bitcast_fusion.1), channel_id=1, source_target_pairs={{0,2},{2,0},{4,6},{6,4},{1,3},{3,1},{5,7},{7,5},{8,10},{10,8},{12,... | collective-permute-start | bytes 7962632 | tf_op jit(solution)/shard_map/ppermute | solution.py:138
  826.0 47.9 %all-to-all-start.3 = ((bf16[4,144,1152]{2,1,0:T(8,128)(2,1)}), bf16[4,144,1152]{2,1,0:T(8,128)(2,1)S(1)}, u32[]{:S(2)}, u32[]{:S(2)}) async-start(bf16[4,144,1152]{2,1,0:T(8,128)(2,1)} %reduce-scatter.4.cloned.1.call-done), calls=%async_computation.4 | async-start | bytes 2654208 | tf_op jit(solution)/shard_map/all_to_all | solution.py:236
  829.5 241.7 %reduce-scatter.8.cloned.1.call-start = ((), (), s32[]{:S(2)}) async-start(), calls=%async_computation.14 | async-start | bytes 6635520 | tf_op jit(solution)/shard_map/reduce_scatter | solution.py:476
  830.0 43.9 %collective-permute-start.53 = (bf16[256,2304]{1,0:T(8,128)(2,1)S(1)}, bf16[256,2304]{1,0:T(8,128)(2,1)}, u32[]{:S(2)}, u32[]{:S(2)}) collective-permute-start(bf16[256,2304]{1,0:T(8,128)(2,1)S(1)} %multiply_convert_fusion.3), channel_id=1, source_target_pairs={{0,1},{1,0},{2,3},{3,2},{4,5},{5,4},{6,7},{7,6},{8,9},{9,8},{10,11... | collective-permute-start | bytes 3538952 | tf_op jit(solution)/shard_map/ppermute | solution.py:141
  888.0 57.0 %all-to-all-start.4 = ((bf16[4,144,1152]{2,1,0:T(8,128)(2,1)}), bf16[4,144,1152]{2,1,0:T(8,128)(2,1)}, u32[]{:S(2)}, u32[]{:S(2)}) async-start(bf16[4,144,1152]{2,1,0:T(8,128)(2,1)} %reduce-scatter.6.cloned.1.call-done), calls=%async_computation.6 | async-start | bytes 2654208 | tf_op jit(solution)/shard_map/all_to_all | solution.py:236
  897.7 45.9 %collective-permute-start.57 = (bf16[4,288,512]{2,1,0:T(8,128)(2,1)S(1)}, bf16[4,288,512]{2,1,0:T(8,128)(2,1)S(1)}, u32[]{:S(2)}, u32[]{:S(2)}) collective-permute-start(bf16[4,288,512]{2,1,0:T(8,128)(2,1)S(1)} %dynamic-slice_bitcast_fusion.7), channel_id=1, source_target_pairs={{0,4},{2,6},{4,0},{6,2},{1,5},{3,7},{5,1},{7,3},{8,12},{10,14},{12... | collective-permute-start | bytes 3538952 | tf_op jit(solution)/shard_map/ppermute | solution.py:135
  945.0 50.5 %all-to-all-start.5 = ((bf16[4,288,512]{2,1,0:T(8,128)(2,1)}), bf16[4,288,512]{2,1,0:T(8,128)(2,1)}, u32[]{:S(2)}, u32[]{:S(2)}) async-start(bf16[4,288,512]{2,1,0:T(8,128)(2,1)} %fusion.97), calls=%async_computation.7 | async-start | bytes 2359296 | tf_op jit(solution)/shard_map/all_to_all | solution.py:236
  969.6 46.8 %collective-permute-start.58 = (bf16[2,512,512]{2,1,0:T(8,128)(2,1)}, bf16[2,512,512]{2,1,0:T(8,128)(2,1)}, u32[]{:S(2)}, u32[]{:S(2)}) collective-permute-start(bf16[2,512,512]{2,1,0:T(8,128)(2,1)} %pad_maximum_fusion.21), channel_id=1, source_target_pairs={{0,4},{2,6},{4,0},{6,2},{1,5},{3,7},{5,1},{7,3},{8,12},{10,14},{12... | collective-permute-start | bytes 3145736 | tf_op jit(solution)/shard_map/ppermute | solution.py:135
  997.0 43.0 %collective-permute-start.62 = (bf16[4,288,512]{2,1,0:T(8,128)(2,1)S(1)}, bf16[4,288,512]{2,1,0:T(8,128)(2,1)S(1)}, u32[]{:S(2)}, u32[]{:S(2)}) collective-permute-start(bf16[4,288,512]{2,1,0:T(8,128)(2,1)S(1)} %dynamic-slice_bitcast_fusion.6), channel_id=1, source_target_pairs={{0,4},{2,6},{4,0},{6,2},{1,5},{3,7},{5,1},{7,3},{8,12},{10,14},{12... | collective-permute-start | bytes 3538952 | tf_op jit(solution)/shard_map/ppermute | solution.py:135
  1020.4 33.1 %collective-permute-start.60 = (bf16[512,512]{1,0:T(8,128)(2,1)S(1)}, bf16[512,512]{1,0:T(8,128)(2,1)S(1)}, u32[]{:S(2)}, u32[]{:S(2)}) collective-permute-start(bf16[512,512]{1,0:T(8,128)(2,1)S(1)} %get-tuple-element.242), channel_id=1, source_target_pairs={{0,16},{8,24},{16,0},{24,8},{1,17},{9,25},{17,1},{25,9},{2,18},{10... | collective-permute-start | bytes 1572872 | tf_op jit(solution)/shard_map/ppermute | solution.py:132
  1071.2 50.6 %collective-permute-start.63 = (bf16[512,2304]{1,0:T(8,128)(2,1)}, bf16[512,2304]{1,0:T(8,128)(2,1)}, u32[]{:S(2)}, u32[]{:S(2)}) collective-permute-start(bf16[512,2304]{1,0:T(8,128)(2,1)} %slice.774), channel_id=1, source_target_pairs={{0,2},{2,0},{4,6},{6,4},{1,3},{3,1},{5,7},{7,5},{8,10},{10,8},{12,... | collective-permute-start | bytes 7077896 | tf_op jit(solution)/shard_map/ppermute | solution.py:138
  1071.2 46.1 %all-to-all-start.6 = ((bf16[4,144,1152]{2,1,0:T(8,128)(2,1)}), bf16[4,144,1152]{2,1,0:T(8,128)(2,1)S(1)}, u32[]{:S(2)}, u32[]{:S(2)}) async-start(bf16[4,144,1152]{2,1,0:T(8,128)(2,1)} %reduce-scatter.8.cloned.1.call-done), calls=%async_computation.9 | async-start | bytes 2654208 | tf_op jit(solution)/shard_map/all_to_all | solution.py:236
  1090.1 43.4 %collective-permute-start.36 = (bf16[256,2304]{1,0:T(8,128)(2,1)S(1)}, bf16[256,2304]{1,0:T(8,128)(2,1)}, u32[]{:S(2)}, u32[]{:S(2)}) collective-permute-start(bf16[256,2304]{1,0:T(8,128)(2,1)S(1)} %copy-done.41), channel_id=1, source_target_pairs={{0,1},{1,0},{2,3},{3,2},{4,5},{5,4},{6,7},{7,6},{8,9},{9,8},{10,11... | collective-permute-start | bytes 3538952 | tf_op jit(solution)/shard_map/ppermute | solution.py:141
  1117.3 48.2 %all-to-all-start.7 = ((bf16[4,288,512]{2,1,0:T(8,128)(2,1)}), bf16[4,288,512]{2,1,0:T(8,128)(2,1)}, u32[]{:S(2)}, u32[]{:S(2)}) async-start(bf16[4,288,512]{2,1,0:T(8,128)(2,1)} %convert_add_fusion.1), calls=%async_computation.10 | async-start | bytes 2359296 | tf_op jit(solution)/shard_map/all_to_all | solution.py:236
  1126.8 42.3 %collective-permute-start.64 = (bf16[256,2304]{1,0:T(8,128)(2,1)}, bf16[256,2304]{1,0:T(8,128)(2,1)}, u32[]{:S(2)}, u32[]{:S(2)}) collective-permute-start(bf16[256,2304]{1,0:T(8,128)(2,1)} %dynamic-slice_convert_fusion), channel_id=1, source_target_pairs={{0,1},{1,0},{2,3},{3,2},{4,5},{5,4},{6,7},{7,6},{8,9},{9,8},{10,11... | collective-permute-start | bytes 3538952 | tf_op jit(solution)/shard_map/ppermute | solution.py:141
  1131.3 32.9 %collective-permute-start.65 = (bf16[4,288,512]{2,1,0:T(8,128)(2,1)S(1)}, bf16[4,288,512]{2,1,0:T(8,128)(2,1)S(1)}, u32[]{:S(2)}, u32[]{:S(2)}) collective-permute-start(bf16[4,288,512]{2,1,0:T(8,128)(2,1)S(1)} %dynamic-slice_bitcast_fusion.5), channel_id=1, source_target_pairs={{0,4},{2,6},{4,0},{6,2},{1,5},{3,7},{5,1},{7,3},{8,12},{10,14},{12... | collective-permute-start | bytes 3538952 | tf_op jit(solution)/shard_map/ppermute | solution.py:135
  1165.5 35.6 %all-to-all-start.8 = ((bf16[4,288,512]{2,1,0:T(8,128)(2,1)}), bf16[4,288,512]{2,1,0:T(8,128)(2,1)S(1)}, u32[]{:S(2)}, u32[]{:S(2)}) async-start(bf16[4,288,512]{2,1,0:T(8,128)(2,1)} %convert_add_fusion), calls=%async_computation.11 | async-start | bytes 2359296 | tf_op jit(solution)/shard_map/all_to_all | solution.py:236
  (240 other events, 2986.0 us)
Sparse Core Ops, SparseCore 0:
  130.1 76.7 all-gather.6
  234.6 66.0 all-gather.8
  322.3 73.9 all-gather.10
  727.1 62.4 reduce-scatter.3
  802.5 75.3 reduce-scatter.5
  881.0 80.7 reduce-scatter.7

commit v3 on v2

--- a/solution.py
+++ b/solution.py
@@ -503,6 +503,11 @@
     up_sum = reduce(up_terms)
     down_got = over_z(tie(down_sum, grad_branch))
     branch_rows = rows_of(grad_branch, tie(tp_swap(grad_branch), up_terms, down_got))
+    post_terms = jnp.stack([grad_post_attn, grad_post_mlp], axis=0)
+    post_terms = post_terms.reshape(2, z_size, y_size, 2, part).transpose(1, 2, 3, 0, 4)
+    post_y = scatter_y(post_terms)
+    branch_rows = tie(branch_rows, post_y)
+    post_z = scatter_z(post_y)
     branch_chip = jnp.concatenate([branch_rows, core_swap(branch_rows)], axis=0)
     grad_attn = matmul(branch_chip, out_w).astype(bf16)
     grad_out_w = matmul_lt(tie(branch_chip, grad_attn), attn_out).astype(bf16)
@@ -520,7 +525,7 @@
     )
     prompt_gkv = jnp.concatenate([prompt_gk, prompt_gv], axis=1)
     gate_got = over_z(tie(gate_sum, grad_attn))
-    grad_heads = tie(grad_heads, gate_got)
+    grad_heads = tie(grad_heads, gate_got, *post_z)
     cont_gq, cont_gkv, own_gkv = [], [], []
     for i in range(2 * cont_count):
         at = prompt_local + (i % cont_count) * cont_size
@@ -551,7 +556,8 @@
         return total
 
     out_got = over_z(out_y)
-    kv_terms, kv_total = scatter_grid(kv_take, pairs, (out_y, out_got))
+    up_got = over_z(tie(up_sum, out_got))
+    kv_terms, kv_total = scatter_grid(kv_take, pairs, (out_y, up_got))
     grad_q = rows_order(prompt_gq.reshape(shared_by, 2, prompt_local, HD), cont_gq)
     grad_q_proj = jnp.concatenate(
         [
@@ -561,11 +567,8 @@
         axis=1,
     ).astype(bf16)
     grad_q_w = matmul_lt(chip_rows, grad_q_proj).astype(bf16)
-    post_terms = jnp.stack([grad_post_attn, grad_post_mlp], axis=0)
-    post_terms = post_terms.reshape(2, z_size, y_size, 2, part).transpose(1, 2, 3, 0, 4)
     q_y = scatter_y(tie(grad_q_w, kv_total).reshape(z_size, y_size, 2 * part, q_cols))
     kv_low = add_up(tie(kv_terms, q_y))
-    up_got = over_z(tie(up_sum, q_y))
     kv_sum = kv_low.reshape(2, prompt_local, 2 * HD)
     halves = []
     for half in range(2):
@@ -583,10 +586,9 @@
     one_got = tp_swap(one_give)
     grad_kv_w = matmul_lt(tie(chip_rows, one_give), grad_kv_proj).astype(bf16)
     kvw_y = scatter_y(grad_kv_w.reshape(z_size, y_size, 2 * part, 2 * kv_cols))
-    q_got = over_z(tie(q_y, up_got).astype(bf16))
-    one_got = tie(one_got, up_got, q_got, kvw_y)
+    q_got = over_z(tie(q_y, one_give).astype(bf16))
+    one_got = tie(one_got, q_got)
     grad_one = take_share(one_core) + one_got.astype(f32)
-    post_z = scatter_z(scatter_y(tie(post_terms, one_give)))
     grad_input = grad_middle + norm_back(grad_one, take_share(normal_one), take_share(inverse_one))
     input_low = grad_input.astype(bf16)
     kvw_got = over_z(kvw_y.astype(bf16))
@@ -596,7 +598,7 @@
     out_sum = jnp.sum(tie(out_got, input_low).astype(f32), axis=0)
     q_sum = jnp.sum(tie(q_got, input_low).astype(f32), axis=0)
     kvw_sum = jnp.sum(tie(kvw_got, input_low).astype(f32), axis=0)
-    post_sum = add_up(tie(post_z, input_low))
+    post_sum = add_up(post_z)
     input_rows = rows_of(input_low, tp_swap(input_low)).astype(f32)
 
     def split_core(summed):

time: 1230 us -> 1210 us (0.984)
  waiting for transfers between devices: 599 us -> 566 us
    ppermute x14, waiting for transfers between devices: 217 us -> 190 us  [y_next(): lax.ppermute(values, 'ctx', [(i, (i + 2) % c_size) for i in range(c_size)])]
    unnamed x379 -> x377, local copies, waits for them, and re-layouts: 59.1 us -> 63.6 us
  transfers between devices with their start and end apart: 91 -> 91, of which waited for: 44 -> 46; matrix products, arithmetic and copies ran while one was open for 36% -> 36% of each run, Pallas kernels for 0% -> 0%
where the time goes in v3:
time: 1210 us; the launch traced here: 1190 us
  waiting for transfers between devices  566 us (47%)
  matrix products  232 us (19%)
  local copies, waits for them, and re-layouts  152 us (13%)
  other arithmetic  125 us (10%)
  starting transfers between devices  96.3 us (8%)
  between operations  23.6 us (2%)
    ppermute x24, waiting for transfers between devices, z_shift(): lax.ppermute(values, 'fsdp', [(i, (i + step) % z_size) for i in range(z_s...  234 us
    ppermute x14, waiting for transfers between devices, y_next(): lax.ppermute(values, 'ctx', [(i, (i + 2) % c_size) for i in range(c_size)])  190 us
    dot_general x20, matrix products, matmul(): return jnp.dot(left, right, preferred_element_type=f32)  89.5 us
    dot_general x22, matrix products, matmul_rt(): lax.dot_general(left, right, (((1,), (1,)), ((), ())), preferred_element_...  76.8 us
    ppermute x6, waiting for transfers between devices, tp_swap(): return lax.ppermute(values, 'tp', [(0, 1), (1, 0)])  76.5 us
    dot_general x12, matrix products, matmul_lt(): lax.dot_general(left, right, (((0,), (0,)), ((), ())), preferred_element_...  65.3 us
    unnamed x377, local copies, waits for them, and re-layouts  63.6 us
    all_to_all x9, waiting for transfers between devices, over_z(): return lax.all_to_all(values, 'fsdp', 0, 0, tiled=True)  49.7 us
  transfers between devices with their start and end apart: 91, of which 46 were waited for; matrix products, arithmetic and copies ran while one was open for 36% of the time, Pallas kernels for 0%

profile of v3, /device:TPU:0, one launch (start us, length us, event | category | flops | bytes accessed | tf_op | source)
XLA Modules:
  0.0 1194.7 jit_solution(5861202423053143938)
XLA Ops:
  23.2 20.6 %collective-permute-done.2 = bf16[2,144,1664]{2,1,0:T(8,128)(2,1)} collective-permute-done((bf16[2,144,1664]{2,1,0:T(8,128)(2,1)}, bf16[2,144,1664]{2,1,0:T(8,128)(2,1)}, u32[]{:S(2)}, u32[]{:S(2)}) %collective-permute-start.2) | collective-permute-done | bytes 958496 | tf_op jit(solution)/shard_map/ppermute | solution.py:135
  48.2 21.7 %collective-permute-done.4 = bf16[2,144,1664]{2,1,0:T(8,128)(2,1)S(1)} collective-permute-done((bf16[2,144,1664]{2,1,0:T(8,128)(2,1)}, bf16[2,144,1664]{2,1,0:T(8,128)(2,1)S(1)}, u32[]{:S(2)}, u32[]{:S(2)}) %collective-permute-start.4) | collective-permute-done | bytes 958496 | tf_op jit(solution)/shard_map/ppermute | solution.py:135
  75.7 18.0 %collective-permute-done.6 = bf16[2,144,1664]{2,1,0:T(8,128)(2,1)S(1)} collective-permute-done((bf16[2,144,1664]{2,1,0:T(8,128)(2,1)S(1)}, bf16[2,144,1664]{2,1,0:T(8,128)(2,1)S(1)}, u32[]{:S(2)}, u32[]{:S(2)}) %collective-permute-start.6) | collective-permute-done | bytes 958496 | tf_op jit(solution)/shard_map/ppermute | solution.py:135
  106.7 23.3 %all-to-all-done = bf16[4,144,1152]{2,1,0:T(8,128)(2,1)} async-done(((bf16[4,144,1152]{2,1,0:T(8,128)(2,1)}), bf16[4,144,1152]{2,1,0:T(8,128)(2,1)}, u32[]{:S(2)}, u32[]{:S(2)}) %all-to-all-start) | async-done | bytes 1327136 | tf_op jit(solution)/shard_map/all_to_all | solution.py:236
  154.2 25.7 %collective-permute-done.8 = bf16[2,144,1664]{2,1,0:T(8,128)(2,1)S(1)} collective-permute-done((bf16[2,144,1664]{2,1,0:T(8,128)(2,1)}, bf16[2,144,1664]{2,1,0:T(8,128)(2,1)S(1)}, u32[]{:S(2)}, u32[]{:S(2)}) %collective-permute-start.8) | collective-permute-done | bytes 958496 | tf_op jit(solution)/shard_map/ppermute | solution.py:135
  180.9 8.3 fusion
  199.2 10.2 collective-permute-done.10
  219.7 8.3 collective-permute-done.11
  234.4 8.1 collective-permute-done.13
  264.8 11.5 collective-permute-done.15
  327.5 36.9 %collective-permute-done.18 = bf16[256,2304]{1,0:T(8,128)(2,1)S(1)} collective-permute-done((bf16[256,2304]{1,0:T(8,128)(2,1)S(1)}, bf16[256,2304]{1,0:T(8,128)(2,1)S(1)}, u32[]{:S(2)}, u32[]{:S(2)}) %collective-permute-start.18) | collective-permute-done | bytes 1179680 | tf_op jit(solution)/shard_map/ppermute | solution.py:141
  372.3 25.7 %collective-permute-done.20 = bf16[256,2304]{1,0:T(8,128)(2,1)} collective-permute-done((bf16[256,2304]{1,0:T(8,128)(2,1)S(1)}, bf16[256,2304]{1,0:T(8,128)(2,1)}, u32[]{:S(2)}, u32[]{:S(2)}) %collective-permute-start.20) | collective-permute-done | bytes 1179680 | tf_op jit(solution)/shard_map/ppermute | solution.py:132
  409.2 19.3 %collective-permute-done.26 = bf16[256,2304]{1,0:T(8,128)(2,1)} collective-permute-done((bf16[256,2304]{1,0:T(8,128)(2,1)}, bf16[256,2304]{1,0:T(8,128)(2,1)}, u32[]{:S(2)}, u32[]{:S(2)}) %collective-permute-start.26) | collective-permute-done | bytes 1179680 | tf_op jit(solution)/shard_map/ppermute | solution.py:132
  447.5 11.6 collective-permute-done.30
  504.8 19.2 %collective-permute-done.25 = bf16[256,2304]{1,0:T(8,128)(2,1)} collective-permute-done((bf16[256,2304]{1,0:T(8,128)(2,1)}, bf16[256,2304]{1,0:T(8,128)(2,1)}, u32[]{:S(2)}, u32[]{:S(2)}) %collective-permute-start.25) | collective-permute-done | bytes 1179680 | tf_op jit(solution)/shard_map/ppermute | solution.py:132
  537.6 18.5 %collective-permute-done.29 = bf16[256,2304]{1,0:T(8,128)(2,1)S(1)} collective-permute-done((bf16[256,2304]{1,0:T(8,128)(2,1)}, bf16[256,2304]{1,0:T(8,128)(2,1)S(1)}, u32[]{:S(2)}, u32[]{:S(2)}) %collective-permute-start.29) | collective-permute-done | bytes 1179680 | tf_op jit(solution)/shard_map/ppermute | solution.py:132
  557.3 27.1 %collective-permute-done.33 = bf16[256,2304]{1,0:T(8,128)(2,1)S(1)} collective-permute-done((bf16[256,2304]{1,0:T(8,128)(2,1)S(1)}, bf16[256,2304]{1,0:T(8,128)(2,1)S(1)}, u32[]{:S(2)}, u32[]{:S(2)}) %collective-permute-start.33) | collective-permute-done | bytes 1179680 | tf_op jit(solution)/shard_map/ppermute | solution.py:132
  606.0 14.3 %collective-permute-done.37 = bf16[256,2304]{1,0:T(8,128)(2,1)S(1)} collective-permute-done((bf16[256,2304]{1,0:T(8,128)(2,1)S(1)}, bf16[256,2304]{1,0:T(8,128)(2,1)S(1)}, u32[]{:S(2)}, u32[]{:S(2)}) %collective-permute-start.37) | collective-permute-done | bytes 1179680 | tf_op jit(solution)/shard_map/ppermute | solution.py:132
  653.3 27.8 %collective-permute-done.46 = bf16[256,2304]{1,0:T(8,128)(2,1)S(1)} collective-permute-done((bf16[256,2304]{1,0:T(8,128)(2,1)S(1)}, bf16[256,2304]{1,0:T(8,128)(2,1)S(1)}, u32[]{:S(2)}, u32[]{:S(2)}) %collective-permute-start.46) | collective-permute-done | bytes 1179680 | tf_op jit(solution)/shard_map/ppermute | solution.py:132
  681.1 7.8 fusion.51
  698.3 15.0 %convolution_convert_fusion.2 = bf16[2304,1152]{1,0:T(8,128)(2,1)S(1)} fusion(bf16[2048,2304]{1,0:T(8,128)(2,1)} %constant_dynamic-update-slice_fusion.6, bf16[512,1152]{1,0:T(8,128)(2,1)S(1)} %copy-done.149, bf16[512,1152]{1,0:T(8,128)(2,1)S(1)} %copy-done.147, bf16[512,1152]{1,0:T(8,128)(2,1)S(1)} %copy-done.145, bf16[512,1152]{1,0:T(8,128)(2,1)S(1)} %copy-done.157), kind=kOutput, calls=%fused_computation.2 | convolution fusion | flops 10893164544 | bytes 19464192 | tf_op jit(solution)/shard_map/dot_general | solution.py:61
  728.6 9.1 fusion.58
  757.1 13.1 %convolution_convert_fusion.1 = bf16[2304,1152]{1,0:T(8,128)(2,1)S(1)} fusion(bf16[2048,2304]{1,0:T(8,128)(2,1)S(1)} %bitcast.564, bf16[512,1152]{1,0:T(8,128)(2,1)S(1)} %get-tuple-element.155, bf16[512,1152]{1,0:T(8,128)(2,1)S(1)} %copy-done.140, bf16[512,1152]{1,0:T(8,128)(2,1)S(1)} %copy-done.138, bf16[512,1152]{1,0:T(8,128)(2,1)S(1)} %copy-done.137), kind=kOutput, calls=%fused_computation.1 | convolution fusion | flops 10893164544 | bytes 19464192 | tf_op jit(solution)/shard_map/dot_general | solution.py:61
  779.4 24.5 %collective-permute-done.50 = bf16[256,2304]{1,0:T(8,128)(2,1)} collective-permute-done((bf16[256,2304]{1,0:T(8,128)(2,1)}, bf16[256,2304]{1,0:T(8,128)(2,1)}, u32[]{:S(2)}, u32[]{:S(2)}) %collective-permute-start.50) | collective-permute-done | bytes 1179680 | tf_op jit(solution)/shard_map/ppermute | solution.py:132
  813.7 13.2 %convolution_convert_fusion = bf16[2304,1152]{1,0:T(8,128)(2,1)S(1)} fusion(bf16[2048,2304]{1,0:T(8,128)(2,1)S(1)} %bitcast.566, bf16[512,1152]{1,0:T(8,128)(2,1)S(1)} %copy-done.159, bf16[512,1152]{1,0:T(8,128)(2,1)S(1)} %copy-done.155, bf16[512,1152]{1,0:T(8,128)(2,1)S(1)} %copy-done.153, bf16[512,1152]{1,0:T(8,128)(2,1)S(1)} %copy-done.151), kind=kOutput, calls=%fused_computation | convolution fusion | flops 10893164544 | bytes 19464192 | tf_op jit(solution)/shard_map/dot_general | solution.py:61
  844.3 32.7 %collective-permute-done.53 = bf16[256,2304]{1,0:T(8,128)(2,1)} collective-permute-done((bf16[256,2304]{1,0:T(8,128)(2,1)S(1)}, bf16[256,2304]{1,0:T(8,128)(2,1)}, u32[]{:S(2)}, u32[]{:S(2)}) %collective-permute-start.53) | collective-permute-done | bytes 1179680 | tf_op jit(solution)/shard_map/ppermute | solution.py:141
  922.7 31.1 %collective-permute-done.61 = bf16[4,288,512]{2,1,0:T(8,128)(2,1)S(1)} collective-permute-done((bf16[4,288,512]{2,1,0:T(8,128)(2,1)S(1)}, bf16[4,288,512]{2,1,0:T(8,128)(2,1)S(1)}, u32[]{:S(2)}, u32[]{:S(2)}) %collective-permute-start.61) | collective-permute-done | bytes 1179680 | tf_op jit(solution)/shard_map/ppermute | solution.py:135
  1008.9 13.3 %all-to-all-done.6 = bf16[4,144,1152]{2,1,0:T(8,128)(2,1)} async-done(((bf16[4,144,1152]{2,1,0:T(8,128)(2,1)}), bf16[4,144,1152]{2,1,0:T(8,128)(2,1)}, u32[]{:S(2)}, u32[]{:S(2)}) %all-to-all-start.6) | async-done | bytes 1327136 | tf_op jit(solution)/shard_map/all_to_all | solution.py:236
  1033.5 17.3 %collective-permute-done.66 = bf16[4,288,512]{2,1,0:T(8,128)(2,1)S(1)} collective-permute-done((bf16[4,288,512]{2,1,0:T(8,128)(2,1)S(1)}, bf16[4,288,512]{2,1,0:T(8,128)(2,1)S(1)}, u32[]{:S(2)}, u32[]{:S(2)}) %collective-permute-start.66) | collective-permute-done | bytes 1179680 | tf_op jit(solution)/shard_map/ppermute | solution.py:135
  1052.1 11.4 collective-permute-done.64
  1094.9 12.1 %all-to-all-start.7 = ((bf16[4,288,512]{2,1,0:T(8,128)(2,1)}), bf16[4,288,512]{2,1,0:T(8,128)(2,1)S(1)}, u32[]{:S(2)}, u32[]{:S(2)}) async-start(bf16[4,288,512]{2,1,0:T(8,128)(2,1)} %convert_add_fusion.1), calls=%async_computation.10 | async-start | bytes 2359296 | tf_op jit(solution)/shard_map/all_to_all | solution.py:236
  1117.9 21.9 %collective-permute-done.71 = bf16[4,288,512]{2,1,0:T(8,128)(2,1)S(1)} collective-permute-done((bf16[4,288,512]{2,1,0:T(8,128)(2,1)S(1)}, bf16[4,288,512]{2,1,0:T(8,128)(2,1)S(1)}, u32[]{:S(2)}, u32[]{:S(2)}) %collective-permute-start.71) | collective-permute-done | bytes 1179680 | tf_op jit(solution)/shard_map/ppermute | solution.py:135
  (808 shorter events, 592.6 us)
Async XLA Ops:
  23.1 193.4 %collective-permute-start.16 = (s32[1]{0:T(128)}, s32[1]{0:T(128)}, u32[]{:S(2)}, u32[]{:S(2)}) collective-permute-start(s32[1]{0:T(128)} %param.19), channel_id=1, source_target_pairs={{0,2},{2,0},{4,6},{6,4},{1,3},{3,1},{5,7},{7,5},{8,10},{10,8},{12,... | collective-permute-start | bytes 20 | tf_op jit(solution)/shard_map/ppermute | solution.py:138
  96.4 33.6 %all-to-all-start = ((bf16[4,144,1152]{2,1,0:T(8,128)(2,1)}), bf16[4,144,1152]{2,1,0:T(8,128)(2,1)}, u32[]{:S(2)}, u32[]{:S(2)}) async-start(bf16[4,144,1152]{2,1,0:T(8,128)(2,1)} %pad_maximum_fusion.10), calls=%async_computation | async-start | bytes 2654208 | tf_op jit(solution)/shard_map/all_to_all | solution.py:236
  100.7 212.7 %all-gather.7.cloned.1.call-start = ((), (), s32[]{:S(2)}) async-start(), calls=%async_computation.15 | async-start | bytes 6635520 | tf_op jit(solution)/shard_map/all_gather | solution.py:274
  133.5 47.4 %collective-permute-start.1 = (bf16[512,2304]{1,0:T(8,128)(2,1)}, bf16[512,2304]{1,0:T(8,128)(2,1)}, u32[]{:S(2)}, u32[]{:S(2)}) collective-permute-start(bf16[512,2304]{1,0:T(8,128)(2,1)} %get-tuple-element.177), channel_id=1, source_target_pairs={{0,2},{2,0},{4,6},{6,4},{1,3},{3,1},{5,7},{7,5},{8,10},{10,8},{12,... | collective-permute-start | bytes 7077896 | tf_op jit(solution)/shard_map/ppermute | solution.py:138
  145.4 34.5 %collective-permute-start.8 = (bf16[2,144,1664]{2,1,0:T(8,128)(2,1)}, bf16[2,144,1664]{2,1,0:T(8,128)(2,1)S(1)}, u32[]{:S(2)}, u32[]{:S(2)}) collective-permute-start(bf16[2,144,1664]{2,1,0:T(8,128)(2,1)} %collective-permute-done.7), channel_id=1, source_target_pairs={{0,4},{2,6},{4,0},{6,2},{1,5},{3,7},{5,1},{7,3},{8,12},{10,14},{12... | collective-permute-start | bytes 2875400 | tf_op jit(solution)/shard_map/ppermute | solution.py:135
  149.8 44.0 %all-to-all-start.1 = ((bf16[4,144,1152]{2,1,0:T(8,128)(2,1)}), bf16[4,144,1152]{2,1,0:T(8,128)(2,1)}, u32[]{:S(2)}, u32[]{:S(2)}) async-start(bf16[4,144,1152]{2,1,0:T(8,128)(2,1)} %pad_maximum_fusion.9), calls=%async_computation.1 | async-start | bytes 2654208 | tf_op jit(solution)/shard_map/all_to_all | solution.py:236
  154.2 213.6 %all-gather.9.cloned.1.call-start = ((), (), s32[]{:S(2)}) async-start(), calls=%async_computation.16 | async-start | bytes 6635520 | tf_op jit(solution)/shard_map/all_gather | solution.py:274
  245.6 33.8 %all-to-all-start.2 = ((bf16[4,144,1152]{2,1,0:T(8,128)(2,1)}), bf16[4,144,1152]{2,1,0:T(8,128)(2,1)}, u32[]{:S(2)}, u32[]{:S(2)}) async-start(bf16[4,144,1152]{2,1,0:T(8,128)(2,1)} %pad_maximum_fusion.11), calls=%async_computation.2 | async-start | bytes 2654208 | tf_op jit(solution)/shard_map/all_to_all | solution.py:236
  249.9 192.8 %all-gather.11.cloned.1.call-start = ((), (), s32[]{:S(2)}) async-start(), calls=%async_computation.17 | async-start | bytes 6635520 | tf_op jit(solution)/shard_map/all_gather | solution.py:274
  321.5 508.6 %reduce-scatter.4.cloned.1.call-start = ((), (), s32[]{:S(2)}) async-start(), calls=%async_computation.12 | async-start | bytes 6635520 | tf_op jit(solution)/shard_map/reduce_scatter | solution.py:476
  322.0 42.5 %collective-permute-start.18 = (bf16[256,2304]{1,0:T(8,128)(2,1)S(1)}, bf16[256,2304]{1,0:T(8,128)(2,1)S(1)}, u32[]{:S(2)}, u32[]{:S(2)}) collective-permute-start(bf16[256,2304]{1,0:T(8,128)(2,1)S(1)} %dynamic-slice_convert_fusion.1), channel_id=1, source_target_pairs={{0,1},{1,0},{2,3},{3,2},{4,5},{5,4},{6,7},{7,6},{8,9},{9,8},{10,11... | collective-permute-start | bytes 3538952 | tf_op jit(solution)/shard_map/ppermute | solution.py:141
  370.9 37.8 %collective-permute-start.22 = (bf16[2,4,144,1152]{3,2,0,1:T(8,128)(2,1)S(1)}, bf16[2,4,144,1152]{3,2,0,1:T(8,128)(2,1)S(1)}, u32[]{:S(2)}, u32[]{:S(2)}) collective-permute-start(bf16[2,4,144,1152]{3,2,0,1:T(8,128)(2,1)S(1)} %bitcast.528), channel_id=1, source_target_pairs={{0,2},{2,0},{4,6},{6,4},{1,3},{3,1},{5,7},{7,5},{8,10},{10,8},{12,... | collective-permute-start | bytes 7962632 | tf_op jit(solution)/shard_map/ppermute | solution.py:138
  398.0 30.7 %collective-permute-start.21 = (bf16[256,2304]{1,0:T(8,128)(2,1)}, bf16[256,2304]{1,0:T(8,128)(2,1)S(1)}, u32[]{:S(2)}, u32[]{:S(2)}) collective-permute-start(bf16[256,2304]{1,0:T(8,128)(2,1)} %collective-permute-done.20), channel_id=1, source_target_pairs={{0,2},{2,0},{4,6},{6,4},{1,3},{3,1},{5,7},{7,5},{8,10},{10,8},{12,... | collective-permute-start | bytes 3538952 | tf_op jit(solution)/shard_map/ppermute | solution.py:138
  428.5 30.7 %collective-permute-start.27 = (bf16[256,2304]{1,0:T(8,128)(2,1)}, bf16[256,2304]{1,0:T(8,128)(2,1)}, u32[]{:S(2)}, u32[]{:S(2)}) collective-permute-start(bf16[256,2304]{1,0:T(8,128)(2,1)} %collective-permute-done.26), channel_id=1, source_target_pairs={{0,2},{2,0},{4,6},{6,4},{1,3},{3,1},{5,7},{7,5},{8,10},{10,8},{12,... | collective-permute-start | bytes 3538952 | tf_op jit(solution)/shard_map/ppermute | solution.py:138
  428.5 30.6 %collective-permute-start.30 = (bf16[256,2304]{1,0:T(8,128)(2,1)}, bf16[256,2304]{1,0:T(8,128)(2,1)}, u32[]{:S(2)}, u32[]{:S(2)}) collective-permute-start(bf16[256,2304]{1,0:T(8,128)(2,1)} %collective-permute-done.26), channel_id=1, source_target_pairs={{0,8},{8,16},{16,24},{24,0},{1,9},{9,17},{17,25},{25,1},{2,10},{10... | collective-permute-start | bytes 3538952 | tf_op jit(solution)/shard_map/ppermute | solution.py:132
  444.6 32.5 %collective-permute-start.23 = (bf16[2,4,144,1152]{3,2,0,1:T(8,128)(2,1)S(1)}, bf16[2,4,144,1152]{3,2,0,1:T(8,128)(2,1)S(1)}, u32[]{:S(2)}, u32[]{:S(2)}) collective-permute-start(bf16[2,4,144,1152]{3,2,0,1:T(8,128)(2,1)S(1)} %dynamic-slice_bitcast_fusion.3), channel_id=1, source_target_pairs={{0,2},{2,0},{4,6},{6,4},{1,3},{3,1},{5,7},{7,5},{8,10},{10,8},{12,... | collective-permute-start | bytes 7962632 | tf_op jit(solution)/shard_map/ppermute | solution.py:138
  504.2 33.4 %collective-permute-start.32 = (bf16[256,2304]{1,0:T(8,128)(2,1)S(1)}, bf16[256,2304]{1,0:T(8,128)(2,1)S(1)}, u32[]{:S(2)}, u32[]{:S(2)}) collective-permute-start(bf16[256,2304]{1,0:T(8,128)(2,1)S(1)} %slice.781), channel_id=1, source_target_pairs={{0,2},{2,0},{4,6},{6,4},{1,3},{3,1},{5,7},{7,5},{8,10},{10,8},{12,... | collective-permute-start | bytes 3538952 | tf_op jit(solution)/shard_map/ppermute | solution.py:138
  653.0 67.1 %collective-permute-start.41 = (bf16[256,2304]{1,0:T(8,128)(2,1)S(1)}, bf16[256,2304]{1,0:T(8,128)(2,1)S(1)}, u32[]{:S(2)}, u32[]{:S(2)}) collective-permute-start(bf16[256,2304]{1,0:T(8,128)(2,1)S(1)} %fusion.74), channel_id=1, source_target_pairs={{0,8},{8,16},{16,24},{24,0},{1,9},{9,17},{17,25},{25,1},{2,10},{10... | collective-permute-start | bytes 3538952 | tf_op jit(solution)/shard_map/ppermute | solution.py:132
  728.2 170.2 %reduce-scatter.6.cloned.1.call-start = ((), (), s32[]{:S(2)}) async-start(), calls=%async_computation.13 | async-start | bytes 6635520 | tf_op jit(solution)/shard_map/reduce_scatter | solution.py:476
  830.1 46.9 %all-to-all-start.3 = ((bf16[4,144,1152]{2,1,0:T(8,128)(2,1)}), bf16[4,144,1152]{2,1,0:T(8,128)(2,1)S(1)}, u32[]{:S(2)}, u32[]{:S(2)}) async-start(bf16[4,144,1152]{2,1,0:T(8,128)(2,1)} %reduce-scatter.4.cloned.1.call-done), calls=%async_computation.4 | async-start | bytes 2654208 | tf_op jit(solution)/shard_map/all_to_all | solution.py:236
  833.8 147.0 %reduce-scatter.8.cloned.1.call-start = ((), (), s32[]{:S(2)}) async-start(), calls=%async_computation.14 | async-start | bytes 6635520 | tf_op jit(solution)/shard_map/reduce_scatter | solution.py:476
  834.7 42.3 %collective-permute-start.53 = (bf16[256,2304]{1,0:T(8,128)(2,1)S(1)}, bf16[256,2304]{1,0:T(8,128)(2,1)}, u32[]{:S(2)}, u32[]{:S(2)}) collective-permute-start(bf16[256,2304]{1,0:T(8,128)(2,1)S(1)} %multiply_convert_fusion.3), channel_id=1, source_target_pairs={{0,1},{1,0},{2,3},{3,2},{4,5},{5,4},{6,7},{7,6},{8,9},{9,8},{10,11... | collective-permute-start | bytes 3538952 | tf_op jit(solution)/shard_map/ppermute | solution.py:141
  898.3 56.8 %all-to-all-start.4 = ((bf16[4,144,1152]{2,1,0:T(8,128)(2,1)}), bf16[4,144,1152]{2,1,0:T(8,128)(2,1)}, u32[]{:S(2)}, u32[]{:S(2)}) async-start(bf16[4,144,1152]{2,1,0:T(8,128)(2,1)} %reduce-scatter.6.cloned.1.call-done), calls=%async_computation.6 | async-start | bytes 2654208 | tf_op jit(solution)/shard_map/all_to_all | solution.py:236
  909.2 44.5 %collective-permute-start.61 = (bf16[4,288,512]{2,1,0:T(8,128)(2,1)S(1)}, bf16[4,288,512]{2,1,0:T(8,128)(2,1)S(1)}, u32[]{:S(2)}, u32[]{:S(2)}) collective-permute-start(bf16[4,288,512]{2,1,0:T(8,128)(2,1)S(1)} %dynamic-slice_bitcast_fusion.7), channel_id=1, source_target_pairs={{0,4},{2,6},{4,0},{6,2},{1,5},{3,7},{5,1},{7,3},{8,12},{10,14},{12... | collective-permute-start | bytes 3538952 | tf_op jit(solution)/shard_map/ppermute | solution.py:135
  955.2 31.3 %all-to-all-start.5 = ((bf16[4,288,512]{2,1,0:T(8,128)(2,1)}), bf16[4,288,512]{2,1,0:T(8,128)(2,1)}, u32[]{:S(2)}, u32[]{:S(2)}) async-start(bf16[4,288,512]{2,1,0:T(8,128)(2,1)} %fusion.98), calls=%async_computation.8 | async-start | bytes 2359296 | tf_op jit(solution)/shard_map/all_to_all | solution.py:236
  986.5 35.8 %all-to-all-start.6 = ((bf16[4,144,1152]{2,1,0:T(8,128)(2,1)}), bf16[4,144,1152]{2,1,0:T(8,128)(2,1)}, u32[]{:S(2)}, u32[]{:S(2)}) async-start(bf16[4,144,1152]{2,1,0:T(8,128)(2,1)} %reduce-scatter.8.cloned.1.call-done), calls=%async_computation.9 | async-start | bytes 2654208 | tf_op jit(solution)/shard_map/all_to_all | solution.py:236
  993.4 31.1 %collective-permute-start.62 = (bf16[2,512,512]{2,1,0:T(8,128)(2,1)}, bf16[2,512,512]{2,1,0:T(8,128)(2,1)}, u32[]{:S(2)}, u32[]{:S(2)}) collective-permute-start(bf16[2,512,512]{2,1,0:T(8,128)(2,1)} %pad_maximum_fusion.20), channel_id=1, source_target_pairs={{0,4},{2,6},{4,0},{6,2},{1,5},{3,7},{5,1},{7,3},{8,12},{10,14},{12... | collective-permute-start | bytes 3145736 | tf_op jit(solution)/shard_map/ppermute | solution.py:135
  1030.4 33.1 %collective-permute-start.64 = (bf16[512,512]{1,0:T(8,128)(2,1)S(1)}, bf16[512,512]{1,0:T(8,128)(2,1)S(1)}, u32[]{:S(2)}, u32[]{:S(2)}) collective-permute-start(bf16[512,512]{1,0:T(8,128)(2,1)S(1)} %get-tuple-element.236), channel_id=1, source_target_pairs={{0,16},{8,24},{16,0},{24,8},{1,17},{9,25},{17,1},{25,9},{2,18},{10... | collective-permute-start | bytes 1572872 | tf_op jit(solution)/shard_map/ppermute | solution.py:132
  1031.8 31.6 %collective-permute-start.65 = (bf16[512,512]{1,0:T(8,128)(2,1)S(1)}, bf16[512,512]{1,0:T(8,128)(2,1)S(1)}, u32[]{:S(2)}, u32[]{:S(2)}) collective-permute-start(bf16[512,512]{1,0:T(8,128)(2,1)S(1)} %fusion.188), channel_id=1, source_target_pairs={{0,24},{8,0},{16,8},{24,16},{1,25},{9,1},{17,9},{25,17},{2,26},{10... | collective-permute-start | bytes 1572872 | tf_op jit(solution)/shard_map/ppermute | solution.py:132
  1093.4 53.0 %collective-permute-start.68 = (bf16[256,2304]{1,0:T(8,128)(2,1)}, bf16[256,2304]{1,0:T(8,128)(2,1)}, u32[]{:S(2)}, u32[]{:S(2)}) collective-permute-start(bf16[256,2304]{1,0:T(8,128)(2,1)} %dynamic-slice_convert_fusion), channel_id=1, source_target_pairs={{0,1},{1,0},{2,3},{3,2},{4,5},{5,4},{6,7},{7,6},{8,9},{9,8},{10,11... | collective-permute-start | bytes 3538952 | tf_op jit(solution)/shard_map/ppermute | solution.py:141
  1094.9 46.4 %all-to-all-start.7 = ((bf16[4,288,512]{2,1,0:T(8,128)(2,1)}), bf16[4,288,512]{2,1,0:T(8,128)(2,1)S(1)}, u32[]{:S(2)}, u32[]{:S(2)}) async-start(bf16[4,288,512]{2,1,0:T(8,128)(2,1)} %convert_add_fusion.1), calls=%async_computation.10 | async-start | bytes 2359296 | tf_op jit(solution)/shard_map/all_to_all | solution.py:236
  1141.2 32.2 %all-to-all-start.8 = ((bf16[4,288,512]{2,1,0:T(8,128)(2,1)}), bf16[4,288,512]{2,1,0:T(8,128)(2,1)S(1)}, u32[]{:S(2)}, u32[]{:S(2)}) async-start(bf16[4,288,512]{2,1,0:T(8,128)(2,1)} %fusion.97), calls=%async_computation.11 | async-start | bytes 2359296 | tf_op jit(solution)/shard_map/all_to_all | solution.py:236
  (238 other events, 3073.9 us)
Sparse Core Ops, SparseCore 0:
  130.1 77.9 all-gather.6
  234.5 66.0 all-gather.8
  321.6 74.0 all-gather.10
  728.3 62.4 reduce-scatter.3
  793.6 76.1 reduce-scatter.5
  879.3 79.2 reduce-scatter.7

commit v4 on v3

--- a/solution.py
+++ b/solution.py
@@ -163,7 +163,7 @@
                 if hop:
                     turn = y_next(turn)
                 held = place(held, turn, (z - step) % z_size, (y - hop) % y_size)
-        return held, arrivals, None
+        return held, arrivals, turn
 
     def row_of(values, at):
         return lax.dynamic_slice_in_dim(values, at, 1, 0)[0]
@@ -263,8 +263,8 @@
     gate_low = z_blocks((w_gate.astype(f32) * gain_three).astype(bf16))
     up_low = z_blocks((w_up.astype(f32) * gain_three).astype(bf16))
     down_low = z_blocks(w_down.T)
-    attn_grid, attn_z, _ = gather_grid(attn_own)
-    gate_held = over_z(tie(gate_low, attn_z[-1]))
+    attn_grid, _, attn_y = gather_grid(attn_own)
+    gate_held = over_z(tie(gate_low, attn_y))
     attn_grid = attn_grid.reshape(width, a_cols + q_cols + 128)
     attn_w = attn_grid[:, :a_cols]
     out_w = attn_grid[:, a_cols : a_cols + q_cols]
@@ -318,12 +318,12 @@
     value_rows = projected[:, q_cols + HD :].astype(bf16)
     kv_rows = jnp.concatenate([key_rows, value_rows], axis=1).reshape(2, rows, 2 * HD)
     prompt_kv = kv_rows[:, :prompt_local].reshape(2 * prompt_local, 2 * HD)
-    every_kv, kv_z, kv_y = gather_grid(tie(prompt_kv, up_held))
+    every_kv, kv_z, kv_y = gather_grid(tie(prompt_kv, gate_held))
     every_kv = every_kv.reshape(z_size, y_size * 2 * prompt_local, 2 * HD)
     span = every_kv.shape[1]
-    down_held = over_z(tie(down_low, kv_z[-1]))
+    every_kv = tie(every_kv, up_held)
+    down_held = over_z(tie(down_low, up_held))
     down_every = spread(down_held)
-    every_kv = tie(every_kv, down_held)
     own_kv = lax.dynamic_slice(every_kv, (z, 0, 0), (1, span, 2 * HD))[0]
     key_places = (
         (jnp.arange(y_size, dtype=jnp.int32)[:, None, None] * 2
@@ -381,7 +381,7 @@
     ).astype(bf16)
     post_rows = matmul_rt(pick, attn_grid[:, a_cols + q_cols :])
     post_attn, post_mlp = post_rows[0:1], post_rows[1:2]
-    branch_partial = matmul_rt(attn_out, out_w)
+    branch_partial = matmul_rt(tie(attn_out, down_held), out_w)
     branch_core = branch_partial[:rows] + core_swap(branch_partial[rows:].astype(bf16)).astype(f32)
     branch_give = give_share(branch_core).astype(bf16)
     branch_got = tp_swap(branch_give)

time: 1210 us -> 1180 us (0.975)
  waiting for transfers between devices: 566 us -> 540 us
    ppermute x24, waiting for transfers between devices: 234 us -> 216 us  [z_shift(): lax.ppermute(values, 'fsdp', [(i, (i + step) % z_size) for i in range(z_s...]
    ppermute x14, waiting for transfers between devices: 190 us -> 173 us  [y_next(): lax.ppermute(values, 'ctx', [(i, (i + 2) % c_size) for i in range(c_size)])]
    unnamed x377 -> x369, local copies, waits for them, and re-layouts: 63.6 us -> 63.7 us
  transfers between devices with their start and end apart: 91 -> 91, of which waited for: 46 -> 47; matrix products, arithmetic and copies ran while one was open for 36% -> 38% of each run, Pallas kernels for 0% -> 0%
where the time goes in v4:
time: 1180 us; the launch traced here: 1170 us
  waiting for transfers between devices  540 us (46%)
  matrix products  230 us (19%)
  local copies, waits for them, and re-layouts  154 us (13%)
  other arithmetic  123 us (10%)
  starting transfers between devices  98.2 us (8%)
  between operations  22.7 us (2%)
    ppermute x24, waiting for transfers between devices, z_shift(): lax.ppermute(values, 'fsdp', [(i, (i + step) % z_size) for i in range(z_s...  216 us
    ppermute x14, waiting for transfers between devices, y_next(): lax.ppermute(values, 'ctx', [(i, (i + 2) % c_size) for i in range(c_size)])  173 us
    dot_general x20, matrix products, matmul(): return jnp.dot(left, right, preferred_element_type=f32)  87.6 us
    dot_general x22, matrix products, matmul_rt(): lax.dot_general(left, right, (((1,), (1,)), ((), ())), preferred_element_...  72.7 us
    ppermute x6, waiting for transfers between devices, tp_swap(): return lax.ppermute(values, 'tp', [(0, 1), (1, 0)])  69.7 us
    dot_general x12, matrix products, matmul_lt(): lax.dot_general(left, right, (((0,), (0,)), ((), ())), preferred_element_...  69.5 us
    unnamed x369, local copies, waits for them, and re-layouts  63.7 us
    all_to_all x9, waiting for transfers between devices, over_z(): return lax.all_to_all(values, 'fsdp', 0, 0, tiled=True)  59.1 us
  transfers between devices with their start and end apart: 91, of which 47 were waited for; matrix products, arithmetic and copies ran while one was open for 38% of the time, Pallas kernels for 0%

profile of v4, /device:TPU:0, one launch (start us, length us, event | category | flops | bytes accessed | tf_op | source)
XLA Modules:
  0.0 1167.4 jit_solution(16776054599140489147)
XLA Ops:
  23.4 20.3 %collective-permute-done.2 = bf16[2,144,1664]{2,1,0:T(8,128)(2,1)} collective-permute-done((bf16[2,144,1664]{2,1,0:T(8,128)(2,1)}, bf16[2,144,1664]{2,1,0:T(8,128)(2,1)}, u32[]{:S(2)}, u32[]{:S(2)}) %collective-permute-start.2) | collective-permute-done | bytes 958496 | tf_op jit(solution)/shard_map/ppermute | solution.py:135
  49.7 20.3 %collective-permute-done.4 = bf16[2,144,1664]{2,1,0:T(8,128)(2,1)} collective-permute-done((bf16[2,144,1664]{2,1,0:T(8,128)(2,1)}, bf16[2,144,1664]{2,1,0:T(8,128)(2,1)}, u32[]{:S(2)}, u32[]{:S(2)}) %collective-permute-start.4) | collective-permute-done | bytes 958496 | tf_op jit(solution)/shard_map/ppermute | solution.py:135
  76.2 17.8 %collective-permute-done.6 = bf16[2,144,1664]{2,1,0:T(8,128)(2,1)S(1)} collective-permute-done((bf16[2,144,1664]{2,1,0:T(8,128)(2,1)}, bf16[2,144,1664]{2,1,0:T(8,128)(2,1)S(1)}, u32[]{:S(2)}, u32[]{:S(2)}) %collective-permute-start.6) | collective-permute-done | bytes 958496 | tf_op jit(solution)/shard_map/ppermute | solution.py:135
  100.5 16.7 %collective-permute-done.8 = bf16[2,144,1664]{2,1,0:T(8,128)(2,1)} collective-permute-done((bf16[2,144,1664]{2,1,0:T(8,128)(2,1)}, bf16[2,144,1664]{2,1,0:T(8,128)(2,1)}, u32[]{:S(2)}, u32[]{:S(2)}) %collective-permute-start.8) | collective-permute-done | bytes 958496 | tf_op jit(solution)/shard_map/ppermute | solution.py:135
  128.6 21.3 %all-to-all-done = bf16[4,144,1152]{2,1,0:T(8,128)(2,1)} async-done(((bf16[4,144,1152]{2,1,0:T(8,128)(2,1)}), bf16[4,144,1152]{2,1,0:T(8,128)(2,1)}, u32[]{:S(2)}, u32[]{:S(2)}) %all-to-all-start) | async-done | bytes 1327136 | tf_op jit(solution)/shard_map/all_to_all | solution.py:236
  159.7 8.7 fusion
  181.4 7.1 collective-permute-done.10
  209.8 11.2 collective-permute-done.11
  228.7 8.8 collective-permute-done.13
  268.3 11.2 all-to-all-done.2
  311.0 31.8 %collective-permute-done.18 = bf16[256,2304]{1,0:T(8,128)(2,1)S(1)} collective-permute-done((bf16[256,2304]{1,0:T(8,128)(2,1)S(1)}, bf16[256,2304]{1,0:T(8,128)(2,1)S(1)}, u32[]{:S(2)}, u32[]{:S(2)}) %collective-permute-start.18) | collective-permute-done | bytes 1179680 | tf_op jit(solution)/shard_map/ppermute | solution.py:141
  353.5 21.9 %collective-permute-done.20 = bf16[256,2304]{1,0:T(8,128)(2,1)} collective-permute-done((bf16[256,2304]{1,0:T(8,128)(2,1)S(1)}, bf16[256,2304]{1,0:T(8,128)(2,1)}, u32[]{:S(2)}, u32[]{:S(2)}) %collective-permute-start.20) | collective-permute-done | bytes 1179680 | tf_op jit(solution)/shard_map/ppermute | solution.py:132
  419.3 19.5 %collective-permute-done.30 = bf16[256,2304]{1,0:T(8,128)(2,1)S(1)} collective-permute-done((bf16[256,2304]{1,0:T(8,128)(2,1)}, bf16[256,2304]{1,0:T(8,128)(2,1)S(1)}, u32[]{:S(2)}, u32[]{:S(2)}) %collective-permute-start.30) | collective-permute-done | bytes 1179680 | tf_op jit(solution)/shard_map/ppermute | solution.py:132
  478.5 20.5 %collective-permute-done.25 = bf16[256,2304]{1,0:T(8,128)(2,1)S(1)} collective-permute-done((bf16[256,2304]{1,0:T(8,128)(2,1)}, bf16[256,2304]{1,0:T(8,128)(2,1)S(1)}, u32[]{:S(2)}, u32[]{:S(2)}) %collective-permute-start.25) | collective-permute-done | bytes 1179680 | tf_op jit(solution)/shard_map/ppermute | solution.py:132
  511.3 19.0 %collective-permute-done.29 = bf16[256,2304]{1,0:T(8,128)(2,1)} collective-permute-done((bf16[256,2304]{1,0:T(8,128)(2,1)S(1)}, bf16[256,2304]{1,0:T(8,128)(2,1)}, u32[]{:S(2)}, u32[]{:S(2)}) %collective-permute-start.29) | collective-permute-done | bytes 1179680 | tf_op jit(solution)/shard_map/ppermute | solution.py:132
  532.8 27.7 %collective-permute-done.33 = bf16[256,2304]{1,0:T(8,128)(2,1)S(1)} collective-permute-done((bf16[256,2304]{1,0:T(8,128)(2,1)S(1)}, bf16[256,2304]{1,0:T(8,128)(2,1)S(1)}, u32[]{:S(2)}, u32[]{:S(2)}) %collective-permute-start.33) | collective-permute-done | bytes 1179680 | tf_op jit(solution)/shard_map/ppermute | solution.py:132
  582.2 14.5 %collective-permute-done.37 = bf16[256,2304]{1,0:T(8,128)(2,1)S(1)} collective-permute-done((bf16[256,2304]{1,0:T(8,128)(2,1)S(1)}, bf16[256,2304]{1,0:T(8,128)(2,1)S(1)}, u32[]{:S(2)}, u32[]{:S(2)}) %collective-permute-start.37) | collective-permute-done | bytes 1179680 | tf_op jit(solution)/shard_map/ppermute | solution.py:132
  599.6 7.4 fusion.44
  629.6 27.8 %collective-permute-done.46 = bf16[256,2304]{1,0:T(8,128)(2,1)S(1)} collective-permute-done((bf16[256,2304]{1,0:T(8,128)(2,1)S(1)}, bf16[256,2304]{1,0:T(8,128)(2,1)S(1)}, u32[]{:S(2)}, u32[]{:S(2)}) %collective-permute-start.46) | collective-permute-done | bytes 1179680 | tf_op jit(solution)/shard_map/ppermute | solution.py:132
  657.5 7.8 fusion.51
  674.7 15.0 %convolution_convert_fusion.2 = bf16[2304,1152]{1,0:T(8,128)(2,1)S(1)} fusion(bf16[2048,2304]{1,0:T(8,128)(2,1)} %constant_dynamic-update-slice_fusion.6, bf16[512,1152]{1,0:T(8,128)(2,1)S(1)} %copy-done.153, bf16[512,1152]{1,0:T(8,128)(2,1)S(1)} %copy-done.151, bf16[512,1152]{1,0:T(8,128)(2,1)S(1)} %copy-done.149, bf16[512,1152]{1,0:T(8,128)(2,1)S(1)} %copy-done.161), kind=kOutput, calls=%fused_computation.2 | convolution fusion | flops 10893164544 | bytes 19464192 | tf_op jit(solution)/shard_map/dot_general | solution.py:61
  704.9 9.1 fusion.58
  733.6 15.3 %convolution_convert_fusion.1 = bf16[2304,1152]{1,0:T(8,128)(2,1)S(1)} fusion(bf16[2048,2304]{1,0:T(8,128)(2,1)} %get-tuple-element.81, bf16[512,1152]{1,0:T(8,128)(2,1)S(1)} %get-tuple-element.157, bf16[512,1152]{1,0:T(8,128)(2,1)S(1)} %copy-done.144, bf16[512,1152]{1,0:T(8,128)(2,1)S(1)} %copy-done.142, bf16[512,1152]{1,0:T(8,128)(2,1)S(1)} %copy-done.141), kind=kOutput, calls=%fused_computation.1 | convolution fusion | flops 10893164544 | bytes 19464192 | tf_op jit(solution)/shard_map/dot_general | solution.py:61
  758.0 24.7 %collective-permute-done.50 = bf16[256,2304]{1,0:T(8,128)(2,1)} collective-permute-done((bf16[256,2304]{1,0:T(8,128)(2,1)}, bf16[256,2304]{1,0:T(8,128)(2,1)}, u32[]{:S(2)}, u32[]{:S(2)}) %collective-permute-start.50) | collective-permute-done | bytes 1179680 | tf_op jit(solution)/shard_map/ppermute | solution.py:132
  792.7 15.0 %convolution_convert_fusion = bf16[2304,1152]{1,0:T(8,128)(2,1)S(1)} fusion(bf16[2048,2304]{1,0:T(8,128)(2,1)} %get-tuple-element.81, bf16[512,1152]{1,0:T(8,128)(2,1)S(1)} %copy-done.163, bf16[512,1152]{1,0:T(8,128)(2,1)S(1)} %copy-done.159, bf16[512,1152]{1,0:T(8,128)(2,1)S(1)} %copy-done.157, bf16[512,1152]{1,0:T(8,128)(2,1)S(1)} %copy-done.155), kind=kOutput, calls=%fused_computation | convolution fusion | flops 10893164544 | bytes 19464192 | tf_op jit(solution)/shard_map/dot_general | solution.py:61
  825.2 30.6 %collective-permute-done.53 = bf16[256,2304]{1,0:T(8,128)(2,1)} collective-permute-done((bf16[256,2304]{1,0:T(8,128)(2,1)S(1)}, bf16[256,2304]{1,0:T(8,128)(2,1)}, u32[]{:S(2)}, u32[]{:S(2)}) %collective-permute-start.53) | collective-permute-done | bytes 1179680 | tf_op jit(solution)/shard_map/ppermute | solution.py:141
  900.7 29.8 %collective-permute-done.61 = bf16[4,288,512]{2,1,0:T(8,128)(2,1)S(1)} collective-permute-done((bf16[4,288,512]{2,1,0:T(8,128)(2,1)S(1)}, bf16[4,288,512]{2,1,0:T(8,128)(2,1)S(1)}, u32[]{:S(2)}, u32[]{:S(2)}) %collective-permute-start.61) | collective-permute-done | bytes 1179680 | tf_op jit(solution)/shard_map/ppermute | solution.py:135
  986.3 13.1 %all-to-all-done.6 = bf16[4,144,1152]{2,1,0:T(8,128)(2,1)} async-done(((bf16[4,144,1152]{2,1,0:T(8,128)(2,1)}), bf16[4,144,1152]{2,1,0:T(8,128)(2,1)}, u32[]{:S(2)}, u32[]{:S(2)}) %all-to-all-start.6) | async-done | bytes 1327136 | tf_op jit(solution)/shard_map/all_to_all | solution.py:236
  1009.3 18.5 %collective-permute-done.66 = bf16[4,288,512]{2,1,0:T(8,128)(2,1)S(1)} collective-permute-done((bf16[4,288,512]{2,1,0:T(8,128)(2,1)S(1)}, bf16[4,288,512]{2,1,0:T(8,128)(2,1)S(1)}, u32[]{:S(2)}, u32[]{:S(2)}) %collective-permute-start.66) | collective-permute-done | bytes 1179680 | tf_op jit(solution)/shard_map/ppermute | solution.py:135
  1029.2 11.4 collective-permute-done.64
  1068.2 12.1 %all-to-all-start.7 = ((bf16[4,288,512]{2,1,0:T(8,128)(2,1)}), bf16[4,288,512]{2,1,0:T(8,128)(2,1)S(1)}, u32[]{:S(2)}, u32[]{:S(2)}) async-start(bf16[4,288,512]{2,1,0:T(8,128)(2,1)} %convert_add_fusion.1), calls=%async_computation.10 | async-start | bytes 2359296 | tf_op jit(solution)/shard_map/all_to_all | solution.py:236
  1091.6 21.6 %collective-permute-done.71 = bf16[4,288,512]{2,1,0:T(8,128)(2,1)S(1)} collective-permute-done((bf16[4,288,512]{2,1,0:T(8,128)(2,1)S(1)}, bf16[4,288,512]{2,1,0:T(8,128)(2,1)S(1)}, u32[]{:S(2)}, u32[]{:S(2)}) %collective-permute-start.71) | collective-permute-done | bytes 1179680 | tf_op jit(solution)/shard_map/ppermute | solution.py:135
  (798 shorter events, 587.1 us)
Async XLA Ops:
  23.1 153.3 %collective-permute-start.16 = (s32[1]{0:T(128)}, s32[1]{0:T(128)}, u32[]{:S(2)}, u32[]{:S(2)}) collective-permute-start(s32[1]{0:T(128)} %param.19), channel_id=1, source_target_pairs={{0,2},{2,0},{4,6},{6,4},{1,3},{3,1},{5,7},{7,5},{8,10},{10,8},{12,... | collective-permute-start | bytes 20 | tf_op jit(solution)/shard_map/ppermute | solution.py:138
  117.3 32.7 %all-to-all-start = ((bf16[4,144,1152]{2,1,0:T(8,128)(2,1)}), bf16[4,144,1152]{2,1,0:T(8,128)(2,1)}, u32[]{:S(2)}, u32[]{:S(2)}) async-start(bf16[4,144,1152]{2,1,0:T(8,128)(2,1)} %pad_maximum_fusion.9), calls=%async_computation | async-start | bytes 2654208 | tf_op jit(solution)/shard_map/all_to_all | solution.py:236
  121.6 178.5 %all-gather.7.cloned.1.call-start = ((), (), s32[]{:S(2)}) async-start(), calls=%async_computation.15 | async-start | bytes 6635520 | tf_op jit(solution)/shard_map/all_gather | solution.py:274
  128.6 31.1 %collective-permute-start.1 = (bf16[512,2304]{1,0:T(8,128)(2,1)}, bf16[512,2304]{1,0:T(8,128)(2,1)}, u32[]{:S(2)}, u32[]{:S(2)}) collective-permute-start(bf16[512,2304]{1,0:T(8,128)(2,1)} %get-tuple-element.179), channel_id=1, source_target_pairs={{0,2},{2,0},{4,6},{6,4},{1,3},{3,1},{5,7},{7,5},{8,10},{10,8},{12,... | collective-permute-start | bytes 7077896 | tf_op jit(solution)/shard_map/ppermute | solution.py:138
  198.6 47.0 %all-to-all-start.1 = ((bf16[4,144,1152]{2,1,0:T(8,128)(2,1)}), bf16[4,144,1152]{2,1,0:T(8,128)(2,1)}, u32[]{:S(2)}, u32[]{:S(2)}) async-start(bf16[4,144,1152]{2,1,0:T(8,128)(2,1)} %pad_maximum_fusion.10), calls=%async_computation.1 | async-start | bytes 2654208 | tf_op jit(solution)/shard_map/all_to_all | solution.py:236
  245.6 33.8 %all-to-all-start.2 = ((bf16[4,144,1152]{2,1,0:T(8,128)(2,1)}), bf16[4,144,1152]{2,1,0:T(8,128)(2,1)}, u32[]{:S(2)}, u32[]{:S(2)}) async-start(bf16[4,144,1152]{2,1,0:T(8,128)(2,1)} %pad_maximum_fusion.11), calls=%async_computation.2 | async-start | bytes 2654208 | tf_op jit(solution)/shard_map/all_to_all | solution.py:236
  251.1 96.3 %all-gather.9.cloned.1.call-start = ((), (), s32[]{:S(2)}) async-start(), calls=%async_computation.16 | async-start | bytes 6635520 | tf_op jit(solution)/shard_map/all_gather | solution.py:274
  251.9 140.3 %all-gather.11.cloned.1.call-start = ((), (), s32[]{:S(2)}) async-start(), calls=%async_computation.17 | async-start | bytes 6635520 | tf_op jit(solution)/shard_map/all_gather | solution.py:274
  303.7 507.2 %reduce-scatter.4.cloned.1.call-start = ((), (), s32[]{:S(2)}) async-start(), calls=%async_computation.12 | async-start | bytes 6635520 | tf_op jit(solution)/shard_map/reduce_scatter | solution.py:476
  305.7 37.0 %collective-permute-start.18 = (bf16[256,2304]{1,0:T(8,128)(2,1)S(1)}, bf16[256,2304]{1,0:T(8,128)(2,1)S(1)}, u32[]{:S(2)}, u32[]{:S(2)}) collective-permute-start(bf16[256,2304]{1,0:T(8,128)(2,1)S(1)} %dynamic-slice_convert_fusion.1), channel_id=1, source_target_pairs={{0,1},{1,0},{2,3},{3,2},{4,5},{5,4},{6,7},{7,6},{8,9},{9,8},{10,11... | collective-permute-start | bytes 3538952 | tf_op jit(solution)/shard_map/ppermute | solution.py:141
  352.1 45.0 %collective-permute-start.22 = (bf16[2,4,144,1152]{3,2,0,1:T(8,128)(2,1)}, bf16[2,4,144,1152]{3,2,0,1:T(8,128)(2,1)}, u32[]{:S(2)}, u32[]{:S(2)}) collective-permute-start(bf16[2,4,144,1152]{3,2,0,1:T(8,128)(2,1)} %bitcast.459), channel_id=1, source_target_pairs={{0,2},{2,0},{4,6},{6,4},{1,3},{3,1},{5,7},{7,5},{8,10},{10,8},{12,... | collective-permute-start | bytes 7962632 | tf_op jit(solution)/shard_map/ppermute | solution.py:138
  375.4 32.5 %collective-permute-start.26 = (bf16[256,2304]{1,0:T(8,128)(2,1)}, bf16[256,2304]{1,0:T(8,128)(2,1)}, u32[]{:S(2)}, u32[]{:S(2)}) collective-permute-start(bf16[256,2304]{1,0:T(8,128)(2,1)} %collective-permute-done.20), channel_id=1, source_target_pairs={{0,8},{8,16},{16,24},{24,0},{1,9},{9,17},{17,25},{25,1},{2,10},{10... | collective-permute-start | bytes 3538952 | tf_op jit(solution)/shard_map/ppermute | solution.py:132
  394.2 55.8 %collective-permute-start.23 = (bf16[2,4,144,1152]{3,2,0,1:T(8,128)(2,1)S(1)}, bf16[2,4,144,1152]{3,2,0,1:T(8,128)(2,1)S(1)}, u32[]{:S(2)}, u32[]{:S(2)}) collective-permute-start(bf16[2,4,144,1152]{3,2,0,1:T(8,128)(2,1)S(1)} %dynamic-slice_bitcast_fusion.3), channel_id=1, source_target_pairs={{0,2},{2,0},{4,6},{6,4},{1,3},{3,1},{5,7},{7,5},{8,10},{10,8},{12,... | collective-permute-start | bytes 7962632 | tf_op jit(solution)/shard_map/ppermute | solution.py:138
  407.9 30.9 %collective-permute-start.27 = (bf16[256,2304]{1,0:T(8,128)(2,1)}, bf16[256,2304]{1,0:T(8,128)(2,1)S(1)}, u32[]{:S(2)}, u32[]{:S(2)}) collective-permute-start(bf16[256,2304]{1,0:T(8,128)(2,1)} %collective-permute-done.26), channel_id=1, source_target_pairs={{0,2},{2,0},{4,6},{6,4},{1,3},{3,1},{5,7},{7,5},{8,10},{10,8},{12,... | collective-permute-start | bytes 3538952 | tf_op jit(solution)/shard_map/ppermute | solution.py:138
  408.0 30.8 %collective-permute-start.30 = (bf16[256,2304]{1,0:T(8,128)(2,1)}, bf16[256,2304]{1,0:T(8,128)(2,1)S(1)}, u32[]{:S(2)}, u32[]{:S(2)}) collective-permute-start(bf16[256,2304]{1,0:T(8,128)(2,1)} %collective-permute-done.26), channel_id=1, source_target_pairs={{0,8},{8,16},{16,24},{24,0},{1,9},{9,17},{17,25},{25,1},{2,10},{10... | collective-permute-start | bytes 3538952 | tf_op jit(solution)/shard_map/ppermute | solution.py:132
  477.9 33.4 %collective-permute-start.32 = (bf16[256,2304]{1,0:T(8,128)(2,1)S(1)}, bf16[256,2304]{1,0:T(8,128)(2,1)S(1)}, u32[]{:S(2)}, u32[]{:S(2)}) collective-permute-start(bf16[256,2304]{1,0:T(8,128)(2,1)S(1)} %slice.781), channel_id=1, source_target_pairs={{0,2},{2,0},{4,6},{6,4},{1,3},{3,1},{5,7},{7,5},{8,10},{10,8},{12,... | collective-permute-start | bytes 3538952 | tf_op jit(solution)/shard_map/ppermute | solution.py:138
  626.9 30.6 %collective-permute-start.43 = (bf16[256,2304]{1,0:T(8,128)(2,1)S(1)}, bf16[256,2304]{1,0:T(8,128)(2,1)S(1)}, u32[]{:S(2)}, u32[]{:S(2)}) collective-permute-start(bf16[256,2304]{1,0:T(8,128)(2,1)S(1)} %collective-permute-done.42), channel_id=1, source_target_pairs={{0,2},{2,0},{4,6},{6,4},{1,3},{3,1},{5,7},{7,5},{8,10},{10,8},{12,... | collective-permute-start | bytes 3538952 | tf_op jit(solution)/shard_map/ppermute | solution.py:138
  629.4 67.1 %collective-permute-start.41 = (bf16[256,2304]{1,0:T(8,128)(2,1)S(1)}, bf16[256,2304]{1,0:T(8,128)(2,1)S(1)}, u32[]{:S(2)}, u32[]{:S(2)}) collective-permute-start(bf16[256,2304]{1,0:T(8,128)(2,1)S(1)} %fusion.74), channel_id=1, source_target_pairs={{0,8},{8,16},{16,24},{24,0},{1,9},{9,17},{17,25},{25,1},{2,10},{10... | collective-permute-start | bytes 3538952 | tf_op jit(solution)/shard_map/ppermute | solution.py:132
  704.6 171.8 %reduce-scatter.6.cloned.1.call-start = ((), (), s32[]{:S(2)}) async-start(), calls=%async_computation.13 | async-start | bytes 6635520 | tf_op jit(solution)/shard_map/reduce_scatter | solution.py:476
  810.9 44.9 %all-to-all-start.3 = ((bf16[4,144,1152]{2,1,0:T(8,128)(2,1)}), bf16[4,144,1152]{2,1,0:T(8,128)(2,1)S(1)}, u32[]{:S(2)}, u32[]{:S(2)}) async-start(bf16[4,144,1152]{2,1,0:T(8,128)(2,1)} %reduce-scatter.4.cloned.1.call-done), calls=%async_computation.4 | async-start | bytes 2654208 | tf_op jit(solution)/shard_map/all_to_all | solution.py:236
  814.6 142.5 %reduce-scatter.8.cloned.1.call-start = ((), (), s32[]{:S(2)}) async-start(), calls=%async_computation.14 | async-start | bytes 6635520 | tf_op jit(solution)/shard_map/reduce_scatter | solution.py:476
  816.9 38.9 %collective-permute-start.53 = (bf16[256,2304]{1,0:T(8,128)(2,1)S(1)}, bf16[256,2304]{1,0:T(8,128)(2,1)}, u32[]{:S(2)}, u32[]{:S(2)}) collective-permute-start(bf16[256,2304]{1,0:T(8,128)(2,1)S(1)} %multiply_convert_fusion.3), channel_id=1, source_target_pairs={{0,1},{1,0},{2,3},{3,2},{4,5},{5,4},{6,7},{7,6},{8,9},{9,8},{10,11... | collective-permute-start | bytes 3538952 | tf_op jit(solution)/shard_map/ppermute | solution.py:141
  876.5 55.4 %all-to-all-start.4 = ((bf16[4,144,1152]{2,1,0:T(8,128)(2,1)}), bf16[4,144,1152]{2,1,0:T(8,128)(2,1)}, u32[]{:S(2)}, u32[]{:S(2)}) async-start(bf16[4,144,1152]{2,1,0:T(8,128)(2,1)} %reduce-scatter.6.cloned.1.call-done), calls=%async_computation.6 | async-start | bytes 2654208 | tf_op jit(solution)/shard_map/all_to_all | solution.py:236
  887.2 43.2 %collective-permute-start.61 = (bf16[4,288,512]{2,1,0:T(8,128)(2,1)S(1)}, bf16[4,288,512]{2,1,0:T(8,128)(2,1)S(1)}, u32[]{:S(2)}, u32[]{:S(2)}) collective-permute-start(bf16[4,288,512]{2,1,0:T(8,128)(2,1)S(1)} %dynamic-slice_bitcast_fusion.7), channel_id=1, source_target_pairs={{0,4},{2,6},{4,0},{6,2},{1,5},{3,7},{5,1},{7,3},{8,12},{10,14},{12... | collective-permute-start | bytes 3538952 | tf_op jit(solution)/shard_map/ppermute | solution.py:135
  931.9 31.6 %all-to-all-start.5 = ((bf16[4,288,512]{2,1,0:T(8,128)(2,1)}), bf16[4,288,512]{2,1,0:T(8,128)(2,1)}, u32[]{:S(2)}, u32[]{:S(2)}) async-start(bf16[4,288,512]{2,1,0:T(8,128)(2,1)} %fusion.98), calls=%async_computation.8 | async-start | bytes 2359296 | tf_op jit(solution)/shard_map/all_to_all | solution.py:236
  963.4 36.0 %all-to-all-start.6 = ((bf16[4,144,1152]{2,1,0:T(8,128)(2,1)}), bf16[4,144,1152]{2,1,0:T(8,128)(2,1)}, u32[]{:S(2)}, u32[]{:S(2)}) async-start(bf16[4,144,1152]{2,1,0:T(8,128)(2,1)} %reduce-scatter.8.cloned.1.call-done), calls=%async_computation.9 | async-start | bytes 2654208 | tf_op jit(solution)/shard_map/all_to_all | solution.py:236
  970.6 31.0 %collective-permute-start.62 = (bf16[2,512,512]{2,1,0:T(8,128)(2,1)}, bf16[2,512,512]{2,1,0:T(8,128)(2,1)}, u32[]{:S(2)}, u32[]{:S(2)}) collective-permute-start(bf16[2,512,512]{2,1,0:T(8,128)(2,1)} %pad_maximum_fusion.20), channel_id=1, source_target_pairs={{0,4},{2,6},{4,0},{6,2},{1,5},{3,7},{5,1},{7,3},{8,12},{10,14},{12... | collective-permute-start | bytes 3145736 | tf_op jit(solution)/shard_map/ppermute | solution.py:135
  1006.3 34.3 %collective-permute-start.64 = (bf16[512,512]{1,0:T(8,128)(2,1)S(1)}, bf16[512,512]{1,0:T(8,128)(2,1)S(1)}, u32[]{:S(2)}, u32[]{:S(2)}) collective-permute-start(bf16[512,512]{1,0:T(8,128)(2,1)S(1)} %get-tuple-element.238), channel_id=1, source_target_pairs={{0,16},{8,24},{16,0},{24,8},{1,17},{9,25},{17,1},{25,9},{2,18},{10... | collective-permute-start | bytes 1572872 | tf_op jit(solution)/shard_map/ppermute | solution.py:132
  1007.7 32.9 %collective-permute-start.65 = (bf16[512,512]{1,0:T(8,128)(2,1)S(1)}, bf16[512,512]{1,0:T(8,128)(2,1)S(1)}, u32[]{:S(2)}, u32[]{:S(2)}) collective-permute-start(bf16[512,512]{1,0:T(8,128)(2,1)S(1)} %fusion.188), channel_id=1, source_target_pairs={{0,24},{8,0},{16,8},{24,16},{1,25},{9,1},{17,9},{25,17},{2,26},{10... | collective-permute-start | bytes 1572872 | tf_op jit(solution)/shard_map/ppermute | solution.py:132
  1067.0 52.6 %collective-permute-start.68 = (bf16[256,2304]{1,0:T(8,128)(2,1)}, bf16[256,2304]{1,0:T(8,128)(2,1)}, u32[]{:S(2)}, u32[]{:S(2)}) collective-permute-start(bf16[256,2304]{1,0:T(8,128)(2,1)} %dynamic-slice_convert_fusion), channel_id=1, source_target_pairs={{0,1},{1,0},{2,3},{3,2},{4,5},{5,4},{6,7},{7,6},{8,9},{9,8},{10,11... | collective-permute-start | bytes 3538952 | tf_op jit(solution)/shard_map/ppermute | solution.py:141
  1068.2 46.4 %all-to-all-start.7 = ((bf16[4,288,512]{2,1,0:T(8,128)(2,1)}), bf16[4,288,512]{2,1,0:T(8,128)(2,1)S(1)}, u32[]{:S(2)}, u32[]{:S(2)}) async-start(bf16[4,288,512]{2,1,0:T(8,128)(2,1)} %convert_add_fusion.1), calls=%async_computation.10 | async-start | bytes 2359296 | tf_op jit(solution)/shard_map/all_to_all | solution.py:236
  1114.6 32.1 %all-to-all-start.8 = ((bf16[4,288,512]{2,1,0:T(8,128)(2,1)}), bf16[4,288,512]{2,1,0:T(8,128)(2,1)S(1)}, u32[]{:S(2)}, u32[]{:S(2)}) async-start(bf16[4,288,512]{2,1,0:T(8,128)(2,1)} %fusion.97), calls=%async_computation.11 | async-start | bytes 2359296 | tf_op jit(solution)/shard_map/all_to_all | solution.py:236
  (234 other events, 3412.1 us)
Sparse Core Ops, SparseCore 0:
  150.1 83.2 all-gather.6
  253.8 70.3 all-gather.8
  326.0 66.1 all-gather.10
  704.7 62.4 reduce-scatter.3
  770.1 72.5 reduce-scatter.5
  858.1 78.2 reduce-scatter.7

commit v5 on v4

--- a/solution.py
+++ b/solution.py
@@ -493,7 +493,7 @@
     grad_gate_w = matmul_lt(tie(all_in, lows[2]), joined(grad_gates)).astype(bf16)
     gate_terms = reduce_terms(grad_gate_w)
     gate_sum = reduce(gate_terms)
-    grad_three = tie(grad_three, gate_terms)
+    grad_three = tie(grad_three, grad_gate_w)
 
     grad_middle = grad_result + norm_back(grad_three, normal_three, inverse_three)
     grad_post_attn = jnp.sum(grad_middle * normal_two, axis=0)
@@ -502,7 +502,7 @@
     up_terms = reduce_terms(grad_up_w)
     up_sum = reduce(up_terms)
     down_got = over_z(tie(down_sum, grad_branch))
-    branch_rows = rows_of(grad_branch, tie(tp_swap(grad_branch), up_terms, down_got))
+    branch_rows = rows_of(grad_branch, tie(tp_swap(grad_branch), grad_up_w, down_got))
     post_terms = jnp.stack([grad_post_attn, grad_post_mlp], axis=0)
     post_terms = post_terms.reshape(2, z_size, y_size, 2, part).transpose(1, 2, 3, 0, 4)
     post_y = scatter_y(post_terms)

time: 1180 us -> 1190 us (level)
    unnamed x369 -> x367, local copies, waits for them, and re-layouts: 63.7 us -> 66.1 us
  transfers between devices with their start and end apart: 91 -> 91, of which waited for: 47 -> 46; matrix products, arithmetic and copies ran while one was open for 38% -> 38% of each run, Pallas kernels for 0% -> 0%
where the time goes in v5:
time: 1190 us; the launch traced here: 1180 us
  waiting for transfers between devices  539 us (45%)
  matrix products  230 us (19%)
  local copies, waits for them, and re-layouts  156 us (13%)
  other arithmetic  127 us (11%)
  starting transfers between devices  100 us (8%)
  between operations  23.6 us (2%)
    ppermute x24, waiting for transfers between devices, z_shift(): lax.ppermute(values, 'fsdp', [(i, (i + step) % z_size) for i in range(z_s...  215 us
    ppermute x14, waiting for transfers between devices, y_next(): lax.ppermute(values, 'ctx', [(i, (i + 2) % c_size) for i in range(c_size)])  176 us
    dot_general x20, matrix products, matmul(): return jnp.dot(left, right, preferred_element_type=f32)  87.6 us
    dot_general x22, matrix products, matmul_rt(): lax.dot_general(left, right, (((1,), (1,)), ((), ())), preferred_element_...  72.7 us
    dot_general x12, matrix products, matmul_lt(): lax.dot_general(left, right, (((0,), (0,)), ((), ())), preferred_element_...  69.3 us
    ppermute x6, waiting for transfers between devices, tp_swap(): return lax.ppermute(values, 'tp', [(0, 1), (1, 0)])  68.2 us
    unnamed x367, local copies, waits for them, and re-layouts  66.1 us
    all_to_all x9, waiting for transfers between devices, over_z(): return lax.all_to_all(values, 'fsdp', 0, 0, tiled=True)  58.3 us
  transfers between devices with their start and end apart: 91, of which 46 were waited for; matrix products, arithmetic and copies ran while one was open for 38% of the time, Pallas kernels for 0%

profile of v5, /device:TPU:0, one launch (start us, length us, event | category | flops | bytes accessed | tf_op | source)
XLA Modules:
  0.0 1175.1 jit_solution(870305144887885352)
XLA Ops:
  23.4 20.3 %collective-permute-done.2 = bf16[2,144,1664]{2,1,0:T(8,128)(2,1)} collective-permute-done((bf16[2,144,1664]{2,1,0:T(8,128)(2,1)}, bf16[2,144,1664]{2,1,0:T(8,128)(2,1)}, u32[]{:S(2)}, u32[]{:S(2)}) %collective-permute-start.2) | collective-permute-done | bytes 958496 | tf_op jit(solution)/shard_map/ppermute | solution.py:135
  49.7 20.3 %collective-permute-done.4 = bf16[2,144,1664]{2,1,0:T(8,128)(2,1)} collective-permute-done((bf16[2,144,1664]{2,1,0:T(8,128)(2,1)}, bf16[2,144,1664]{2,1,0:T(8,128)(2,1)}, u32[]{:S(2)}, u32[]{:S(2)}) %collective-permute-start.4) | collective-permute-done | bytes 958496 | tf_op jit(solution)/shard_map/ppermute | solution.py:135
  76.2 17.8 %collective-permute-done.6 = bf16[2,144,1664]{2,1,0:T(8,128)(2,1)S(1)} collective-permute-done((bf16[2,144,1664]{2,1,0:T(8,128)(2,1)}, bf16[2,144,1664]{2,1,0:T(8,128)(2,1)S(1)}, u32[]{:S(2)}, u32[]{:S(2)}) %collective-permute-start.6) | collective-permute-done | bytes 958496 | tf_op jit(solution)/shard_map/ppermute | solution.py:135
  100.5 16.7 %collective-permute-done.8 = bf16[2,144,1664]{2,1,0:T(8,128)(2,1)} collective-permute-done((bf16[2,144,1664]{2,1,0:T(8,128)(2,1)}, bf16[2,144,1664]{2,1,0:T(8,128)(2,1)}, u32[]{:S(2)}, u32[]{:S(2)}) %collective-permute-start.8) | collective-permute-done | bytes 958496 | tf_op jit(solution)/shard_map/ppermute | solution.py:135
  128.5 21.4 %all-to-all-done = bf16[4,144,1152]{2,1,0:T(8,128)(2,1)} async-done(((bf16[4,144,1152]{2,1,0:T(8,128)(2,1)}), bf16[4,144,1152]{2,1,0:T(8,128)(2,1)}, u32[]{:S(2)}, u32[]{:S(2)}) %all-to-all-start) | async-done | bytes 1327136 | tf_op jit(solution)/shard_map/all_to_all | solution.py:236
  159.7 8.7 fusion
  209.8 11.2 collective-permute-done.11
  228.7 8.8 collective-permute-done.13
  268.3 11.2 all-to-all-done.2
  311.1 31.8 %collective-permute-done.18 = bf16[256,2304]{1,0:T(8,128)(2,1)S(1)} collective-permute-done((bf16[256,2304]{1,0:T(8,128)(2,1)S(1)}, bf16[256,2304]{1,0:T(8,128)(2,1)S(1)}, u32[]{:S(2)}, u32[]{:S(2)}) %collective-permute-start.18) | collective-permute-done | bytes 1179680 | tf_op jit(solution)/shard_map/ppermute | solution.py:141
  353.6 21.9 %collective-permute-done.20 = bf16[256,2304]{1,0:T(8,128)(2,1)} collective-permute-done((bf16[256,2304]{1,0:T(8,128)(2,1)S(1)}, bf16[256,2304]{1,0:T(8,128)(2,1)}, u32[]{:S(2)}, u32[]{:S(2)}) %collective-permute-start.20) | collective-permute-done | bytes 1179680 | tf_op jit(solution)/shard_map/ppermute | solution.py:132
  410.0 6.9 multiply_convert_fusion.13
  419.3 19.5 %collective-permute-done.30 = bf16[256,2304]{1,0:T(8,128)(2,1)S(1)} collective-permute-done((bf16[256,2304]{1,0:T(8,128)(2,1)}, bf16[256,2304]{1,0:T(8,128)(2,1)S(1)}, u32[]{:S(2)}, u32[]{:S(2)}) %collective-permute-start.30) | collective-permute-done | bytes 1179680 | tf_op jit(solution)/shard_map/ppermute | solution.py:132
  478.5 20.5 %collective-permute-done.25 = bf16[256,2304]{1,0:T(8,128)(2,1)S(1)} collective-permute-done((bf16[256,2304]{1,0:T(8,128)(2,1)}, bf16[256,2304]{1,0:T(8,128)(2,1)S(1)}, u32[]{:S(2)}, u32[]{:S(2)}) %collective-permute-start.25) | collective-permute-done | bytes 1179680 | tf_op jit(solution)/shard_map/ppermute | solution.py:132
  511.4 18.9 %collective-permute-done.29 = bf16[256,2304]{1,0:T(8,128)(2,1)} collective-permute-done((bf16[256,2304]{1,0:T(8,128)(2,1)S(1)}, bf16[256,2304]{1,0:T(8,128)(2,1)}, u32[]{:S(2)}, u32[]{:S(2)}) %collective-permute-start.29) | collective-permute-done | bytes 1179680 | tf_op jit(solution)/shard_map/ppermute | solution.py:132
  532.9 27.7 %collective-permute-done.33 = bf16[256,2304]{1,0:T(8,128)(2,1)S(1)} collective-permute-done((bf16[256,2304]{1,0:T(8,128)(2,1)S(1)}, bf16[256,2304]{1,0:T(8,128)(2,1)S(1)}, u32[]{:S(2)}, u32[]{:S(2)}) %collective-permute-start.33) | collective-permute-done | bytes 1179680 | tf_op jit(solution)/shard_map/ppermute | solution.py:132
  582.2 14.5 %collective-permute-done.37 = bf16[256,2304]{1,0:T(8,128)(2,1)S(1)} collective-permute-done((bf16[256,2304]{1,0:T(8,128)(2,1)S(1)}, bf16[256,2304]{1,0:T(8,128)(2,1)S(1)}, u32[]{:S(2)}, u32[]{:S(2)}) %collective-permute-start.37) | collective-permute-done | bytes 1179680 | tf_op jit(solution)/shard_map/ppermute | solution.py:132
  599.6 7.4 fusion.44
  629.7 27.8 %collective-permute-done.46 = bf16[256,2304]{1,0:T(8,128)(2,1)S(1)} collective-permute-done((bf16[256,2304]{1,0:T(8,128)(2,1)S(1)}, bf16[256,2304]{1,0:T(8,128)(2,1)S(1)}, u32[]{:S(2)}, u32[]{:S(2)}) %collective-permute-start.46) | collective-permute-done | bytes 1179680 | tf_op jit(solution)/shard_map/ppermute | solution.py:132
  657.5 7.8 fusion.51
  674.8 15.0 %convolution_convert_fusion.2 = bf16[2304,1152]{1,0:T(8,128)(2,1)S(1)} fusion(bf16[2048,2304]{1,0:T(8,128)(2,1)} %constant_dynamic-update-slice_fusion.6, bf16[512,1152]{1,0:T(8,128)(2,1)S(1)} %copy-done.152, bf16[512,1152]{1,0:T(8,128)(2,1)S(1)} %copy-done.150, bf16[512,1152]{1,0:T(8,128)(2,1)S(1)} %copy-done.148, bf16[512,1152]{1,0:T(8,128)(2,1)S(1)} %copy-done.160), kind=kOutput, calls=%fused_computation.2 | convolution fusion | flops 10893164544 | bytes 19464192 | tf_op jit(solution)/shard_map/dot_general | solution.py:61
  705.0 9.1 fusion.58
  733.6 15.3 %convolution_convert_fusion.1 = bf16[2304,1152]{1,0:T(8,128)(2,1)S(1)} fusion(bf16[2048,2304]{1,0:T(8,128)(2,1)} %get-tuple-element.81, bf16[512,1152]{1,0:T(8,128)(2,1)S(1)} %get-tuple-element.157, bf16[512,1152]{1,0:T(8,128)(2,1)S(1)} %copy-done.143, bf16[512,1152]{1,0:T(8,128)(2,1)S(1)} %copy-done.141, bf16[512,1152]{1,0:T(8,128)(2,1)S(1)} %copy-done.140), kind=kOutput, calls=%fused_computation.1 | convolution fusion | flops 10893164544 | bytes 19464192 | tf_op jit(solution)/shard_map/dot_general | solution.py:61
  758.0 24.7 %collective-permute-done.50 = bf16[256,2304]{1,0:T(8,128)(2,1)} collective-permute-done((bf16[256,2304]{1,0:T(8,128)(2,1)}, bf16[256,2304]{1,0:T(8,128)(2,1)}, u32[]{:S(2)}, u32[]{:S(2)}) %collective-permute-start.50) | collective-permute-done | bytes 1179680 | tf_op jit(solution)/shard_map/ppermute | solution.py:132
  793.1 15.1 %convolution_convert_fusion = bf16[2304,1152]{1,0:T(8,128)(2,1)S(1)} fusion(bf16[2048,2304]{1,0:T(8,128)(2,1)} %get-tuple-element.81, bf16[512,1152]{1,0:T(8,128)(2,1)S(1)} %copy-done.162, bf16[512,1152]{1,0:T(8,128)(2,1)S(1)} %copy-done.158, bf16[512,1152]{1,0:T(8,128)(2,1)S(1)} %copy-done.156, bf16[512,1152]{1,0:T(8,128)(2,1)S(1)} %copy-done.154), kind=kOutput, calls=%fused_computation | convolution fusion | flops 10893164544 | bytes 19464192 | tf_op jit(solution)/shard_map/dot_general | solution.py:61
  826.0 29.9 %collective-permute-done.52 = bf16[256,2304]{1,0:T(8,128)(2,1)} collective-permute-done((bf16[256,2304]{1,0:T(8,128)(2,1)}, bf16[256,2304]{1,0:T(8,128)(2,1)}, u32[]{:S(2)}, u32[]{:S(2)}) %collective-permute-start.52) | collective-permute-done | bytes 1179680 | tf_op jit(solution)/shard_map/ppermute | solution.py:141
  908.1 29.9 %collective-permute-done.61 = bf16[4,288,512]{2,1,0:T(8,128)(2,1)S(1)} collective-permute-done((bf16[4,288,512]{2,1,0:T(8,128)(2,1)S(1)}, bf16[4,288,512]{2,1,0:T(8,128)(2,1)S(1)}, u32[]{:S(2)}, u32[]{:S(2)}) %collective-permute-start.61) | collective-permute-done | bytes 1179680 | tf_op jit(solution)/shard_map/ppermute | solution.py:135
  993.5 13.5 %all-to-all-done.6 = bf16[4,144,1152]{2,1,0:T(8,128)(2,1)} async-done(((bf16[4,144,1152]{2,1,0:T(8,128)(2,1)}), bf16[4,144,1152]{2,1,0:T(8,128)(2,1)}, u32[]{:S(2)}, u32[]{:S(2)}) %all-to-all-start.6) | async-done | bytes 1327136 | tf_op jit(solution)/shard_map/all_to_all | solution.py:236
  1016.8 18.6 %collective-permute-done.66 = bf16[4,288,512]{2,1,0:T(8,128)(2,1)S(1)} collective-permute-done((bf16[4,288,512]{2,1,0:T(8,128)(2,1)S(1)}, bf16[4,288,512]{2,1,0:T(8,128)(2,1)S(1)}, u32[]{:S(2)}, u32[]{:S(2)}) %collective-permute-start.66) | collective-permute-done | bytes 1179680 | tf_op jit(solution)/shard_map/ppermute | solution.py:135
  1036.7 11.0 collective-permute-done.64
  1075.8 12.1 %all-to-all-start.7 = ((bf16[4,288,512]{2,1,0:T(8,128)(2,1)}), bf16[4,288,512]{2,1,0:T(8,128)(2,1)S(1)}, u32[]{:S(2)}, u32[]{:S(2)}) async-start(bf16[4,288,512]{2,1,0:T(8,128)(2,1)} %convert_add_fusion.1), calls=%async_computation.10 | async-start | bytes 2359296 | tf_op jit(solution)/shard_map/all_to_all | solution.py:236
  1098.7 22.1 %collective-permute-done.71 = bf16[4,288,512]{2,1,0:T(8,128)(2,1)S(1)} collective-permute-done((bf16[4,288,512]{2,1,0:T(8,128)(2,1)S(1)}, bf16[4,288,512]{2,1,0:T(8,128)(2,1)S(1)}, u32[]{:S(2)}, u32[]{:S(2)}) %collective-permute-start.71) | collective-permute-done | bytes 1179680 | tf_op jit(solution)/shard_map/ppermute | solution.py:135
  (796 shorter events, 594.0 us)
Async XLA Ops:
  23.1 153.3 %collective-permute-start.16 = (s32[1]{0:T(128)}, s32[1]{0:T(128)}, u32[]{:S(2)}, u32[]{:S(2)}) collective-permute-start(s32[1]{0:T(128)} %param.19), channel_id=1, source_target_pairs={{0,2},{2,0},{4,6},{6,4},{1,3},{3,1},{5,7},{7,5},{8,10},{10,8},{12,... | collective-permute-start | bytes 20 | tf_op jit(solution)/shard_map/ppermute | solution.py:138
  117.3 32.7 %all-to-all-start = ((bf16[4,144,1152]{2,1,0:T(8,128)(2,1)}), bf16[4,144,1152]{2,1,0:T(8,128)(2,1)}, u32[]{:S(2)}, u32[]{:S(2)}) async-start(bf16[4,144,1152]{2,1,0:T(8,128)(2,1)} %pad_maximum_fusion.9), calls=%async_computation | async-start | bytes 2654208 | tf_op jit(solution)/shard_map/all_to_all | solution.py:236
  121.6 178.6 %all-gather.7.cloned.1.call-start = ((), (), s32[]{:S(2)}) async-start(), calls=%async_computation.15 | async-start | bytes 6635520 | tf_op jit(solution)/shard_map/all_gather | solution.py:274
  128.5 31.1 %collective-permute-start.1 = (bf16[512,2304]{1,0:T(8,128)(2,1)}, bf16[512,2304]{1,0:T(8,128)(2,1)}, u32[]{:S(2)}, u32[]{:S(2)}) collective-permute-start(bf16[512,2304]{1,0:T(8,128)(2,1)} %get-tuple-element.179), channel_id=1, source_target_pairs={{0,2},{2,0},{4,6},{6,4},{1,3},{3,1},{5,7},{7,5},{8,10},{10,8},{12,... | collective-permute-start | bytes 7077896 | tf_op jit(solution)/shard_map/ppermute | solution.py:138
  198.6 47.1 %all-to-all-start.1 = ((bf16[4,144,1152]{2,1,0:T(8,128)(2,1)}), bf16[4,144,1152]{2,1,0:T(8,128)(2,1)}, u32[]{:S(2)}, u32[]{:S(2)}) async-start(bf16[4,144,1152]{2,1,0:T(8,128)(2,1)} %pad_maximum_fusion.10), calls=%async_computation.1 | async-start | bytes 2654208 | tf_op jit(solution)/shard_map/all_to_all | solution.py:236
  245.6 33.9 %all-to-all-start.2 = ((bf16[4,144,1152]{2,1,0:T(8,128)(2,1)}), bf16[4,144,1152]{2,1,0:T(8,128)(2,1)}, u32[]{:S(2)}, u32[]{:S(2)}) async-start(bf16[4,144,1152]{2,1,0:T(8,128)(2,1)} %pad_maximum_fusion.11), calls=%async_computation.2 | async-start | bytes 2654208 | tf_op jit(solution)/shard_map/all_to_all | solution.py:236
  251.2 96.4 %all-gather.9.cloned.1.call-start = ((), (), s32[]{:S(2)}) async-start(), calls=%async_computation.16 | async-start | bytes 6635520 | tf_op jit(solution)/shard_map/all_gather | solution.py:274
  251.9 140.3 %all-gather.11.cloned.1.call-start = ((), (), s32[]{:S(2)}) async-start(), calls=%async_computation.17 | async-start | bytes 6635520 | tf_op jit(solution)/shard_map/all_gather | solution.py:274
  303.8 506.8 %reduce-scatter.4.cloned.1.call-start = ((), (), s32[]{:S(2)}) async-start(), calls=%async_computation.12 | async-start | bytes 6635520 | tf_op jit(solution)/shard_map/reduce_scatter | solution.py:476
  305.8 37.0 %collective-permute-start.18 = (bf16[256,2304]{1,0:T(8,128)(2,1)S(1)}, bf16[256,2304]{1,0:T(8,128)(2,1)S(1)}, u32[]{:S(2)}, u32[]{:S(2)}) collective-permute-start(bf16[256,2304]{1,0:T(8,128)(2,1)S(1)} %dynamic-slice_convert_fusion.1), channel_id=1, source_target_pairs={{0,1},{1,0},{2,3},{3,2},{4,5},{5,4},{6,7},{7,6},{8,9},{9,8},{10,11... | collective-permute-start | bytes 3538952 | tf_op jit(solution)/shard_map/ppermute | solution.py:141
  352.2 45.0 %collective-permute-start.22 = (bf16[2,4,144,1152]{3,2,0,1:T(8,128)(2,1)}, bf16[2,4,144,1152]{3,2,0,1:T(8,128)(2,1)}, u32[]{:S(2)}, u32[]{:S(2)}) collective-permute-start(bf16[2,4,144,1152]{3,2,0,1:T(8,128)(2,1)} %bitcast.459), channel_id=1, source_target_pairs={{0,2},{2,0},{4,6},{6,4},{1,3},{3,1},{5,7},{7,5},{8,10},{10,8},{12,... | collective-permute-start | bytes 7962632 | tf_op jit(solution)/shard_map/ppermute | solution.py:138
  375.5 32.5 %collective-permute-start.26 = (bf16[256,2304]{1,0:T(8,128)(2,1)}, bf16[256,2304]{1,0:T(8,128)(2,1)}, u32[]{:S(2)}, u32[]{:S(2)}) collective-permute-start(bf16[256,2304]{1,0:T(8,128)(2,1)} %collective-permute-done.20), channel_id=1, source_target_pairs={{0,8},{8,16},{16,24},{24,0},{1,9},{9,17},{17,25},{25,1},{2,10},{10... | collective-permute-start | bytes 3538952 | tf_op jit(solution)/shard_map/ppermute | solution.py:132
  394.3 55.8 %collective-permute-start.23 = (bf16[2,4,144,1152]{3,2,0,1:T(8,128)(2,1)S(1)}, bf16[2,4,144,1152]{3,2,0,1:T(8,128)(2,1)S(1)}, u32[]{:S(2)}, u32[]{:S(2)}) collective-permute-start(bf16[2,4,144,1152]{3,2,0,1:T(8,128)(2,1)S(1)} %dynamic-slice_bitcast_fusion.3), channel_id=1, source_target_pairs={{0,2},{2,0},{4,6},{6,4},{1,3},{3,1},{5,7},{7,5},{8,10},{10,8},{12,... | collective-permute-start | bytes 7962632 | tf_op jit(solution)/shard_map/ppermute | solution.py:138
  407.9 30.9 %collective-permute-start.27 = (bf16[256,2304]{1,0:T(8,128)(2,1)}, bf16[256,2304]{1,0:T(8,128)(2,1)S(1)}, u32[]{:S(2)}, u32[]{:S(2)}) collective-permute-start(bf16[256,2304]{1,0:T(8,128)(2,1)} %collective-permute-done.26), channel_id=1, source_target_pairs={{0,2},{2,0},{4,6},{6,4},{1,3},{3,1},{5,7},{7,5},{8,10},{10,8},{12,... | collective-permute-start | bytes 3538952 | tf_op jit(solution)/shard_map/ppermute | solution.py:138
  408.0 30.8 %collective-permute-start.30 = (bf16[256,2304]{1,0:T(8,128)(2,1)}, bf16[256,2304]{1,0:T(8,128)(2,1)S(1)}, u32[]{:S(2)}, u32[]{:S(2)}) collective-permute-start(bf16[256,2304]{1,0:T(8,128)(2,1)} %collective-permute-done.26), channel_id=1, source_target_pairs={{0,8},{8,16},{16,24},{24,0},{1,9},{9,17},{17,25},{25,1},{2,10},{10... | collective-permute-start | bytes 3538952 | tf_op jit(solution)/shard_map/ppermute | solution.py:132
  478.0 33.4 %collective-permute-start.32 = (bf16[256,2304]{1,0:T(8,128)(2,1)S(1)}, bf16[256,2304]{1,0:T(8,128)(2,1)S(1)}, u32[]{:S(2)}, u32[]{:S(2)}) collective-permute-start(bf16[256,2304]{1,0:T(8,128)(2,1)S(1)} %slice.781), channel_id=1, source_target_pairs={{0,2},{2,0},{4,6},{6,4},{1,3},{3,1},{5,7},{7,5},{8,10},{10,8},{12,... | collective-permute-start | bytes 3538952 | tf_op jit(solution)/shard_map/ppermute | solution.py:138
  627.0 30.6 %collective-permute-start.43 = (bf16[256,2304]{1,0:T(8,128)(2,1)S(1)}, bf16[256,2304]{1,0:T(8,128)(2,1)S(1)}, u32[]{:S(2)}, u32[]{:S(2)}) collective-permute-start(bf16[256,2304]{1,0:T(8,128)(2,1)S(1)} %collective-permute-done.42), channel_id=1, source_target_pairs={{0,2},{2,0},{4,6},{6,4},{1,3},{3,1},{5,7},{7,5},{8,10},{10,8},{12,... | collective-permute-start | bytes 3538952 | tf_op jit(solution)/shard_map/ppermute | solution.py:138
  627.0 30.6 %collective-permute-start.46 = (bf16[256,2304]{1,0:T(8,128)(2,1)S(1)}, bf16[256,2304]{1,0:T(8,128)(2,1)S(1)}, u32[]{:S(2)}, u32[]{:S(2)}) collective-permute-start(bf16[256,2304]{1,0:T(8,128)(2,1)S(1)} %collective-permute-done.42), channel_id=1, source_target_pairs={{0,8},{8,16},{16,24},{24,0},{1,9},{9,17},{17,25},{25,1},{2,10},{10... | collective-permute-start | bytes 3538952 | tf_op jit(solution)/shard_map/ppermute | solution.py:132
  629.4 67.1 %collective-permute-start.41 = (bf16[256,2304]{1,0:T(8,128)(2,1)S(1)}, bf16[256,2304]{1,0:T(8,128)(2,1)S(1)}, u32[]{:S(2)}, u32[]{:S(2)}) collective-permute-start(bf16[256,2304]{1,0:T(8,128)(2,1)S(1)} %fusion.74), channel_id=1, source_target_pairs={{0,8},{8,16},{16,24},{24,0},{1,9},{9,17},{17,25},{25,1},{2,10},{10... | collective-permute-start | bytes 3538952 | tf_op jit(solution)/shard_map/ppermute | solution.py:132
  704.7 179.5 %reduce-scatter.6.cloned.1.call-start = ((), (), s32[]{:S(2)}) async-start(), calls=%async_computation.13 | async-start | bytes 6635520 | tf_op jit(solution)/shard_map/reduce_scatter | solution.py:476
  810.6 45.3 %all-to-all-start.3 = ((bf16[4,144,1152]{2,1,0:T(8,128)(2,1)}), bf16[4,144,1152]{2,1,0:T(8,128)(2,1)}, u32[]{:S(2)}, u32[]{:S(2)}) async-start(bf16[4,144,1152]{2,1,0:T(8,128)(2,1)} %reduce-scatter.4.cloned.1.call-done), calls=%async_computation.4 | async-start | bytes 2654208 | tf_op jit(solution)/shard_map/all_to_all | solution.py:236
  815.0 149.9 %reduce-scatter.8.cloned.1.call-start = ((), (), s32[]{:S(2)}) async-start(), calls=%async_computation.14 | async-start | bytes 6635520 | tf_op jit(solution)/shard_map/reduce_scatter | solution.py:476
  815.2 40.7 %collective-permute-start.52 = (bf16[256,2304]{1,0:T(8,128)(2,1)}, bf16[256,2304]{1,0:T(8,128)(2,1)}, u32[]{:S(2)}, u32[]{:S(2)}) collective-permute-start(bf16[256,2304]{1,0:T(8,128)(2,1)} %multiply_convert_fusion.3), channel_id=1, source_target_pairs={{0,1},{1,0},{2,3},{3,2},{4,5},{5,4},{6,7},{7,6},{8,9},{9,8},{10,11... | collective-permute-start | bytes 3538952 | tf_op jit(solution)/shard_map/ppermute | solution.py:141
  884.2 55.2 %all-to-all-start.4 = ((bf16[4,144,1152]{2,1,0:T(8,128)(2,1)}), bf16[4,144,1152]{2,1,0:T(8,128)(2,1)}, u32[]{:S(2)}, u32[]{:S(2)}) async-start(bf16[4,144,1152]{2,1,0:T(8,128)(2,1)} %reduce-scatter.6.cloned.1.call-done), calls=%async_computation.6 | async-start | bytes 2654208 | tf_op jit(solution)/shard_map/all_to_all | solution.py:236
  894.5 43.5 %collective-permute-start.61 = (bf16[4,288,512]{2,1,0:T(8,128)(2,1)S(1)}, bf16[4,288,512]{2,1,0:T(8,128)(2,1)S(1)}, u32[]{:S(2)}, u32[]{:S(2)}) collective-permute-start(bf16[4,288,512]{2,1,0:T(8,128)(2,1)S(1)} %dynamic-slice_bitcast_fusion.7), channel_id=1, source_target_pairs={{0,4},{2,6},{4,0},{6,2},{1,5},{3,7},{5,1},{7,3},{8,12},{10,14},{12... | collective-permute-start | bytes 3538952 | tf_op jit(solution)/shard_map/ppermute | solution.py:135
  939.4 31.5 %all-to-all-start.5 = ((bf16[4,288,512]{2,1,0:T(8,128)(2,1)}), bf16[4,288,512]{2,1,0:T(8,128)(2,1)}, u32[]{:S(2)}, u32[]{:S(2)}) async-start(bf16[4,288,512]{2,1,0:T(8,128)(2,1)} %fusion.98), calls=%async_computation.8 | async-start | bytes 2359296 | tf_op jit(solution)/shard_map/all_to_all | solution.py:236
  971.0 36.0 %all-to-all-start.6 = ((bf16[4,144,1152]{2,1,0:T(8,128)(2,1)}), bf16[4,144,1152]{2,1,0:T(8,128)(2,1)}, u32[]{:S(2)}, u32[]{:S(2)}) async-start(bf16[4,144,1152]{2,1,0:T(8,128)(2,1)} %reduce-scatter.8.cloned.1.call-done), calls=%async_computation.9 | async-start | bytes 2654208 | tf_op jit(solution)/shard_map/all_to_all | solution.py:236
  1013.7 34.0 %collective-permute-start.64 = (bf16[512,512]{1,0:T(8,128)(2,1)S(1)}, bf16[512,512]{1,0:T(8,128)(2,1)S(1)}, u32[]{:S(2)}, u32[]{:S(2)}) collective-permute-start(bf16[512,512]{1,0:T(8,128)(2,1)S(1)} %get-tuple-element.238), channel_id=1, source_target_pairs={{0,16},{8,24},{16,0},{24,8},{1,17},{9,25},{17,1},{25,9},{2,18},{10... | collective-permute-start | bytes 1572872 | tf_op jit(solution)/shard_map/ppermute | solution.py:132
  1015.1 32.6 %collective-permute-start.65 = (bf16[512,512]{1,0:T(8,128)(2,1)S(1)}, bf16[512,512]{1,0:T(8,128)(2,1)S(1)}, u32[]{:S(2)}, u32[]{:S(2)}) collective-permute-start(bf16[512,512]{1,0:T(8,128)(2,1)S(1)} %fusion.188), channel_id=1, source_target_pairs={{0,24},{8,0},{16,8},{24,16},{1,25},{9,1},{17,9},{25,17},{2,26},{10... | collective-permute-start | bytes 1572872 | tf_op jit(solution)/shard_map/ppermute | solution.py:132
  1074.3 53.0 %collective-permute-start.68 = (bf16[256,2304]{1,0:T(8,128)(2,1)}, bf16[256,2304]{1,0:T(8,128)(2,1)}, u32[]{:S(2)}, u32[]{:S(2)}) collective-permute-start(bf16[256,2304]{1,0:T(8,128)(2,1)} %dynamic-slice_convert_fusion), channel_id=1, source_target_pairs={{0,1},{1,0},{2,3},{3,2},{4,5},{5,4},{6,7},{7,6},{8,9},{9,8},{10,11... | collective-permute-start | bytes 3538952 | tf_op jit(solution)/shard_map/ppermute | solution.py:141
  1075.8 46.4 %all-to-all-start.7 = ((bf16[4,288,512]{2,1,0:T(8,128)(2,1)}), bf16[4,288,512]{2,1,0:T(8,128)(2,1)S(1)}, u32[]{:S(2)}, u32[]{:S(2)}) async-start(bf16[4,288,512]{2,1,0:T(8,128)(2,1)} %convert_add_fusion.1), calls=%async_computation.10 | async-start | bytes 2359296 | tf_op jit(solution)/shard_map/all_to_all | solution.py:236
  1122.2 32.1 %all-to-all-start.8 = ((bf16[4,288,512]{2,1,0:T(8,128)(2,1)}), bf16[4,288,512]{2,1,0:T(8,128)(2,1)S(1)}, u32[]{:S(2)}, u32[]{:S(2)}) async-start(bf16[4,288,512]{2,1,0:T(8,128)(2,1)} %fusion.97), calls=%async_computation.11 | async-start | bytes 2359296 | tf_op jit(solution)/shard_map/all_to_all | solution.py:236
  (233 other events, 3421.4 us)
Sparse Core Ops, SparseCore 0:
  150.1 83.2 all-gather.6
  253.9 70.2 all-gather.8
  326.0 66.2 all-gather.10
  704.8 62.4 reduce-scatter.3
  770.2 73.7 reduce-scatter.5
  863.7 78.1 reduce-scatter.7
